TPU v7x, 32 devices: a whole 2x2x4 slice. The times are simulated.
32 devices in a mesh: segment: 8 (over y, x, core), head: 4 (over z).
Axes of the slice: x: 2, y: 2, z: 4, core: 2. Of those that a mesh axis runs over, the one named last changes fastest.
Arguments:
- grad_in: float32 [8, 128, 512], P('segment'), may hold values from -6 to 6
- memory: bfloat16 [8, 128, 512], P('segment'), may hold values from -120 to 120
- enc_grad_in: float32 [8, 128, 512], P('segment', None, 'head'), may hold values from -3 to 3
- act_stash: bfloat16 [8, 3, 128, 512], P('segment'), may hold values from -120 to 120
- slot_order: int32 [8, 3], P('segment'), may hold values from 0 to 2, each once within a row
- lengths: int32 [8, 3], P('segment'), may hold values from 16 to 128, as said below
- w_query: bfloat16 [8, 512, 4096], P('segment', None, 'head'), may hold values from -0.0234375 to 0.0234375
- w_key: bfloat16 [8, 512, 4096], P('segment', None, 'head'), may hold values from -0.25 to 0.25
- w_value: bfloat16 [8, 512, 4096], P('segment', None, 'head'), may hold values from -0.25 to 0.25
- w_out: bfloat16 [8, 4096, 512], P('segment', 'head'), may hold values from -0.09375 to 0.09375
Outputs:
- grad_out: float32 [8, 128, 512], P('segment')
- enc_grad_out: float32 [8, 128, 512], P('segment', None, 'head')
Inputs may be any that keep to these rules, and one draw needn't show every extreme that they name: `slot_order`: each row lists every stash slot once. `lengths`: some entry equals 128.
All inputs are finite; a program needn't handle non-finite values.
Results may differ from a plain program's by a relative error of at most 0.018.
The roundings to bfloat16 on the way count: a program that leaves them out, or rounds other values in their place, can miss the bound.
Values may be sent and summed in bfloat16 or wider, within the bound.
No kernel may reach another device: no remote copies, remote signals or barrier semaphores. Data moves between devices by JAX's collectives and lax.ppermute only.
A program may use at most 64 MiB of HBM per device.

v0:
```python
import jax
import jax.numpy as jnp
from jax import lax
from jax.sharding import PartitionSpec as P

HEAD_DIM = 128
TICKS = 3


def shifted(value, axis, steps):
    count = lax.axis_size(axis)
    pairs = [(source, (source + steps) % count) for source in range(count)]
    return lax.ppermute(value, axis, pairs)


def local_terms(
    gradient_low, held, decoded, length, query_weight, key_weight, value_weight, out_weight
):
    inner = query_weight.shape[1]
    head_local = inner // HEAD_DIM
    dec_rows = decoded.shape[0]
    enc_rows = held.shape[0]
    queries = jnp.dot(decoded, query_weight, preferred_element_type=jnp.float32).astype(
        jnp.bfloat16
    )
    keys = jnp.dot(held, key_weight, preferred_element_type=jnp.float32).astype(jnp.bfloat16)
    values = jnp.dot(held, value_weight, preferred_element_type=jnp.float32).astype(jnp.bfloat16)
    query_heads = queries.reshape(dec_rows, head_local, HEAD_DIM)
    key_heads = keys.reshape(enc_rows, head_local, HEAD_DIM)
    value_heads = values.reshape(enc_rows, head_local, HEAD_DIM)
    scores = jnp.einsum("qhd,khd->hqk", query_heads, key_heads, preferred_element_type=jnp.float32)
    allowed = lax.broadcasted_iota(jnp.int32, (1, 1, enc_rows), 2) < length
    scores = jnp.where(allowed, scores, jnp.float32(-1e30))
    row_max = jnp.max(scores, axis=-1, keepdims=True)
    expo = jnp.exp(scores - row_max)
    attention = expo / jnp.sum(expo, axis=-1, keepdims=True)
    attention_low = attention.astype(jnp.bfloat16)
    context_grad = jnp.einsum(
        "qe,ie->qi", gradient_low, out_weight, preferred_element_type=jnp.float32
    ).astype(jnp.bfloat16)
    context_heads = context_grad.reshape(dec_rows, head_local, HEAD_DIM)
    prob_grad = jnp.einsum(
        "qhd,khd->hqk", context_heads, value_heads, preferred_element_type=jnp.float32
    )
    score_grad = (
        attention * (prob_grad - jnp.sum(attention * prob_grad, axis=-1, keepdims=True))
    ).astype(jnp.bfloat16)
    query_grad = (
        jnp.einsum("hqk,khd->qhd", score_grad, key_heads, preferred_element_type=jnp.float32)
        .astype(jnp.bfloat16)
        .reshape(dec_rows, inner)
    )
    key_grad = (
        jnp.einsum("hqk,qhd->khd", score_grad, query_heads, preferred_element_type=jnp.float32)
        .astype(jnp.bfloat16)
        .reshape(enc_rows, inner)
    )
    value_grad = (
        jnp.einsum("hqk,qhd->khd", attention_low, context_heads, preferred_element_type=jnp.float32)
        .astype(jnp.bfloat16)
        .reshape(enc_rows, inner)
    )
    decoder_part = jnp.einsum(
        "qi,ei->qe", query_grad, query_weight, preferred_element_type=jnp.float32
    )
    memory_part = jnp.einsum("ki,ei->ke", key_grad, key_weight, preferred_element_type=jnp.float32)
    memory_part = memory_part + jnp.einsum(
        "ki,ei->ke", value_grad, value_weight, preferred_element_type=jnp.float32
    )
    return (decoder_part, memory_part)


def body(
    grad_in, memory, enc_grad_in, act_stash, slot_order, lengths, w_query, w_key, w_value, w_out
):
    held = memory[0]
    stash_local = act_stash[0]
    order_row = slot_order[0]
    length_row = lengths[0]
    head_count = lax.axis_size("head")
    shard_width = enc_grad_in.shape[2]
    feature_share = grad_in.shape[2] // head_count
    gradient = lax.dynamic_slice_in_dim(
        grad_in[0], lax.axis_index("head") * feature_share, feature_share, 1
    )
    carried = jnp.zeros((held.shape[0], shard_width * head_count), jnp.float32)
    carried = lax.dynamic_update_slice_in_dim(
        carried, enc_grad_in[0], lax.axis_index("head") * shard_width, 1
    )
    for tick_index in range(TICKS):
        if tick_index == 0:
            gradient_low = grad_in[0].astype(jnp.bfloat16)
        else:
            gradient_low = lax.all_gather(gradient.astype(jnp.bfloat16), "head", axis=1, tiled=True)
        decoded = lax.dynamic_index_in_dim(stash_local, order_row[tick_index], 0, keepdims=False)
        decoder_part, memory_part = local_terms(
            gradient_low,
            held,
            decoded,
            length_row[tick_index],
            w_query[0],
            w_key[0],
            w_value[0],
            w_out[0],
        )
        gradient = gradient + lax.psum_scatter(
            decoder_part, "head", scatter_dimension=1, tiled=True
        )
        carried = carried + memory_part
        gradient, carried = shifted((gradient, carried), "segment", -1)
        if tick_index + 1 < TICKS:
            held = shifted(held, "segment", -1)
    carried = lax.psum_scatter(carried, "head", scatter_dimension=1, tiled=True)
    gradient = lax.all_gather(gradient, "head", axis=1, tiled=True)
    return (gradient[None], carried[None])


def solution(mesh):
    in_specs = (
        P("segment", None, None),
        P("segment", None, None),
        P("segment", None, "head"),
        P("segment", None, None, None),
        P("segment", None),
        P("segment", None),
        P("segment", None, "head"),
        P("segment", None, "head"),
        P("segment", None, "head"),
        P("segment", "head", None),
    )
    out_specs = (P("segment", None, None), P("segment", None, "head"))
    return jax.shard_map(body, mesh=mesh, in_specs=in_specs, out_specs=out_specs, check_vma=False)
```

profile of v0, /device:TPU:0, one launch (start us, length us, event | category | flops | bytes accessed | tf_op | source)
XLA Modules:
  0.0 184.4 jit_solution(5758655735363486501)
XLA Ops:
  7.2 3.4 %collective-permute-start.1 = (bf16[128,512]{1,0:T(8,128)(2,1)}, bf16[128,512]{1,0:T(8,128)(2,1)}, u32[]{:S(2)}, u32[]{:S(2)}) collective-permute-start(bf16[128,512]{1,0:T(8,128)(2,1)} %bitcast.204), channel_id=1, source_target_pairs={{0,28},{4,0},{8,4},{12,8},{16,12},{20,16},{24,20},{28,24},{1,29},{... | collective-permute-start | bytes 393224 | tf_op jit(solution)/shard_map/ppermute | solution.py:13
  16.7 2.2 %convolution_convert_fusion.18 = bf16[128,1024]{1,0:T(8,128)(2,1)} fusion(bf16[1,1024,512]{2,1,0:T(8,128)(2,1)S(1)} %copy-done.3, f32[1,128,512]{2,1,0:T(8,128)} %param.10), kind=kOutput, calls=%fused_computation.30 | convolution fusion | flops 134414336 | bytes 1572864 | tf_op jit(solution)/shard_map/qe,ie->qi/dot_general | solution.py:38
  24.6 2.1 %fusion.68 = (f32[8,128]{1,0:T(8,128)S(1)}, f32[8,128,128]{1,2,0:T(8,128)}) fusion(bf16[128,8,128]{0,2,1:T(8,128)(2,1)S(1)} %bitcast.191, bf16[128,8,128]{0,2,1:T(8,128)(2,1)} %bitcast.194, pred[128]{0:T(512)(128)(4,1)S(1)} %iota_compare_fusion.2), kind=kOutput, calls=%fused_computation.109 | convolution fusion | flops 33947776 | bytes 1052800 | tf_op jit(solution)/shard_map/sub | solution.py:35
  30.6 2.3 %convolution_convert_fusion.4 = bf16[8,128,128]{2,1,0:T(8,128)(2,1)} fusion(bf16[128,8,128]{0,2,1:T(8,128)(2,1)} %bitcast.208, f32[8,128]{1,0:T(8,128)S(1)} %get-tuple-element.8, bf16[128,8,128]{0,2,1:T(8,128)(2,1)} %bitcast.192, bf16[128,8,128]{0,2,1:T(8,128)(2,1)} %bitcast.195, pred[128]{0:T(512)(128)(4,1)S(1)} %iota_compare_fusion.2), kind=kOutput, calls=%fused_computation.16 | convolution fusion | flops 67765376 | bytes 1052800 | tf_op jit(solution)/shard_map/hqk,qhd->khd/dot_general | solution.py:59
  33.0 2.0 %convolution_convert_fusion.5 = bf16[8,128,128]{2,1,0:T(8,128)(2,1)} fusion(bf16[128,8,128]{0,2,1:T(8,128)(2,1)} %bitcast.193, bf16[8,128,128]{1,2,0:T(8,128)(2,1)S(1)} %multiply_convert_fusion.2), kind=kOutput, calls=%fused_computation.17 | convolution fusion | flops 33685504 | bytes 786432 | tf_op jit(solution)/shard_map/hqk,qhd->khd/dot_general | solution.py:54
  36.4 2.2 %convolution_add_fusion.2 = f32[128,512]{1,0:T(8,128)} fusion(f32[128,512]{1,0:T(8,128)S(1)} %fusion.35, bf16[128,1024]{0,1:T(8,128)(2,1)} %bitcast.206, bf16[1,512,1024]{2,1,0:T(8,128)(2,1)S(1)} %copy-done.2), kind=kOutput, calls=%fused_computation.39 | convolution fusion | flops 134283264 | bytes 1835008 | tf_op jit(solution)/shard_map/ki,ei->ke/dot_general | solution.py:67
  43.9 1.9 %convolution_convert_fusion.9 = bf16[128,1024]{1,0:T(8,128)(2,1)} fusion(bf16[1,512,1024]{2,1,0:T(8,128)(2,1)S(1)} %copy-done, bf16[1,3,128,512]{3,2,1,0:T(8,128)(2,1)} %param.13, s32[]{:T(128)S(6)} %select_n.29), kind=kOutput, calls=%fused_computation.21 | convolution fusion | flops 134348800 | bytes 1441796 | tf_op jit(solution)/shard_map/dot_general | solution.py:23
  46.5 1.9 %convolution_convert_fusion.14 = bf16[128,1024]{1,0:T(8,128)(2,1)} fusion(bf16[1,512,1024]{2,1,0:T(8,128)(2,1)S(1)} %copy-done, bf16[1,3,128,512]{3,2,1,0:T(8,128)(2,1)} %param.13, s32[]{:T(128)S(6)} %select_n.27), kind=kOutput, calls=%fused_computation.26 | convolution fusion | flops 134348800 | bytes 1441796 | tf_op jit(solution)/shard_map/dot_general | solution.py:23
  52.7 1.9 %convolution_convert_fusion.15 = bf16[128,1024]{1,0:T(8,128)(2,1)} fusion(bf16[128,512]{1,0:T(8,128)(2,1)} %collective-permute-done.1, bf16[1,512,1024]{2,1,0:T(8,128)(2,1)S(1)} %copy-done.1), kind=kOutput, calls=%fused_computation.27 | convolution fusion | flops 134348800 | bytes 1441792 | tf_op jit(solution)/shard_map/dot_general | solution.py:26
  56.5 2.2 %fusion.69 = (f32[8,128]{1,0:T(8,128)S(1)}, f32[8,128,128]{1,2,0:T(8,128)}) fusion(bf16[128,8,128]{0,2,1:T(8,128)(2,1)} %bitcast.185, bf16[128,8,128]{0,2,1:T(8,128)(2,1)} %bitcast.188, pred[128]{0:T(512)(128)(4,1)S(1)} %iota_compare_fusion.1), kind=kOutput, calls=%fused_computation.110 | convolution fusion | flops 33947776 | bytes 1052800 | tf_op jit(solution)/shard_map/sub | solution.py:35
  59.3 2.0 %fusion.10 = bf16[16,8,8,128]{3,2,1,0:T(8,128)(2,1)} fusion(bf16[128,512]{1,0:T(8,128)(2,1)} %collective-permute-done.1, bf16[1,512,1024]{2,1,0:T(8,128)(2,1)S(1)} %copy-done.2), kind=kOutput, calls=%fused_computation.34 | convolution fusion | flops 134348800 | bytes 1441792 | tf_op jit(solution)/shard_map/dot_general | solution.py:27
  64.9 2.1 %fusion.70 = (f32[8,128]{1,0:T(8,128)S(1)}, f32[8,128,128]{1,2,0:T(8,128)}) fusion(bf16[128,8,128]{0,2,1:T(8,128)(2,1)S(1)} %bitcast.179, bf16[128,8,128]{0,2,1:T(8,128)(2,1)} %bitcast.182, pred[128]{0:T(512)(128)(4,1)S(1)} %iota_compare_fusion), kind=kOutput, calls=%fused_computation.111 | convolution fusion | flops 33947776 | bytes 1052800 | tf_op jit(solution)/shard_map/sub | solution.py:35
  68.0 2.7 %collective-permute-start = (f32[128,128]{1,0:T(8,128)S(1)}, f32[128,128]{1,0:T(8,128)S(1)}, u32[]{:S(2)}, u32[]{:S(2)}) collective-permute-start(f32[128,128]{1,0:T(8,128)S(1)} %bitcast_add_fusion.1), channel_id=1, source_target_pairs={{0,28},{4,0},{8,4},{12,8},{16,12},{20,16},{24,20},{28,24},{1,29},{... | collective-permute-start | bytes 196616 | tf_op jit(solution)/shard_map/ppermute | solution.py:13
  73.2 12.5 %all_gather.9 = bf16[128,512]{1,0:T(8,128)(2,1)S(1)} all-gather(bf16[128,128]{1,0:T(8,128)(2,1)S(1)} %convert_element_type.131), channel_id=1, replica_groups=mesh['segment'=8,'head'=4] {'head'}, dimensions={1}, use_global_device_ids=true | all-gather | bytes 163840 | tf_op jit(solution)/shard_map/all_gather | solution.py:94
  91.0 2.4 %convolution_convert_fusion.2 = bf16[8,128,128]{2,1,0:T(8,128)(2,1)} fusion(bf16[128,8,128]{0,2,1:T(8,128)(2,1)} %bitcast.210, f32[8,128]{1,0:T(8,128)S(1)} %get-tuple-element.12, bf16[128,8,128]{0,2,1:T(8,128)(2,1)} %bitcast.186, bf16[128,8,128]{0,2,1:T(8,128)(2,1)} %bitcast.189, pred[128]{0:T(512)(128)(4,1)S(1)} %iota_compare_fusion.1), kind=kOutput, calls=%fused_computation.14 | convolution fusion | flops 67765376 | bytes 1052800 | tf_op jit(solution)/shard_map/hqk,qhd->khd/dot_general | solution.py:59
  95.1 14.4 %reduce-scatter.7.cloned.1.call-done = f32[128,128]{1,0:T(8,128)} async-done(((f32[128,512]{1,0:T(8,128)}), f32[128,128]{1,0:T(8,128)}) %reduce-scatter.7.cloned.1.call-update) | async-done | bytes 65552 | tf_op jit(solution)/shard_map/reduce_scatter | solution.py:106
  110.5 2.3 %fusion.12 = f32[128,512]{1,0:T(8,128)} fusion(f32[128,512]{1,0:T(8,128)} %collective-permute-done.5, f32[128,512]{1,0:T(8,128)S(1)} %fusion.33, bf16[128,1024]{0,1:T(8,128)(2,1)} %bitcast.213, bf16[1,512,1024]{2,1,0:T(8,128)(2,1)S(1)} %copy-done.2), kind=kOutput, calls=%fused_computation.38 | convolution fusion | flops 134348800 | bytes 2097152 | tf_op jit(solution)/shard_map/ki,ei->ke/dot_general | solution.py:67
  112.8 2.4 %collective-permute-start.6 = (f32[128,512]{1,0:T(8,128)}, f32[128,512]{1,0:T(8,128)}, u32[]{:S(2)}, u32[]{:S(2)}) collective-permute-start(f32[128,512]{1,0:T(8,128)} %fusion.12), channel_id=1, source_target_pairs={{0,28},{4,0},{8,4},{12,8},{16,12},{20,16},{24,20},{28,24},{1,29},{... | collective-permute-start | bytes 786440 | tf_op jit(solution)/shard_map/ppermute | solution.py:13
  115.2 12.3 %all_gather.10 = bf16[128,512]{1,0:T(8,128)(2,1)S(1)} all-gather(bf16[128,128]{1,0:T(8,128)(2,1)S(1)} %convert_element_type.139), channel_id=1, replica_groups=mesh['segment'=8,'head'=4] {'head'}, dimensions={1}, use_global_device_ids=true | all-gather | bytes 163840 | tf_op jit(solution)/shard_map/all_gather | solution.py:94
  130.5 2.3 %convolution_convert_fusion = bf16[8,128,128]{2,1,0:T(8,128)(2,1)} fusion(bf16[128,8,128]{0,2,1:T(8,128)(2,1)} %bitcast.211, f32[8,128]{1,0:T(8,128)S(1)} %get-tuple-element.16, bf16[128,8,128]{0,2,1:T(8,128)(2,1)S(1)} %bitcast.180, bf16[128,8,128]{0,2,1:T(8,128)(2,1)} %bitcast.183, pred[128]{0:T(512)(128)(4,1)S(1)} %iota_compare_fusion), kind=kOutput, calls=%fused_computation.12 | convolution fusion | flops 67765376 | bytes 1052800 | tf_op jit(solution)/shard_map/hqk,qhd->khd/dot_general | solution.py:59
  140.7 3.9 %collective-permute-done.7 = f32[128,512]{1,0:T(8,128)S(1)} collective-permute-done((f32[128,512]{1,0:T(8,128)S(1)}, f32[128,512]{1,0:T(8,128)S(1)}, u32[]{:S(2)}, u32[]{:S(2)}) %collective-permute-start.7) | collective-permute-done | bytes 262176 | tf_op jit(solution)/shard_map/ppermute | solution.py:13
  145.3 9.7 %reduce-scatter.9.cloned.1.call-done = f32[128,128]{1,0:T(8,128)} async-done(((f32[128,512]{1,0:T(8,128)}), f32[128,128]{1,0:T(8,128)}) %reduce-scatter.9.cloned.1.call-update) | async-done | bytes 65552 | tf_op jit(solution)/shard_map/reduce_scatter | solution.py:106
  157.8 14.7 %all_gather.11 = f32[128,512]{1,0:T(8,128)S(1)} all-gather(f32[128,128]{1,0:T(8,128)S(1)} %collective-permute-done.4), channel_id=1, replica_groups=mesh['segment'=8,'head'=4] {'head'}, dimensions={1}, use_global_device_ids=true | all-gather | bytes 327680 | tf_op jit(solution)/shard_map/all_gather | solution.py:114
  172.5 4.6 %reduce-scatter.11.cloned.1.call-done = f32[128,128]{1,0:T(8,128)} async-done(((f32[128,512]{1,0:T(8,128)}), f32[128,128]{1,0:T(8,128)}) %reduce-scatter.11.cloned.1.call-update) | async-done | bytes 65552 | tf_op jit(solution)/shard_map/reduce_scatter | solution.py:113
  (112 shorter events, 54.0 us)
Async XLA Ops:
  7.2 8.1 %copy-start = (bf16[1,512,1024]{2,1,0:T(8,128)(2,1)S(1)}, bf16[1,512,1024]{2,1,0:T(8,128)(2,1)}, u32[]{:S(2)}) copy-start(bf16[1,512,1024]{2,1,0:T(8,128)(2,1)} %param.16) | copy-start | bytes 3145732
  7.2 3.5 %copy-start.21 = (s32[1,3]{1,0:T(1,128)S(1)}, s32[1,3]{1,0:T(1,128)}, u32[]{:S(2)}) copy-start(s32[1,3]{1,0:T(1,128)} %param.14) | copy-start | bytes 40
  7.2 9.5 %copy-start.3 = (bf16[1,1024,512]{2,1,0:T(8,128)(2,1)S(1)}, bf16[1,1024,512]{2,1,0:T(8,128)(2,1)}, u32[]{:S(2)}) copy-start(bf16[1,1024,512]{2,1,0:T(8,128)(2,1)} %param.19) | copy-start | bytes 3145732
  7.2 59.8 %reduce-scatter.5.cloned.1.call-start = ((), (), s32[]{:S(2)}) async-start(), calls=%async_computation.4 | async-start | bytes 327680 | tf_op jit(solution)/shard_map/reduce_scatter | solution.py:106
  7.2 45.5 %collective-permute-start.1 = (bf16[128,512]{1,0:T(8,128)(2,1)}, bf16[128,512]{1,0:T(8,128)(2,1)}, u32[]{:S(2)}, u32[]{:S(2)}) collective-permute-start(bf16[128,512]{1,0:T(8,128)(2,1)} %bitcast.204), channel_id=1, source_target_pairs={{0,28},{4,0},{8,4},{12,8},{16,12},{20,16},{24,20},{28,24},{1,29},{... | collective-permute-start | bytes 393224 | tf_op jit(solution)/shard_map/ppermute | solution.py:13
  16.7 7.9 %copy-start.10 = (bf16[128,1024]{0,1:T(8,128)(2,1)}, bf16[128,1024]{0,1:T(8,128)(2,1)S(1)}, u32[]{:S(2)}) copy-start(bf16[128,1024]{0,1:T(8,128)(2,1)S(1)} %copy.52) | copy-start | bytes 786436
  16.7 4.1 %copy-start.1 = (bf16[1,512,1024]{2,1,0:T(8,128)(2,1)S(1)}, bf16[1,512,1024]{2,1,0:T(8,128)(2,1)}, u32[]{:S(2)}) copy-start(bf16[1,512,1024]{2,1,0:T(8,128)(2,1)} %param.17) | copy-start | bytes 3145732
  20.7 2.8 %copy-start.2 = (bf16[1,512,1024]{2,1,0:T(8,128)(2,1)S(1)}, bf16[1,512,1024]{2,1,0:T(8,128)(2,1)}, u32[]{:S(2)}) copy-start(bf16[1,512,1024]{2,1,0:T(8,128)(2,1)} %param.18) | copy-start | bytes 3145732
  30.6 79.0 %reduce-scatter.7.cloned.1.call-start = ((), (), s32[]{:S(2)}) async-start(), calls=%async_computation.5 | async-start | bytes 327680 | tf_op jit(solution)/shard_map/reduce_scatter | solution.py:106
  36.4 2.2 %copy-start.20 = (f32[1,128,128]{2,1,0:T(8,128)S(1)}, f32[1,128,128]{2,1,0:T(8,128)}, u32[]{:S(2)}) copy-start(f32[1,128,128]{2,1,0:T(8,128)} %param.12) | copy-start | bytes 196612
  40.0 70.4 %collective-permute-start.5 = (f32[128,512]{1,0:T(8,128)}, f32[128,512]{1,0:T(8,128)}, u32[]{:S(2)}, u32[]{:S(2)}) collective-permute-start(f32[128,512]{1,0:T(8,128)} %fusion.60), channel_id=1, source_target_pairs={{0,28},{4,0},{8,4},{12,8},{16,12},{20,16},{24,20},{28,24},{1,29},{... | collective-permute-start | bytes 786440 | tf_op jit(solution)/shard_map/ppermute | solution.py:13
  50.2 14.8 %copy-start.6 = (bf16[128,1024]{0,1:T(8,128)(2,1)}, bf16[128,1024]{0,1:T(8,128)(2,1)S(1)}, u32[]{:S(2)}) copy-start(bf16[128,1024]{0,1:T(8,128)(2,1)S(1)} %copy.58) | copy-start | bytes 786436
  58.6 3.5 %collective-permute-start.3 = (bf16[128,512]{1,0:T(8,128)(2,1)}, bf16[128,512]{1,0:T(8,128)(2,1)S(1)}, u32[]{:S(2)}, u32[]{:S(2)}) collective-permute-start(bf16[128,512]{1,0:T(8,128)(2,1)} %collective-permute-done.1), channel_id=1, source_target_pairs={{0,28},{4,0},{8,4},{12,8},{16,12},{20,16},{24,20},{28,24},{1,29},{... | collective-permute-start | bytes 393224 | tf_op jit(solution)/shard_map/ppermute | solution.py:13
  67.0 18.7 %copy-start.4 = (bf16[1,1024,512]{2,1,0:T(8,128)(2,1)S(1)}, bf16[1,1024,512]{2,1,0:T(8,128)(2,1)}, u32[]{:S(2)}) copy-start(bf16[1,1024,512]{2,1,0:T(8,128)(2,1)} %param.19) | copy-start | bytes 3145732
  68.0 4.6 %collective-permute-start = (f32[128,128]{1,0:T(8,128)S(1)}, f32[128,128]{1,0:T(8,128)S(1)}, u32[]{:S(2)}, u32[]{:S(2)}) collective-permute-start(f32[128,128]{1,0:T(8,128)S(1)} %bitcast_add_fusion.1), channel_id=1, source_target_pairs={{0,28},{4,0},{8,4},{12,8},{16,12},{20,16},{24,20},{28,24},{1,29},{... | collective-permute-start | bytes 196616 | tf_op jit(solution)/shard_map/ppermute | solution.py:13
  90.9 64.1 %reduce-scatter.9.cloned.1.call-start = ((), (), s32[]{:S(2)}) async-start(), calls=%async_computation.6 | async-start | bytes 327680 | tf_op jit(solution)/shard_map/reduce_scatter | solution.py:106
  94.6 14.9 %copy-start.18 = (f32[128,128]{1,0:T(8,128)S(1)}, f32[128,128]{1,0:T(8,128)}, u32[]{:S(2)}) copy-start(f32[128,128]{1,0:T(8,128)} %copy-done.17) | copy-start | bytes 196612
  110.4 4.8 %collective-permute-start.2 = (f32[128,128]{1,0:T(8,128)S(1)}, f32[128,128]{1,0:T(8,128)S(1)}, u32[]{:S(2)}, u32[]{:S(2)}) collective-permute-start(f32[128,128]{1,0:T(8,128)S(1)} %add.56), channel_id=1, source_target_pairs={{0,28},{4,0},{8,4},{12,8},{16,12},{20,16},{24,20},{28,24},{1,29},{... | collective-permute-start | bytes 196616 | tf_op jit(solution)/shard_map/ppermute | solution.py:13
  110.5 17.0 %copy-start.5 = (bf16[1,1024,512]{2,1,0:T(8,128)(2,1)S(1)}, bf16[1,1024,512]{2,1,0:T(8,128)(2,1)}, u32[]{:S(2)}) copy-start(bf16[1,1024,512]{2,1,0:T(8,128)(2,1)} %param.19) | copy-start | bytes 3145732
  112.8 26.9 %collective-permute-start.6 = (f32[128,512]{1,0:T(8,128)}, f32[128,512]{1,0:T(8,128)}, u32[]{:S(2)}, u32[]{:S(2)}) collective-permute-start(f32[128,512]{1,0:T(8,128)} %fusion.12), channel_id=1, source_target_pairs={{0,28},{4,0},{8,4},{12,8},{16,12},{20,16},{24,20},{28,24},{1,29},{... | collective-permute-start | bytes 786440 | tf_op jit(solution)/shard_map/ppermute | solution.py:13
  128.7 1.8 copy-start.7
  138.3 38.9 %reduce-scatter.11.cloned.1.call-start = ((), (), s32[]{:S(2)}) async-start(), calls=%async_computation.7 | async-start | bytes 327680 | tf_op jit(solution)/shard_map/reduce_scatter | solution.py:113
  140.7 3.9 %collective-permute-start.7 = (f32[128,512]{1,0:T(8,128)S(1)}, f32[128,512]{1,0:T(8,128)S(1)}, u32[]{:S(2)}, u32[]{:S(2)}) collective-permute-start(f32[128,512]{1,0:T(8,128)S(1)} %add.65), channel_id=1, source_target_pairs={{0,28},{4,0},{8,4},{12,8},{16,12},{20,16},{24,20},{28,24},{1,29},{... | collective-permute-start | bytes 786440 | tf_op jit(solution)/shard_map/ppermute | solution.py:13
  155.9 2.0 %collective-permute-start.4 = (f32[128,128]{1,0:T(8,128)S(1)}, f32[128,128]{1,0:T(8,128)S(1)}, u32[]{:S(2)}, u32[]{:S(2)}) collective-permute-start(f32[128,128]{1,0:T(8,128)S(1)} %add.58), channel_id=1, source_target_pairs={{0,28},{4,0},{8,4},{12,8},{16,12},{20,16},{24,20},{28,24},{1,29},{... | collective-permute-start | bytes 196616 | tf_op jit(solution)/shard_map/ppermute | solution.py:13
  (10 other events, 11.5 us)
Sparse Core Ops, SparseCore 0:
  30.7 19.9 reduce-scatter.4
  91.1 18.4 reduce-scatter.6
  138.4 16.6 reduce-scatter.8
  157.7 19.3 reduce-scatter.10
where the time goes:
time: 186 us; the launch traced here: 184 us
  matrix products  51.4 us (28%)
  blocking collectives  39.4 us (21%)
  waiting for transfers between devices  36.4 us (20%)
  between operations  19.9 us (11%)
  local copies, waits for them, and re-layouts  19.8 us (11%)
  starting transfers between devices  10.2 us (5%)
  other arithmetic  7.23 us (4%)
    all_gather x2, blocking collectives, body(): lax.all_gather(gradient.astype(jnp.bfloat16), 'head', axis=1, tiled=True)  24.7 us
    reduce_scatter x3, waiting for transfers between devices, body(): lax.psum_scatter(decoder_part, 'head', scatter_dimension=1, tiled=True)  24.2 us
    all_gather x1, blocking collectives, body(): gradient = lax.all_gather(gradient, 'head', axis=1, tiled=True)  14.7 us
    ppermute x8, starting transfers between devices, shifted(): return lax.ppermute(value, axis, pairs)  10 us
    ppermute x8, waiting for transfers between devices, shifted(): return lax.ppermute(value, axis, pairs)  7.54 us
    dot_general x3, matrix products, local_terms(): jnp.einsum('hqk,qhd->khd', attention_low, context_heads, preferred_elemen...  6.98 us
    sub x3, matrix products, local_terms(): expo = jnp.exp(scores - row_max)  6.36 us
    reshape x3, local copies, waits for them, and re-layouts, local_terms(): key_heads = keys.reshape(enc_rows, head_local, HEAD_DIM)  5.37 us
  transfers between devices with their start and end apart: 12, of which 7 were waited for; matrix products, arithmetic and copies ran while one was open for 40% of the time, Pallas kernels for 0%

commit v1 on v0

v1 whole, which is shorter than its diff:
```python
import jax
import jax.numpy as jnp
from jax import lax
from jax.experimental import pallas as pl
from jax.experimental.pallas import tpu as pltpu
from jax.sharding import PartitionSpec as P

HEAD_DIM = 128
TICKS = 3
LOW = jnp.bfloat16
FULL = jnp.float32


def dot(a, b, ca, cb):
    return lax.dot_general(a, b, (((ca,), (cb,)), ((), ())), preferred_element_type=FULL)


def cols(head):
    return slice(head * HEAD_DIM, (head + 1) * HEAD_DIM)


def tree_sum(terms):
    terms = list(terms)
    while len(terms) > 1:
        terms = [
            terms[i] + terms[i + 1] if i + 1 < len(terms) else terms[i]
            for i in range(0, len(terms), 2)
        ]
    return terms[0]


def project(decoded, held, length, wq, wk, wv, q_out, k_out, v_out, att_out):
    q_out[...] = dot(decoded, wq[...], 1, 0).astype(LOW)
    k_out[...] = dot(held, wk[...], 1, 0).astype(LOW)
    v_out[...] = dot(held, wv[...], 1, 0).astype(LOW)
    rows = held.shape[0]
    allowed = lax.broadcasted_iota(jnp.int32, (1, rows), 1) < length
    for head in range(q_out.shape[1] // HEAD_DIM):
        scores = dot(q_out[:, cols(head)], k_out[:, cols(head)], 1, 1)
        scores = jnp.where(allowed, scores, FULL(-1e30))
        expo = jnp.exp(scores - jnp.max(scores, axis=-1, keepdims=True))
        att_out[head] = expo * (1.0 / jnp.sum(expo, axis=-1, keepdims=True))


def chain(gradient, k_in, v_in, att, wq, wo, cg_out, sg_out, qg_tmp):
    cg_out[...] = dot(gradient.astype(LOW), wo[...], 1, 1).astype(LOW)
    for head in range(cg_out.shape[1] // HEAD_DIM):
        prob = dot(cg_out[:, cols(head)], v_in[:, cols(head)], 1, 1)
        weight = att[head]
        mean = jnp.sum(weight * prob, axis=-1, keepdims=True)
        sg_out[head] = (weight * (prob - mean)).astype(LOW)
        qg_tmp[:, cols(head)] = dot(sg_out[head], k_in[:, cols(head)], 1, 0).astype(LOW)
    return dot(qg_tmp[...], wq[...], 1, 1).astype(LOW)


def memory_terms(q_in, att, cg, sg, wk, wv, kg_tmp, vg_tmp):
    for head in range(cg.shape[1] // HEAD_DIM):
        kg_tmp[:, cols(head)] = dot(sg[head], q_in[:, cols(head)], 0, 0).astype(LOW)
        vg_tmp[:, cols(head)] = dot(att[head].astype(LOW), cg[:, cols(head)], 0, 0).astype(LOW)
    return dot(kg_tmp[...], wk[...], 1, 1) + dot(vg_tmp[...], wv[...], 1, 1)


def split(gradient):
    high = gradient.astype(LOW)
    return high, (gradient - high.astype(FULL)).astype(LOW)


def received(first, others, width):
    base = first[:, width : 2 * width].astype(FULL) + first[:, 2 * width : 3 * width].astype(FULL)
    parts = [first[:, :width].astype(FULL)] + [other[...].astype(FULL) for other in others]
    return base + tree_sum(parts)


def kernel(body, outs, scratch, smem, name):
    vmem = pl.BlockSpec(memory_space=pltpu.VMEM)
    scalar = pl.BlockSpec(memory_space=pltpu.SMEM)

    def call(*args):
        return pl.pallas_call(
            body,
            out_shape=[jax.ShapeDtypeStruct(shape, kind) for shape, kind in outs],
            in_specs=[scalar if i < smem else vmem for i in range(len(args))],
            out_specs=[vmem] * len(outs),
            scratch_shapes=[pltpu.VMEM(shape, kind) for shape, kind in scratch],
            name=name,
        )(*args)

    return call


def body(
    grad_in, memory, enc_grad_in, act_stash, slot_order, lengths, w_query, w_key, w_value, w_out
):
    segments = lax.axis_size("segment")
    groups = lax.axis_size("head")
    rows, width = grad_in.shape[1:]
    enc_rows = memory.shape[1]
    inner = w_query.shape[2]
    heads = inner // HEAD_DIM
    share = enc_grad_in.shape[2]
    wq, wk, wv, wo = w_query[0], w_key[0], w_value[0], w_out[0]
    stash, order, length = act_stash[0], slot_order, lengths
    mine = lax.axis_index("head").astype(jnp.int32).reshape(1)

    def send(value, k):
        pairs = [
            (s * groups + h, ((s - 1) % segments) * groups + (h ^ k))
            for s in range(segments)
            for h in range(groups)
        ]
        return lax.ppermute(value, ("segment", "head"), pairs)

    proj_outs = [
        ((rows, inner), LOW),
        ((enc_rows, inner), LOW),
        ((enc_rows, inner), LOW),
        ((heads, rows, enc_rows), FULL),
    ]
    chain_outs = [((rows, inner), LOW), ((heads, rows, enc_rows), LOW)]
    first_msg = ((rows, 4 * width), LOW)
    part_msg = ((rows, width), LOW)

    def write_first(msg, part_out, part, gradient, held):
        high, low = split(gradient)
        msg[:, :width] = part
        msg[:, width : 2 * width] = high
        msg[:, 2 * width : 3 * width] = low
        msg[:, 3 * width :] = held
        part_out[...] = part

    def open_body(
        order_ref, length_ref, g, mem, stash_ref, wq_, wk_, wv_, wo_,
        q, k, v, att, cg, sg, msg, part_out, tmp,
    ):
        project(stash_ref[order_ref[0, 0]], mem[...], length_ref[0, 0], wq_, wk_, wv_, q, k, v, att)
        part = chain(g[...], k, v, att, wq_, wo_, cg, sg, tmp)
        write_first(msg, part_out, part, g[...], mem[...])

    def fill_body(tick):
        def run(
            order_ref, length_ref, carry, q0, att0, cg, sg, first, stash_ref, wq_, wk_, wv_,
            q, k, v, att, carry_out, kg_tmp, vg_tmp,
        ):
            carry_out[...] = carry[...] + memory_terms(q0, att0, cg, sg, wk_, wv_, kg_tmp, vg_tmp)
            project(
                stash_ref[order_ref[0, tick]], first[:, 3 * width :], length_ref[0, tick],
                wq_, wk_, wv_, q, k, v, att,
            )

        return run

    def step_body(first, *refs):
        others, refs = refs[: groups - 1], refs[groups - 1 :]
        k, v, att, wq_, wo_, cg, sg, msg, part_out, tmp = refs
        gradient = received(first, others, width)
        part = chain(gradient, k, v, att, wq_, wo_, cg, sg, tmp)
        write_first(msg, part_out, part, gradient, first[:, 3 * width :])

    def last_body(mine_ref, first, *refs):
        others, refs = refs[: groups - 1], refs[groups - 1 :]
        carry, q, k, v, att, wq_, wk_, wv_, wo_ = refs[:9]
        msgs, (cg, sg, pieces, tmp, kg_tmp, vg_tmp) = refs[9 : 9 + groups], refs[9 + groups :]
        gradient = received(first, others, width)
        part = chain(gradient, k, v, att, wq_, wo_, cg, sg, tmp)
        total = carry[...] + memory_terms(q, att, cg, sg, wk_, wv_, kg_tmp, vg_tmp)
        for g in range(groups):
            pieces[g] = total[:, g * share : (g + 1) * share].astype(LOW)
        high, low = split(gradient)
        for j, msg in enumerate(msgs):
            base = 3 * width if j == 0 else width
            msg[:, :width] = part
            if j == 0:
                msg[:, width : 2 * width] = high
                msg[:, 2 * width : 3 * width] = low
            msg[:, base:] = pieces[mine_ref[0] ^ j]

    def close_body(first, *refs):
        others, (grad_out, enc_out) = refs[: groups - 1], refs[groups - 1 :]
        grad_out[...] = received(first, [other.at[:, :width] for other in others], width)
        pieces = [first[:, 3 * width :].astype(FULL)]
        pieces += [other[:, width:].astype(FULL) for other in others]
        enc_out[...] = tree_sum(pieces)

    grad_tmp = ((rows, inner), LOW)
    enc_tmp = ((enc_rows, inner), LOW)
    q, k, v, att, cg, sg, msg, part = kernel(
        open_body, proj_outs + chain_outs + [first_msg, part_msg], [grad_tmp], 2, "open"
    )(order, length, grad_in[0], memory[0], stash, wq, wk, wv, wo)
    carry = lax.dynamic_update_slice_in_dim(
        jnp.zeros((enc_rows, width), FULL), enc_grad_in[0], lax.axis_index("head") * share, 1
    )
    for tick in range(1, TICKS):
        others = [send(part, j) for j in range(groups - 1, 0, -1)][::-1]
        first = send(msg, 0)
        q, k, v, att, carry = kernel(
            fill_body(tick), proj_outs + [((enc_rows, width), FULL)], [enc_tmp] * 2, 2, "fill"
        )(order, length, carry, q, att, cg, sg, first, stash, wq, wk, wv)
        carry = send(carry, 0)
        if tick + 1 < TICKS:
            cg, sg, msg, part = kernel(
                step_body, chain_outs + [first_msg, part_msg], [grad_tmp], 0, "step"
            )(first, *others, k, v, att, wq, wo)
    msgs = kernel(
        last_body,
        [((rows, 3 * width + share), LOW)] + [((rows, width + share), LOW)] * (groups - 1),
        chain_outs + [((groups, enc_rows, share), LOW), grad_tmp, enc_tmp, enc_tmp],
        1,
        "last",
    )(mine, first, *others, carry, q, k, v, att, wq, wk, wv, wo)
    others = [send(msgs[j], j) for j in range(groups - 1, 0, -1)][::-1]
    first = send(msgs[0], 0)
    gradient, carried = kernel(
        close_body, [((rows, width), FULL), ((enc_rows, share), FULL)], [], 0, "close"
    )(first, *others)
    return (gradient[None], carried[None])


def solution(mesh):
    in_specs = (
        P("segment", None, None),
        P("segment", None, None),
        P("segment", None, "head"),
        P("segment", None, None, None),
        P("segment", None),
        P("segment", None),
        P("segment", None, "head"),
        P("segment", None, "head"),
        P("segment", None, "head"),
        P("segment", "head", None),
    )
    out_specs = (P("segment", None, None), P("segment", None, "head"))
    return jax.shard_map(body, mesh=mesh, in_specs=in_specs, out_specs=out_specs, check_vma=False)
```

time: 186 us -> 99.8 us (0.54)
  matrix products: 51.4 us -> 0 us
  blocking collectives: 39.4 us -> 0 us
  Pallas kernels: 0 us -> 32 us
  between operations: 19.9 us -> 0.75 us
  local copies, waits for them, and re-layouts: 19.8 us -> 5.43 us
  starting transfers between devices: 10.2 us -> 23 us
  other arithmetic: 7.23 us -> 0 us
    dot_general x33 -> x0, matrix products: 45.1 us -> none  [the longest x3 6.98 us: local_terms(): jnp.einsum('hqk,qhd->khd', attention_low, context_heads, preferred_elemen...]
    all_gather x3 -> x0, blocking collectives: 39.4 us -> none  [the longest x2 24.7 us: body(): lax.all_gather(gradient.astype(jnp.bfloat16), 'head', axis=1, tiled=True)]
    pallas_call x0 -> x6, Pallas kernels: none -> 32 us  [call(): pl.pallas_call(body, out_shape=[jax.ShapeDtypeStruct(shape, kind) for sha...]
    ppermute x8 -> x14, waiting for transfers between devices: 7.54 us -> 37.4 us  [send(): return lax.ppermute(value, ('segment', 'head'), pairs)]
    reduce_scatter x4 -> x0, waiting for transfers between devices: 28.8 us -> none  [the longest x3 24.2 us: body(): lax.psum_scatter(decoder_part, 'head', scatter_dimension=1, tiled=True)]
    reshape x9 -> x0, local copies, waits for them, and re-layouts: 13 us -> none  [the longest x3 5.37 us: local_terms(): key_heads = keys.reshape(enc_rows, head_local, HEAD_DIM)]
    ppermute x8 -> x14, starting transfers between devices: 10 us -> 23 us  [send(): return lax.ppermute(value, ('segment', 'head'), pairs)]
    sub x3 -> x0, matrix products: 6.36 us -> none  [local_terms(): expo = jnp.exp(scores - row_max)]
  transfers between devices with their start and end apart: 12 -> 14, of which waited for: 7 -> 7; matrix products, arithmetic and copies ran while one was open for 40% -> 0% of each run, Pallas kernels for 0% -> 5%
where the time goes in v1:
time: 99.8 us; the launch traced here: 98.7 us
  waiting for transfers between devices  37.4 us (37%)
  Pallas kernels  32 us (32%)
  starting transfers between devices  23 us (23%)
  local copies, waits for them, and re-layouts  5.43 us (5%)
    ppermute x14, waiting for transfers between devices, send(): return lax.ppermute(value, ('segment', 'head'), pairs)  37.4 us
    pallas_call x6, Pallas kernels, call(): pl.pallas_call(body, out_shape=[jax.ShapeDtypeStruct(shape, kind) for sha...  32 us
    ppermute x14, starting transfers between devices, send(): return lax.ppermute(value, ('segment', 'head'), pairs)  23 us
    unnamed x36, local copies, waits for them, and re-layouts  5.4 us
  transfers between devices with their start and end apart: 14, of which 7 were waited for; matrix products, arithmetic and copies ran while one was open for 0% of the time, Pallas kernels for 5%

profile of v1, /device:TPU:0, one launch (start us, length us, event | category | flops | bytes accessed | tf_op | source)
XLA Modules:
  0.0 98.7 jit_solution(3715789036954416330)
XLA Ops:
  0.6 6.4 %open.1 = (bf16[128,1024]{1,0:T(8,128)(2,1)}, bf16[128,1024]{1,0:T(8,128)(2,1)}, bf16[128,1024]{1,0:T(8,128)(2,1)}, f32[8,128,128]{2,1,0:T(8,128)}, bf16[128,102...) custom-call(s32[1,3]{1,0:T(1,128)} %order_ref.5, ...), custom_call_target="tpu_custom_call" | custom-call | tf_op jit(solution)/shard_map/open/pallas_call | solution.py:79
  7.1 3.4 %collective-permute-start = (bf16[128,2048]{1,0:T(8,128)(2,1)}, bf16[128,2048]{1,0:T(8,128)(2,1)S(1)}, u32[]{:S(2)}, u32[]{:S(2)}) collective-permute-start(bf16[128,2048]{1,0:T(8,128)(2,1)} %get-tuple-element.28), channel_id=1, source_target_pairs={{0,28},{1,29},{2,30},{3,31},{4,0},{5,1},{6,2},{7,3},{8,4},{9,5},{1... | collective-permute-start | bytes 1572872 | tf_op jit(solution)/shard_map/ppermute | solution.py:111
  10.4 1.7 %collective-permute-start.1 = (bf16[128,512]{1,0:T(8,128)(2,1)}, bf16[128,512]{1,0:T(8,128)(2,1)S(1)}, u32[]{:S(2)}, u32[]{:S(2)}) collective-permute-start(bf16[128,512]{1,0:T(8,128)(2,1)} %get-tuple-element.29), channel_id=1, source_target_pairs={{0,29},{1,28},{2,31},{3,30},{4,1},{5,0},{6,3},{7,2},{8,5},{9,4},{1... | collective-permute-start | bytes 393224 | tf_op jit(solution)/shard_map/ppermute | solution.py:111
  12.1 2.3 %collective-permute-start.2 = (bf16[128,512]{1,0:T(8,128)(2,1)}, bf16[128,512]{1,0:T(8,128)(2,1)S(1)}, u32[]{:S(2)}, u32[]{:S(2)}) collective-permute-start(bf16[128,512]{1,0:T(8,128)(2,1)} %get-tuple-element.29), channel_id=1, source_target_pairs={{0,30},{1,31},{2,28},{3,29},{4,2},{5,3},{6,0},{7,1},{8,6},{9,7},{1... | collective-permute-start | bytes 393224 | tf_op jit(solution)/shard_map/ppermute | solution.py:111
  15.5 4.4 %collective-permute-done.first = bf16[128,2048]{1,0:T(8,128)(2,1)S(1)} collective-permute-done((bf16[128,2048]{1,0:T(8,128)(2,1)}, bf16[128,2048]{1,0:T(8,128)(2,1)S(1)}, u32[]{:S(2)}, u32[]{:S(2)}) %collective-permute-start) | collective-permute-done | bytes 524320 | tf_op jit(solution)/shard_map/ppermute | solution.py:111
  20.7 5.4 %fill.2 = (bf16[128,1024]{1,0:T(8,128)(2,1)}, bf16[128,1024]{1,0:T(8,128)(2,1)}, bf16[128,1024]{1,0:T(8,128)(2,1)}, f32[8,128,128]{2,1,0:T(8,128)}, f32[128,512]{1,0:T(8,128)}) custom-call(s32[1,3]{1,0:T(1,128)} %order_ref.5, s32[1,3]{1,0:T(1,128)} %length_ref.5, f32[128,512]{1,0:T(8,128)} %copy-done.2, bf16[128,1024]{1,0:T(8,128)(2,1)} %get-tuple-element.30.q0, ...), custom_call_target="tpu_custom_call" | custom-call | tf_op jit(solution)/shard_map/fill/pallas_call | solution.py:79
  26.8 5.6 %step.1 = (bf16[128,1024]{1,0:T(8,128)(2,1)}, bf16[8,128,128]{2,1,0:T(8,128)(2,1)}, bf16[128,2048]{1,0:T(8,128)(2,1)}, bf16[128,512]{1,0:T(8,128)(2,1)}) custom-call(bf16[128,2048]{1,0:T(8,128)(2,1)} %copy-done, bf16[128,512]{1,0:T(8,128)(2,1)} %copy-done.9, bf16[128,512]{1,0:T(8,128)(2,1)} %copy-done.10, bf16[128,512]{1,0:T(8,128)(2,1)} %copy-done.11, ...), custom_call_target="tpu_custom_call" | custom-call | tf_op jit(solution)/shard_map/step/pallas_call | solution.py:79
  32.4 3.0 %collective-permute-start.4 = (bf16[128,2048]{1,0:T(8,128)(2,1)}, bf16[128,2048]{1,0:T(8,128)(2,1)S(1)}, u32[]{:S(2)}, u32[]{:S(2)}) collective-permute-start(bf16[128,2048]{1,0:T(8,128)(2,1)} %get-tuple-element.37), channel_id=1, source_target_pairs={{0,28},{1,29},{2,30},{3,31},{4,0},{5,1},{6,2},{7,3},{8,4},{9,5},{1... | collective-permute-start | bytes 1572872 | tf_op jit(solution)/shard_map/ppermute | solution.py:111
  35.5 9.7 %collective-permute-done.8.carry = f32[128,512]{1,0:T(8,128)S(1)} collective-permute-done((f32[128,512]{1,0:T(8,128)S(1)}, f32[128,512]{1,0:T(8,128)S(1)}, u32[]{:S(2)}, u32[]{:S(2)}) %collective-permute-start.8) | collective-permute-done | bytes 262176 | tf_op jit(solution)/shard_map/ppermute | solution.py:111
  46.0 5.4 %fill.3 = (bf16[128,1024]{1,0:T(8,128)(2,1)}, bf16[128,1024]{1,0:T(8,128)(2,1)}, bf16[128,1024]{1,0:T(8,128)(2,1)}, f32[8,128,128]{2,1,0:T(8,128)}, f32[128,512]{1,0:T(8,128)}) custom-call(s32[1,3]{1,0:T(1,128)} %order_ref.5, s32[1,3]{1,0:T(1,128)} %length_ref.5, f32[128,512]{1,0:T(8,128)} %copy-done.4, bf16[128,1024]{1,0:T(8,128)(2,1)} %get-tuple-element.40.q0, ...), custom_call_target="tpu_custom_call" | custom-call | tf_op jit(solution)/shard_map/fill/pallas_call | solution.py:79
  51.4 2.8 %collective-permute-start.9 = (f32[128,512]{1,0:T(8,128)}, f32[128,512]{1,0:T(8,128)S(1)}, u32[]{:S(2)}, u32[]{:S(2)}) collective-permute-start(f32[128,512]{1,0:T(8,128)} %get-tuple-element.43), channel_id=1, source_target_pairs={{0,28},{1,29},{2,30},{3,31},{4,0},{5,1},{6,2},{7,3},{8,4},{9,5},{1... | collective-permute-start | bytes 786440 | tf_op jit(solution)/shard_map/ppermute | solution.py:111
  54.3 1.2 %collective-permute-start.5 = (bf16[128,512]{1,0:T(8,128)(2,1)S(1)}, bf16[128,512]{1,0:T(8,128)(2,1)S(1)}, u32[]{:S(2)}, u32[]{:S(2)}) collective-permute-start(bf16[128,512]{1,0:T(8,128)(2,1)S(1)} %copy-done.17), channel_id=1, source_target_pairs={{0,29},{1,28},{2,31},{3,30},{4,1},{5,0},{6,3},{7,2},{8,5},{9,4},{1... | collective-permute-start | bytes 393224 | tf_op jit(solution)/shard_map/ppermute | solution.py:111
  55.4 1.1 %collective-permute-start.6 = (bf16[128,512]{1,0:T(8,128)(2,1)S(1)}, bf16[128,512]{1,0:T(8,128)(2,1)S(1)}, u32[]{:S(2)}, u32[]{:S(2)}) collective-permute-start(bf16[128,512]{1,0:T(8,128)(2,1)S(1)} %copy-done.17), channel_id=1, source_target_pairs={{0,30},{1,31},{2,28},{3,29},{4,2},{5,3},{6,0},{7,1},{8,6},{9,7},{1... | collective-permute-start | bytes 393224 | tf_op jit(solution)/shard_map/ppermute | solution.py:111
  56.5 1.1 %collective-permute-start.7 = (bf16[128,512]{1,0:T(8,128)(2,1)S(1)}, bf16[128,512]{1,0:T(8,128)(2,1)S(1)}, u32[]{:S(2)}, u32[]{:S(2)}) collective-permute-start(bf16[128,512]{1,0:T(8,128)(2,1)S(1)} %copy-done.17), channel_id=1, source_target_pairs={{0,31},{1,30},{2,29},{3,28},{4,3},{5,2},{6,1},{7,0},{8,7},{9,6},{1... | collective-permute-start | bytes 393224 | tf_op jit(solution)/shard_map/ppermute | solution.py:111
  57.6 4.9 %collective-permute-done.5.refs_0_ = bf16[128,512]{1,0:T(8,128)(2,1)S(1)} collective-permute-done((bf16[128,512]{1,0:T(8,128)(2,1)S(1)}, bf16[128,512]{1,0:T(8,128)(2,1)S(1)}, u32[]{:S(2)}, u32[]{:S(2)}) %collective-permute-start.5) | collective-permute-done | bytes 131104 | tf_op jit(solution)/shard_map/ppermute | solution.py:111
  62.5 5.4 %collective-permute-done.6.refs_1_ = bf16[128,512]{1,0:T(8,128)(2,1)S(1)} collective-permute-done((bf16[128,512]{1,0:T(8,128)(2,1)S(1)}, bf16[128,512]{1,0:T(8,128)(2,1)S(1)}, u32[]{:S(2)}, u32[]{:S(2)}) %collective-permute-start.6) | collective-permute-done | bytes 131104 | tf_op jit(solution)/shard_map/ppermute | solution.py:111
  68.7 7.2 %last.1 = (bf16[128,1664]{1,0:T(8,128)(2,1)}, bf16[128,640]{1,0:T(8,128)(2,1)}, bf16[128,640]{1,0:T(8,128)(2,1)}, bf16[128,640]{1,0:T(8,128)(2,1)}) custom-call(s32[1]{0:T(128)} %bitcast.mine_ref, bf16[128,2048]{1,0:T(8,128)(2,1)} %copy-done.1, bf16[128,512]{1,0:T(8,128)(2,1)} %copy-done.12, bf16[128,512]{1,0:T(8,128)(2,1)} %copy-done.13, ...), custom_call_target="tpu_custom_call" | custom-call | tf_op jit(solution)/shard_map/last/pallas_call | solution.py:79
  75.9 1.9 %collective-permute-start.10 = (bf16[128,1664]{1,0:T(8,128)(2,1)}, bf16[128,1664]{1,0:T(8,128)(2,1)S(1)}, u32[]{:S(2)}, u32[]{:S(2)}) collective-permute-start(bf16[128,1664]{1,0:T(8,128)(2,1)} %get-tuple-element.48), channel_id=1, source_target_pairs={{0,28},{1,29},{2,30},{3,31},{4,0},{5,1},{6,2},{7,3},{8,4},{9,5},{1... | collective-permute-start | bytes 1277960 | tf_op jit(solution)/shard_map/ppermute | solution.py:111
  77.9 2.7 %collective-permute-start.11 = (bf16[128,640]{1,0:T(8,128)(2,1)}, bf16[128,640]{1,0:T(8,128)(2,1)S(1)}, u32[]{:S(2)}, u32[]{:S(2)}) collective-permute-start(bf16[128,640]{1,0:T(8,128)(2,1)} %get-tuple-element.49), channel_id=1, source_target_pairs={{0,29},{1,28},{2,31},{3,30},{4,1},{5,0},{6,3},{7,2},{8,5},{9,4},{1... | collective-permute-start | bytes 491528 | tf_op jit(solution)/shard_map/ppermute | solution.py:111
  80.6 1.0 collective-permute-start.12
  82.2 3.3 %collective-permute-done.11.refs_0_ = bf16[128,640]{1,0:T(8,128)(2,1)S(1)} collective-permute-done((bf16[128,640]{1,0:T(8,128)(2,1)}, bf16[128,640]{1,0:T(8,128)(2,1)S(1)}, u32[]{:S(2)}, u32[]{:S(2)}) %collective-permute-start.11) | collective-permute-done | bytes 163872 | tf_op jit(solution)/shard_map/ppermute | solution.py:111
  85.5 3.6 %collective-permute-done.12.refs_1_ = bf16[128,640]{1,0:T(8,128)(2,1)S(1)} collective-permute-done((bf16[128,640]{1,0:T(8,128)(2,1)}, bf16[128,640]{1,0:T(8,128)(2,1)S(1)}, u32[]{:S(2)}, u32[]{:S(2)}) %collective-permute-start.12) | collective-permute-done | bytes 163872 | tf_op jit(solution)/shard_map/ppermute | solution.py:111
  89.1 6.1 %collective-permute-done.13.refs_2_ = bf16[128,640]{1,0:T(8,128)(2,1)S(1)} collective-permute-done((bf16[128,640]{1,0:T(8,128)(2,1)}, bf16[128,640]{1,0:T(8,128)(2,1)S(1)}, u32[]{:S(2)}, u32[]{:S(2)}) %collective-permute-start.13) | collective-permute-done | bytes 163872 | tf_op jit(solution)/shard_map/ppermute | solution.py:111
  96.7 2.0 %close.1 = (f32[128,512]{1,0:T(8,128)}, f32[128,128]{1,0:T(8,128)}) custom-call(bf16[128,1664]{1,0:T(8,128)(2,1)} %copy-done.3, bf16[128,640]{1,0:T(8,128)(2,1)} %copy-done.6, bf16[128,640]{1,0:T(8,128)(2,1)} %copy-done.7, bf16[128,640]{1,0:T(8,128)(2,1)} %copy-done.8), custom_call_target="tpu_custom_call" | custom-call | tf_op jit(solution)/shard_map/close/pallas_call | solution.py:79
  (48 shorter events, 6.4 us)
Async XLA Ops:
  7.1 12.8 %collective-permute-start = (bf16[128,2048]{1,0:T(8,128)(2,1)}, bf16[128,2048]{1,0:T(8,128)(2,1)S(1)}, u32[]{:S(2)}, u32[]{:S(2)}) collective-permute-start(bf16[128,2048]{1,0:T(8,128)(2,1)} %get-tuple-element.28), channel_id=1, source_target_pairs={{0,28},{1,29},{2,30},{3,31},{4,0},{5,1},{6,2},{7,3},{8,4},{9,5},{1... | collective-permute-start | bytes 1572872 | tf_op jit(solution)/shard_map/ppermute | solution.py:111
  10.4 15.6 %collective-permute-start.1 = (bf16[128,512]{1,0:T(8,128)(2,1)}, bf16[128,512]{1,0:T(8,128)(2,1)S(1)}, u32[]{:S(2)}, u32[]{:S(2)}) collective-permute-start(bf16[128,512]{1,0:T(8,128)(2,1)} %get-tuple-element.29), channel_id=1, source_target_pairs={{0,29},{1,28},{2,31},{3,30},{4,1},{5,0},{6,3},{7,2},{8,5},{9,4},{1... | collective-permute-start | bytes 393224 | tf_op jit(solution)/shard_map/ppermute | solution.py:111
  12.1 14.0 %collective-permute-start.2 = (bf16[128,512]{1,0:T(8,128)(2,1)}, bf16[128,512]{1,0:T(8,128)(2,1)S(1)}, u32[]{:S(2)}, u32[]{:S(2)}) collective-permute-start(bf16[128,512]{1,0:T(8,128)(2,1)} %get-tuple-element.29), channel_id=1, source_target_pairs={{0,30},{1,31},{2,28},{3,29},{4,2},{5,3},{6,0},{7,1},{8,6},{9,7},{1... | collective-permute-start | bytes 393224 | tf_op jit(solution)/shard_map/ppermute | solution.py:111
  14.4 11.7 %collective-permute-start.3 = (bf16[128,512]{1,0:T(8,128)(2,1)}, bf16[128,512]{1,0:T(8,128)(2,1)S(1)}, u32[]{:S(2)}, u32[]{:S(2)}) collective-permute-start(bf16[128,512]{1,0:T(8,128)(2,1)} %get-tuple-element.29), channel_id=1, source_target_pairs={{0,31},{1,30},{2,29},{3,28},{4,3},{5,2},{6,1},{7,0},{8,7},{9,6},{1... | collective-permute-start | bytes 393224 | tf_op jit(solution)/shard_map/ppermute | solution.py:111
  14.6 0.8 copy-start.15
  15.5 4.4 %copy-start.2 = (f32[128,512]{1,0:T(8,128)}, f32[128,512]{1,0:T(8,128)S(1)}, u32[]{:S(2)}) copy-start(f32[128,512]{1,0:T(8,128)S(1)} %bitcast_dynamic-update-slice_fusion.carry) | copy-start | bytes 786436
  19.9 0.8 copy-start
  26.8 8.6 %copy-start.16 = (f32[128,512]{1,0:T(8,128)S(1)}, f32[128,512]{1,0:T(8,128)}, u32[]{:S(2)}) copy-start(f32[128,512]{1,0:T(8,128)} %get-tuple-element.39) | copy-start | bytes 786436
  32.4 12.7 %collective-permute-start.4 = (bf16[128,2048]{1,0:T(8,128)(2,1)}, bf16[128,2048]{1,0:T(8,128)(2,1)S(1)}, u32[]{:S(2)}, u32[]{:S(2)}) collective-permute-start(bf16[128,2048]{1,0:T(8,128)(2,1)} %get-tuple-element.37), channel_id=1, source_target_pairs={{0,28},{1,29},{2,30},{3,31},{4,0},{5,1},{6,2},{7,3},{8,4},{9,5},{1... | collective-permute-start | bytes 1572872 | tf_op jit(solution)/shard_map/ppermute | solution.py:111
  35.4 9.7 %collective-permute-start.8 = (f32[128,512]{1,0:T(8,128)S(1)}, f32[128,512]{1,0:T(8,128)S(1)}, u32[]{:S(2)}, u32[]{:S(2)}) collective-permute-start(f32[128,512]{1,0:T(8,128)S(1)} %copy-done.16), channel_id=1, source_target_pairs={{0,28},{1,29},{2,30},{3,31},{4,0},{5,1},{6,2},{7,3},{8,4},{9,5},{1... | collective-permute-start | bytes 786440 | tf_op jit(solution)/shard_map/ppermute | solution.py:111
  45.1 0.9 copy-start.1
  46.0 8.2 %copy-start.17 = (bf16[128,512]{1,0:T(8,128)(2,1)S(1)}, bf16[128,512]{1,0:T(8,128)(2,1)}, u32[]{:S(2)}) copy-start(bf16[128,512]{1,0:T(8,128)(2,1)} %get-tuple-element.38) | copy-start | bytes 393220
  51.4 16.5 %collective-permute-start.9 = (f32[128,512]{1,0:T(8,128)}, f32[128,512]{1,0:T(8,128)S(1)}, u32[]{:S(2)}, u32[]{:S(2)}) collective-permute-start(f32[128,512]{1,0:T(8,128)} %get-tuple-element.43), channel_id=1, source_target_pairs={{0,28},{1,29},{2,30},{3,31},{4,0},{5,1},{6,2},{7,3},{8,4},{9,5},{1... | collective-permute-start | bytes 786440 | tf_op jit(solution)/shard_map/ppermute | solution.py:111
  54.3 8.3 %collective-permute-start.5 = (bf16[128,512]{1,0:T(8,128)(2,1)S(1)}, bf16[128,512]{1,0:T(8,128)(2,1)S(1)}, u32[]{:S(2)}, u32[]{:S(2)}) collective-permute-start(bf16[128,512]{1,0:T(8,128)(2,1)S(1)} %copy-done.17), channel_id=1, source_target_pairs={{0,29},{1,28},{2,31},{3,30},{4,1},{5,0},{6,3},{7,2},{8,5},{9,4},{1... | collective-permute-start | bytes 393224 | tf_op jit(solution)/shard_map/ppermute | solution.py:111
  55.4 12.5 %collective-permute-start.6 = (bf16[128,512]{1,0:T(8,128)(2,1)S(1)}, bf16[128,512]{1,0:T(8,128)(2,1)S(1)}, u32[]{:S(2)}, u32[]{:S(2)}) collective-permute-start(bf16[128,512]{1,0:T(8,128)(2,1)S(1)} %copy-done.17), channel_id=1, source_target_pairs={{0,30},{1,31},{2,28},{3,29},{4,2},{5,3},{6,0},{7,1},{8,6},{9,7},{1... | collective-permute-start | bytes 393224 | tf_op jit(solution)/shard_map/ppermute | solution.py:111
  56.5 11.4 %collective-permute-start.7 = (bf16[128,512]{1,0:T(8,128)(2,1)S(1)}, bf16[128,512]{1,0:T(8,128)(2,1)S(1)}, u32[]{:S(2)}, u32[]{:S(2)}) collective-permute-start(bf16[128,512]{1,0:T(8,128)(2,1)S(1)} %copy-done.17), channel_id=1, source_target_pairs={{0,31},{1,30},{2,29},{3,28},{4,3},{5,2},{6,1},{7,0},{8,7},{9,6},{1... | collective-permute-start | bytes 393224 | tf_op jit(solution)/shard_map/ppermute | solution.py:111
  62.5 5.4 %copy-start.12 = (bf16[128,512]{1,0:T(8,128)(2,1)}, bf16[128,512]{1,0:T(8,128)(2,1)S(1)}, u32[]{:S(2)}) copy-start(bf16[128,512]{1,0:T(8,128)(2,1)S(1)} %collective-permute-done.5.refs_0_) | copy-start | bytes 393220
  67.9 0.8 copy-start.5
  75.9 19.3 %collective-permute-start.10 = (bf16[128,1664]{1,0:T(8,128)(2,1)}, bf16[128,1664]{1,0:T(8,128)(2,1)S(1)}, u32[]{:S(2)}, u32[]{:S(2)}) collective-permute-start(bf16[128,1664]{1,0:T(8,128)(2,1)} %get-tuple-element.48), channel_id=1, source_target_pairs={{0,28},{1,29},{2,30},{3,31},{4,0},{5,1},{6,2},{7,3},{8,4},{9,5},{1... | collective-permute-start | bytes 1277960 | tf_op jit(solution)/shard_map/ppermute | solution.py:111
  77.9 7.7 %collective-permute-start.11 = (bf16[128,640]{1,0:T(8,128)(2,1)}, bf16[128,640]{1,0:T(8,128)(2,1)S(1)}, u32[]{:S(2)}, u32[]{:S(2)}) collective-permute-start(bf16[128,640]{1,0:T(8,128)(2,1)} %get-tuple-element.49), channel_id=1, source_target_pairs={{0,29},{1,28},{2,31},{3,30},{4,1},{5,0},{6,3},{7,2},{8,5},{9,4},{1... | collective-permute-start | bytes 491528 | tf_op jit(solution)/shard_map/ppermute | solution.py:111
  80.6 8.5 %collective-permute-start.12 = (bf16[128,640]{1,0:T(8,128)(2,1)}, bf16[128,640]{1,0:T(8,128)(2,1)S(1)}, u32[]{:S(2)}, u32[]{:S(2)}) collective-permute-start(bf16[128,640]{1,0:T(8,128)(2,1)} %get-tuple-element.50), channel_id=1, source_target_pairs={{0,30},{1,31},{2,28},{3,29},{4,2},{5,3},{6,0},{7,1},{8,6},{9,7},{1... | collective-permute-start | bytes 491528 | tf_op jit(solution)/shard_map/ppermute | solution.py:111
  81.6 13.6 %collective-permute-start.13 = (bf16[128,640]{1,0:T(8,128)(2,1)}, bf16[128,640]{1,0:T(8,128)(2,1)S(1)}, u32[]{:S(2)}, u32[]{:S(2)}) collective-permute-start(bf16[128,640]{1,0:T(8,128)(2,1)} %get-tuple-element.51), channel_id=1, source_target_pairs={{0,31},{1,30},{2,29},{3,28},{4,3},{5,2},{6,1},{7,0},{8,7},{9,6},{1... | collective-permute-start | bytes 491528 | tf_op jit(solution)/shard_map/ppermute | solution.py:111
  85.5 9.7 %copy-start.6 = (bf16[128,640]{1,0:T(8,128)(2,1)}, bf16[128,640]{1,0:T(8,128)(2,1)S(1)}, u32[]{:S(2)}) copy-start(bf16[128,640]{1,0:T(8,128)(2,1)S(1)} %collective-permute-done.11.refs_0_) | copy-start | bytes 491524
  89.1 6.2 %copy-start.7 = (bf16[128,640]{1,0:T(8,128)(2,1)}, bf16[128,640]{1,0:T(8,128)(2,1)S(1)}, u32[]{:S(2)}) copy-start(bf16[128,640]{1,0:T(8,128)(2,1)S(1)} %collective-permute-done.12.refs_1_) | copy-start | bytes 491524
  (8 other events, 5.5 us)

commit v2 on v1

v2 whole, which is shorter than its diff:
```python
import jax
import jax.numpy as jnp
from jax import lax
from jax.experimental import pallas as pl
from jax.experimental.pallas import tpu as pltpu
from jax.sharding import PartitionSpec as P


HEAD_DIM = 128
LOW = jnp.bfloat16
FULL = jnp.float32
VMEM_LIMIT = 8 << 20


def dot(a, b, ca, cb):
    return lax.dot_general(a, b, (((ca,), (cb,)), ((), ())), preferred_element_type=FULL)


def cols(head):
    return slice(head * HEAD_DIM, (head + 1) * HEAD_DIM)


def tree_sum(terms):
    terms = list(terms)
    while len(terms) > 1:
        terms = [
            terms[i] + terms[i + 1] if i + 1 < len(terms) else terms[i]
            for i in range(0, len(terms), 2)
        ]
    return terms[0]


def project(decoded, held, allowed, wq, wk, wv, q_out, k_out, v_out, att_out):
    q_out[...] = dot(decoded, wq[...], 1, 0).astype(LOW)
    k_out[...] = dot(held, wk[...], 1, 0).astype(LOW)
    v_out[...] = dot(held, wv[...], 1, 0).astype(LOW)
    for head in range(q_out.shape[1] // HEAD_DIM):
        scores = dot(q_out[:, cols(head)], k_out[:, cols(head)], 1, 1)
        scores = jnp.where(allowed > 0, scores, FULL(-1e30))
        expo = jnp.exp(scores - jnp.max(scores, axis=-1, keepdims=True))
        att_out[head] = expo * (1.0 / jnp.sum(expo, axis=-1, keepdims=True))


def chain(gradient, k_in, v_in, att, wq, wo, cg_out, sg_out, qg_tmp):
    cg_out[...] = dot(gradient.astype(LOW), wo[...], 1, 1).astype(LOW)
    for head in range(cg_out.shape[1] // HEAD_DIM):
        prob = dot(cg_out[:, cols(head)], v_in[:, cols(head)], 1, 1)
        weight = att[head]
        mean = jnp.sum(weight * prob, axis=-1, keepdims=True)
        sg_out[head] = (weight * (prob - mean)).astype(LOW)
        qg_tmp[:, cols(head)] = dot(sg_out[head], k_in[:, cols(head)], 1, 0).astype(LOW)
    return dot(qg_tmp[...], wq[...], 1, 1).astype(LOW)


def memory_terms(q_in, att, cg, sg, wk, wv, kg_tmp, vg_tmp):
    for head in range(cg.shape[1] // HEAD_DIM):
        kg_tmp[:, cols(head)] = dot(sg[head], q_in[:, cols(head)], 0, 0).astype(LOW)
        vg_tmp[:, cols(head)] = dot(att[head].astype(LOW), cg[:, cols(head)], 0, 0).astype(LOW)
    return dot(kg_tmp[...], wk[...], 1, 1) + dot(vg_tmp[...], wv[...], 1, 1)


def split(gradient):
    high = gradient.astype(LOW)
    return high, (gradient - high.astype(FULL)).astype(LOW)


def received(first, others, width):
    base = first[:, width : 2 * width].astype(FULL) + first[:, 2 * width : 3 * width].astype(FULL)
    parts = [first[:, :width].astype(FULL)] + [other[...].astype(FULL) for other in others]
    return base + tree_sum(parts)


def kernel(body, outs, scratch, kinds=None, out_space=pltpu.VMEM):
    def call(*args):
        spaces = list(kinds) + [pltpu.VMEM] * (len(args) - len(kinds)) if kinds else [pltpu.VMEM] * len(args)
        args = [
            arg if space == pltpu.SMEM else pltpu.with_memory_space_constraint(arg, space)
            for arg, space in zip(args, spaces)
        ]
        return pl.pallas_call(
            body,
            out_shape=[out_space(shape, kind) for shape, kind in outs],
            in_specs=[pl.BlockSpec(memory_space=space) for space in spaces],
            out_specs=[pl.BlockSpec(memory_space=pltpu.VMEM)] * len(outs),
            scratch_shapes=scratch,
            compiler_params=pltpu.CompilerParams(vmem_limit_bytes=VMEM_LIMIT),
        )(*args)

    return call


def body(
    grad_in, memory, enc_grad_in, act_stash, slot_order, lengths, w_query, w_key, w_value, w_out
):
    segments = lax.axis_size("segment")
    groups = lax.axis_size("head")
    rows, width = grad_in.shape[1:]
    enc_rows = memory.shape[1]
    inner = w_query.shape[2]
    heads = inner // HEAD_DIM
    share = enc_grad_in.shape[2]
    ticks = act_stash.shape[1]
    mine = lax.axis_index("head").astype(jnp.int32).reshape(1)

    def send(value, k):
        pairs = [
            (s * groups + h, ((s - 1) % segments) * groups + (h ^ k))
            for s in range(segments)
            for h in range(groups)
        ]
        return lax.ppermute(value, ("segment", "head"), pairs)

    def exchange(first, part):
        head = send(first, 0)
        others = []
        for j in range(1, groups):
            others.append(send(part[j] if isinstance(part, list) else part, j))
        return head, others

    proj_outs = [
        ((rows, inner), LOW),
        ((enc_rows, inner), LOW),
        ((enc_rows, inner), LOW),
        ((heads, rows, enc_rows), FULL),
    ]
    chain_outs = [((rows, inner), LOW), ((heads, rows, enc_rows), LOW)]
    part_msg = ((rows, width), LOW)
    inner_tmp = pltpu.VMEM((rows, inner), LOW)
    held_at = slice(3 * width, 4 * width)
    carry_at = slice(4 * width, 5 * width)

    def write_first(msg, part_out, part, gradient, held):
        high, low = split(gradient)
        msg[:, :width] = part
        msg[:, width : 2 * width] = high
        msg[:, 2 * width : 3 * width] = low
        msg[:, held_at] = held
        part_out[...] = part

    def open_body(mine_ref, order_ref, length_ref, *refs):
        (stash, *hbm), refs = refs[:7], refs[7:]
        (q, att, cg, sg, msg, part_out, own, dec, allowed, *weights), refs = refs[:13], refs[13:]
        wq, wk, wv, wo = weights
        g, mem, k, v, tmp, sems = refs
        local = [wq, mem, wk, g, wo, wv]
        copies = [
            pltpu.make_async_copy(stash.at[0, order_ref[0, t]], dec.at[t], sems.at[len(local) + t])
            for t in range(ticks)
        ]
        copies += [
            pltpu.make_async_copy(src.at[0], dst, sems.at[i])
            for i, (src, dst) in enumerate(zip(hbm, local))
        ]
        for copy in copies:
            copy.start()
        positions = lax.broadcasted_iota(jnp.int32, (1, enc_rows), 1)
        for t in range(ticks):
            allowed[t : t + 1, :] = (positions < length_ref[0, t]).astype(FULL)
        heads_at = lax.broadcasted_iota(jnp.int32, own.shape, 1)
        own[...] = (heads_at == mine_ref[0]).astype(FULL)
        for copy in copies:
            copy.wait()
        project(dec[0], mem[...], allowed[0:1, :], wq, wk, wv, q, k, v, att)
        part = chain(g[...], k, v, att, wq, wo, cg, sg, tmp)
        write_first(msg, part_out, part, g[...], mem[...])

    def memory_open_body(own, enc, q, att, cg, sg, wk, wv, carry_out, kg_tmp, vg_tmp):
        total = memory_terms(q, att, cg, sg, wk, wv, kg_tmp, vg_tmp)
        for g in range(groups):
            at = slice(g * share, (g + 1) * share)
            carry_out[:, at] = (total[:, at] + enc[0] * own[0:1, g : g + 1]).astype(LOW)

    def memory_body(first, q, att, cg, sg, wk, wv, carry_out, kg_tmp, vg_tmp):
        total = memory_terms(q, att, cg, sg, wk, wv, kg_tmp, vg_tmp)
        carry_out[...] = first[:, carry_at].astype(FULL) + total

    def project_body(tick):
        def run(first, dec, allowed, wq, wk, wv, q, k, v, att):
            at = slice(tick, tick + 1)
            project(dec[tick], first[:, held_at], allowed[at, :], wq, wk, wv, q, k, v, att)

        return run

    def step_body(first, *refs):
        others, refs = refs[: groups - 1], refs[groups - 1 :]
        carry, k, v, att, wq, wo, cg, sg, msg, part_out, tmp = refs
        gradient = received(first, others, width)
        part = chain(gradient, k, v, att, wq, wo, cg, sg, tmp)
        write_first(msg, part_out, part, gradient, first[:, held_at])
        msg[:, carry_at] = carry[...]

    def last_body(mine_ref, first, *refs):
        others, refs = refs[: groups - 1], refs[groups - 1 :]
        carry, q, k, v, att, wq, wk, wv, wo = refs[:9]
        msgs, (cg, sg, pieces, tmp, kg_tmp, vg_tmp) = refs[9 : 9 + groups], refs[9 + groups :]
        gradient = received(first, others, width)
        part = chain(gradient, k, v, att, wq, wo, cg, sg, tmp)
        total = carry[...] + memory_terms(q, att, cg, sg, wk, wv, kg_tmp, vg_tmp)
        for g in range(groups):
            pieces[g] = total[:, g * share : (g + 1) * share].astype(LOW)
        high, low = split(gradient)
        for j, msg in enumerate(msgs):
            base = 3 * width if j == 0 else width
            msg[:, :width] = part
            if j == 0:
                msg[:, width : 2 * width] = high
                msg[:, 2 * width : 3 * width] = low
            msg[:, base:] = pieces[mine_ref[0] ^ j]

    def close_body(first, *refs):
        others, (grad_out, enc_out) = refs[: groups - 1], refs[groups - 1 :]
        grad_out[...] = received(first, [other.at[:, :width] for other in others], width)
        pieces = [first[:, 3 * width :].astype(FULL)]
        pieces += [other[:, width:].astype(FULL) for other in others]
        enc_out[...] = tree_sum(pieces)

    smem = pltpu.SMEM
    open_outs = proj_outs[:1] + proj_outs[3:] + chain_outs + [((rows, 4 * width), LOW), part_msg]
    open_outs += [((8, groups), FULL), (act_stash.shape[1:], LOW), ((8, enc_rows), FULL)]
    open_outs += [(w.shape[1:], LOW) for w in (w_query, w_key, w_value, w_out)]
    q, att, cg, sg, msg, part, own, dec, allowed, wq, wk, wv, wo = kernel(
        open_body,
        open_outs,
        [
            pltpu.VMEM((rows, width), FULL),
            pltpu.VMEM((enc_rows, width), LOW),
            pltpu.VMEM((enc_rows, inner), LOW),
            pltpu.VMEM((enc_rows, inner), LOW),
            inner_tmp,
            pltpu.SemaphoreType.DMA((6 + ticks,)),
        ],
        [smem] * 3 + [pltpu.HBM] * 7,
    )(mine, slot_order, lengths, act_stash, w_query, memory, w_key, grad_in, w_out, w_value)
    first, others = exchange(msg, part)
    (carry,) = kernel(memory_open_body, [((enc_rows, width), LOW)], [inner_tmp] * 2)(
        own, enc_grad_in, q, att, cg, sg, wk, wv
    )
    q, k, v, att = kernel(project_body(1), proj_outs, [])(first, dec, allowed, wq, wk, wv)
    cg, sg, msg, part = kernel(
        step_body, chain_outs + [((rows, 5 * width), LOW), part_msg], [inner_tmp]
    )(first, *others, carry, k, v, att, wq, wo)
    first, others = exchange(msg, part)
    (carry,) = kernel(memory_body, [((enc_rows, width), FULL)], [inner_tmp] * 2)(
        first, q, att, cg, sg, wk, wv
    )
    carry = send(carry, 0)
    q, k, v, att = kernel(project_body(2), proj_outs, [])(first, dec, allowed, wq, wk, wv)
    msgs = kernel(
        last_body,
        [((rows, 3 * width + share), LOW)] + [((rows, width + share), LOW)] * (groups - 1),
        [pltpu.VMEM(*shape) for shape in chain_outs]
        + [pltpu.VMEM((groups, enc_rows, share), LOW), inner_tmp, inner_tmp, inner_tmp],
        [smem],
    )(mine, first, *others, carry, q, k, v, att, wq, wk, wv, wo)
    first, others = exchange(msgs[0], list(msgs))
    gradient, carried = kernel(
        close_body, [((rows, width), FULL), ((enc_rows, share), FULL)], [],
        out_space=jax.ShapeDtypeStruct,
    )(first, *others)
    return (gradient[None], carried[None])


def solution(mesh):
    in_specs = (
        P("segment", None, None),
        P("segment", None, None),
        P("segment", None, "head"),
        P("segment", None, None, None),
        P("segment", None),
        P("segment", None),
        P("segment", None, "head"),
        P("segment", None, "head"),
        P("segment", None, "head"),
        P("segment", "head", None),
    )
    out_specs = (P("segment", None, None), P("segment", None, "head"))

    return jax.shard_map(body, mesh=mesh, in_specs=in_specs, out_specs=out_specs, check_vma=False)
```

time: 99.8 us -> 77.7 us (0.78)
  Pallas kernels: 32 us -> 17.1 us
  local copies, waits for them, and re-layouts: 5.43 us -> 0.66 us
  starting transfers between devices: 23 us -> 20.4 us
    pallas_call x6 -> x8, Pallas kernels: 32 us -> 17.1 us  [call(): pl.pallas_call(body, out_shape=[out_space(shape, kind) for shape, kind in...]
    unnamed x36 -> x6, local copies, waits for them, and re-layouts: 5.4 us -> 0.66 us
    ppermute x14 -> x13, starting transfers between devices: 23 us -> 20.4 us  [send(): return lax.ppermute(value, ('segment', 'head'), pairs)]
    ppermute x14 -> x13, waiting for transfers between devices: 37.4 us -> 37.7 us  [send(): return lax.ppermute(value, ('segment', 'head'), pairs)]
  transfers between devices with their start and end apart: 14 -> 13, of which waited for: 7 -> 7; matrix products, arithmetic and copies ran while one was open for 0% -> 0% of each run, Pallas kernels for 5% -> 4%
where the time goes in v2:
time: 77.7 us; the launch traced here: 76.5 us
  waiting for transfers between devices  37.7 us (49%)
  starting transfers between devices  20.4 us (26%)
  Pallas kernels  17.1 us (22%)
    ppermute x13, waiting for transfers between devices, send(): return lax.ppermute(value, ('segment', 'head'), pairs)  37.7 us
    ppermute x13, starting transfers between devices, send(): return lax.ppermute(value, ('segment', 'head'), pairs)  20.4 us
    pallas_call x8, Pallas kernels, call(): pl.pallas_call(body, out_shape=[out_space(shape, kind) for shape, kind in...  17.1 us
  transfers between devices with their start and end apart: 13, of which 7 were waited for; matrix products, arithmetic and copies ran while one was open for 0% of the time, Pallas kernels for 4%

profile of v2, /device:TPU:0, one launch (start us, length us, event | category | flops | bytes accessed | tf_op | source)
XLA Modules:
  0.0 76.5 jit_solution(16545836922348198359)
XLA Ops:
  0.7 0.6 copy-done.1
  1.3 6.4 %shard_map.113 = (bf16[128,1024]{1,0:T(8,128)(2,1)S(1)}, f32[8,128,128]{2,1,0:T(8,128)S(1)}, bf16[128,1024]{1,0:T(8,128)(2,1)S(1)}, bf16[8,128,128]{2,1,0:T(8,12...) custom-call(s32[1]{0:T(128)} %bitcast.mine_ref, ...), custom_call_target="tpu_custom_call" | custom-call | tf_op jit(solution)/shard_map/pallas_call | solution.py:80
  7.7 3.4 %collective-permute-start = (bf16[128,2048]{1,0:T(8,128)(2,1)S(1)}, bf16[128,2048]{1,0:T(8,128)(2,1)S(1)}, u32[]{:S(2)}, u32[]{:S(2)}) collective-permute-start(bf16[128,2048]{1,0:T(8,128)(2,1)S(1)} %get-tuple-element.33), channel_id=1, source_target_pairs={{0,28},{1,29},{2,30},{3,31},{4,0},{5,1},{6,2},{7,3},{8,4},{9,5},{1... | collective-permute-start | bytes 1572872 | tf_op jit(solution)/shard_map/ppermute | solution.py:111
  11.1 3.7 %collective-permute-start.3 = (bf16[128,512]{1,0:T(8,128)(2,1)S(1)}, bf16[128,512]{1,0:T(8,128)(2,1)S(1)}, u32[]{:S(2)}, u32[]{:S(2)}) collective-permute-start(bf16[128,512]{1,0:T(8,128)(2,1)S(1)} %get-tuple-element.34), channel_id=1, source_target_pairs={{0,31},{1,30},{2,29},{3,28},{4,3},{5,2},{6,1},{7,0},{8,7},{9,6},{1... | collective-permute-start | bytes 393224 | tf_op jit(solution)/shard_map/ppermute | solution.py:111
  14.8 0.5 collective-permute-start.1
  15.3 1.1 %shard_map.114.refs_3_ = bf16[128,512]{1,0:T(8,128)(2,1)S(1)} custom-call(f32[8,4]{1,0:T(8,128)S(1)} %get-tuple-element.35.own, f32[1,128,128]{2,1,0:T(8,128)S(1)} %copy-done, bf16[128,1024]{1,0:T(8,128)(2,1)S(1)} %get-tuple-element.36.q, f32[8,128,128]{2,1,0:T(8,128)S(1)} %get-tuple-element.37.att, bf16[128,1024]{1,0:T(8,128)(2,1)S(1)} %get-tuple-element.38.cg, ...), custom_call_target="tpu_custom_call" | custom-call | tf_op jit(solution)/shard_map/pallas_call | solution.py:80
  16.4 4.1 %collective-permute-done.first = bf16[128,2048]{1,0:T(8,128)(2,1)S(1)} collective-permute-done((bf16[128,2048]{1,0:T(8,128)(2,1)S(1)}, bf16[128,2048]{1,0:T(8,128)(2,1)S(1)}, u32[]{:S(2)}, u32[]{:S(2)}) %collective-permute-start) | collective-permute-done | bytes 524320 | tf_op jit(solution)/shard_map/ppermute | solution.py:111
  20.5 1.0 %shard_map.115 = (bf16[128,1024]{1,0:T(8,128)(2,1)S(1)}, bf16[128,1024]{1,0:T(8,128)(2,1)S(1)}, bf16[128,1024]{1,0:T(8,128)(2,1)S(1)}, f32[8,128,128]{2,1,0:T(8,128)S(1)}) custom-call(bf16[128,2048]{1,0:T(8,128)(2,1)S(1)} %collective-permute-done.first, bf16[3,128,512]{2,1,0:T(8,128)(2,1)S(1)} %get-tuple-element.42.dec, ...), custom_call_target="tpu_custom_call" | custom-call | tf_op jit(solution)/shard_map/pallas_call | solution.py:80
  21.5 4.2 %collective-permute-done.2.refs_1_ = bf16[128,512]{1,0:T(8,128)(2,1)S(1)} collective-permute-done((bf16[128,512]{1,0:T(8,128)(2,1)S(1)}, bf16[128,512]{1,0:T(8,128)(2,1)S(1)}, u32[]{:S(2)}, u32[]{:S(2)}) %collective-permute-start.2) | collective-permute-done | bytes 131104 | tf_op jit(solution)/shard_map/ppermute | solution.py:111
  25.6 2.5 %shard_map.116 = (bf16[128,1024]{1,0:T(8,128)(2,1)S(1)}, bf16[8,128,128]{2,1,0:T(8,128)(2,1)S(1)}, bf16[128,2560]{1,0:T(8,128)(2,1)S(1)}, bf16[128,512]{1,0:T(8,128)(2,1)S(1)}) custom-call(bf16[128,2048]{1,0:T(8,128)(2,1)S(1)} %collective-permute-done.first, bf16[128,512]{1,0:T(8,128)(2,1)S(1)} %collective-permute-done.1.refs_0_, ...), custom_call_target="tpu_custom_call" | custom-call | tf_op jit(solution)/shard_map/pallas_call | solution.py:80
  28.1 2.5 %collective-permute-start.4 = (bf16[128,2560]{1,0:T(8,128)(2,1)S(1)}, bf16[128,2560]{1,0:T(8,128)(2,1)S(1)}, u32[]{:S(2)}, u32[]{:S(2)}) collective-permute-start(bf16[128,2560]{1,0:T(8,128)(2,1)S(1)} %get-tuple-element.49), channel_id=1, source_target_pairs={{0,28},{1,29},{2,30},{3,31},{4,0},{5,1},{6,2},{7,3},{8,4},{9,5},{1... | collective-permute-start | bytes 1966088 | tf_op jit(solution)/shard_map/ppermute | solution.py:111
  30.7 8.1 %collective-permute-done.4.first = bf16[128,2560]{1,0:T(8,128)(2,1)S(1)} collective-permute-done((bf16[128,2560]{1,0:T(8,128)(2,1)S(1)}, bf16[128,2560]{1,0:T(8,128)(2,1)S(1)}, u32[]{:S(2)}, u32[]{:S(2)}) %collective-permute-start.4) | collective-permute-done | bytes 655392 | tf_op jit(solution)/shard_map/ppermute | solution.py:111
  38.8 1.1 %shard_map.117 = f32[128,512]{1,0:T(8,128)S(1)} custom-call(bf16[128,2560]{1,0:T(8,128)(2,1)S(1)} %collective-permute-done.4.first, bf16[128,1024]{1,0:T(8,128)(2,1)S(1)} %get-tuple-element.51.q, f32[8,128,128]{2,1,0:T(8,128)S(1)} %get-tuple-element.47.refs_6_.att, bf16[128,1024]{1,0:T(8,128)(2,1)S(1)} %get-tuple-element.52.cg, ...), custom_call_target="tpu_custom_call" | custom-call | tf_op jit(solution)/shard_map/pallas_call | solution.py:80
  39.9 2.9 %collective-permute-start.8 = (f32[128,512]{1,0:T(8,128)S(1)}, f32[128,512]{1,0:T(8,128)S(1)}, u32[]{:S(2)}, u32[]{:S(2)}) collective-permute-start(f32[128,512]{1,0:T(8,128)S(1)} %shard_map.117), channel_id=1, source_target_pairs={{0,28},{1,29},{2,30},{3,31},{4,0},{5,1},{6,2},{7,3},{8,4},{9,5},{1... | collective-permute-start | bytes 786440 | tf_op jit(solution)/shard_map/ppermute | solution.py:111
  42.7 2.0 %collective-permute-start.7 = (bf16[128,512]{1,0:T(8,128)(2,1)S(1)}, bf16[128,512]{1,0:T(8,128)(2,1)S(1)}, u32[]{:S(2)}, u32[]{:S(2)}) collective-permute-start(bf16[128,512]{1,0:T(8,128)(2,1)S(1)} %get-tuple-element.50), channel_id=1, source_target_pairs={{0,31},{1,30},{2,29},{3,28},{4,3},{5,2},{6,1},{7,0},{8,7},{9,6},{1... | collective-permute-start | bytes 393224 | tf_op jit(solution)/shard_map/ppermute | solution.py:111
  45.0 1.0 %shard_map.118 = (bf16[128,1024]{1,0:T(8,128)(2,1)S(1)}, bf16[128,1024]{1,0:T(8,128)(2,1)S(1)}, bf16[128,1024]{1,0:T(8,128)(2,1)S(1)}, f32[8,128,128]{2,1,0:T(8,128)S(1)}) custom-call(bf16[128,2560]{1,0:T(8,128)(2,1)S(1)} %collective-permute-done.4.first, bf16[3,128,512]{2,1,0:T(8,128)(2,1)S(1)} %get-tuple-element.42.dec, ...), custom_call_target="tpu_custom_call" | custom-call | tf_op jit(solution)/shard_map/pallas_call | solution.py:80
  45.9 4.4 %collective-permute-done.7.refs_2_ = bf16[128,512]{1,0:T(8,128)(2,1)S(1)} collective-permute-done((bf16[128,512]{1,0:T(8,128)(2,1)S(1)}, bf16[128,512]{1,0:T(8,128)(2,1)S(1)}, u32[]{:S(2)}, u32[]{:S(2)}) %collective-permute-start.7) | collective-permute-done | bytes 131104 | tf_op jit(solution)/shard_map/ppermute | solution.py:111
  50.3 5.8 %collective-permute-done.6.refs_1_ = bf16[128,512]{1,0:T(8,128)(2,1)S(1)} collective-permute-done((bf16[128,512]{1,0:T(8,128)(2,1)S(1)}, bf16[128,512]{1,0:T(8,128)(2,1)S(1)}, u32[]{:S(2)}, u32[]{:S(2)}) %collective-permute-start.6) | collective-permute-done | bytes 131104 | tf_op jit(solution)/shard_map/ppermute | solution.py:111
  56.1 3.3 %shard_map.119 = (bf16[128,1664]{1,0:T(8,128)(2,1)S(1)}, bf16[128,640]{1,0:T(8,128)(2,1)S(1)}, bf16[128,640]{1,0:T(8,128)(2,1)S(1)}, bf16[128,640]{1,0:T(8,128)(2,1)S(1)}) custom-call(s32[1]{0:T(128)} %bitcast.mine_ref, bf16[128,2560]{1,0:T(8,128)(2,1)S(1)} %collective-permute-done.4.first, bf16[128,512]{1,0:T(8,128)(2,1)S(1)} %collective-permute-done.5.refs_0_, ...), custom_call_target="tpu_custom_call" | custom-call | tf_op jit(solution)/shard_map/pallas_call | solution.py:80
  59.4 1.9 %collective-permute-start.9 = (bf16[128,1664]{1,0:T(8,128)(2,1)S(1)}, bf16[128,1664]{1,0:T(8,128)(2,1)S(1)}, u32[]{:S(2)}, u32[]{:S(2)}) collective-permute-start(bf16[128,1664]{1,0:T(8,128)(2,1)S(1)} %get-tuple-element.58), channel_id=1, source_target_pairs={{0,28},{1,29},{2,30},{3,31},{4,0},{5,1},{6,2},{7,3},{8,4},{9,5},{1... | collective-permute-start | bytes 1277960 | tf_op jit(solution)/shard_map/ppermute | solution.py:111
  61.4 3.2 %collective-permute-start.12 = (bf16[128,640]{1,0:T(8,128)(2,1)S(1)}, bf16[128,640]{1,0:T(8,128)(2,1)S(1)}, u32[]{:S(2)}, u32[]{:S(2)}) collective-permute-start(bf16[128,640]{1,0:T(8,128)(2,1)S(1)} %get-tuple-element.61), channel_id=1, source_target_pairs={{0,31},{1,30},{2,29},{3,28},{4,3},{5,2},{6,1},{7,0},{8,7},{9,6},{1... | collective-permute-start | bytes 491528 | tf_op jit(solution)/shard_map/ppermute | solution.py:111
  64.6 5.7 %collective-permute-done.10.refs_0_ = bf16[128,640]{1,0:T(8,128)(2,1)S(1)} collective-permute-done((bf16[128,640]{1,0:T(8,128)(2,1)S(1)}, bf16[128,640]{1,0:T(8,128)(2,1)S(1)}, u32[]{:S(2)}, u32[]{:S(2)}) %collective-permute-start.10) | collective-permute-done | bytes 163872 | tf_op jit(solution)/shard_map/ppermute | solution.py:111
  70.2 5.5 %collective-permute-done.11.refs_1_ = bf16[128,640]{1,0:T(8,128)(2,1)S(1)} collective-permute-done((bf16[128,640]{1,0:T(8,128)(2,1)S(1)}, bf16[128,640]{1,0:T(8,128)(2,1)S(1)}, u32[]{:S(2)}, u32[]{:S(2)}) %collective-permute-start.11) | collective-permute-done | bytes 163872 | tf_op jit(solution)/shard_map/ppermute | solution.py:111
  75.7 0.8 %shard_map.120 = (f32[128,512]{1,0:T(8,128)}, f32[128,128]{1,0:T(8,128)}) custom-call(bf16[128,1664]{1,0:T(8,128)(2,1)S(1)} %collective-permute-done.9.first, bf16[128,640]{1,0:T(8,128)(2,1)S(1)} %collective-permute-done.10.refs_0_, bf16[128,640]{1,0:T(8,128)(2,1)S(1)} %collective-permute-done.11.refs_1_, bf16[128,640]{1,0:T(8,128)(2,1)S(1)} %collective-permute-done.12.refs_2_), custom_call_target="tpu_custom_call" | custom-call | tf_op jit(solution)/shard_map/pallas_call | solution.py:80
  (16 shorter events, 0.3 us)
Async XLA Ops:
  0.6 0.7 copy-start.1
  0.6 0.7 copy-start.2
  1.3 14.0 %copy-start = (f32[1,128,128]{2,1,0:T(8,128)S(1)}, f32[1,128,128]{2,1,0:T(8,128)}, u32[]{:S(2)}) copy-start(f32[1,128,128]{2,1,0:T(8,128)} %enc.1) | copy-start | bytes 196612
  7.7 12.8 %collective-permute-start = (bf16[128,2048]{1,0:T(8,128)(2,1)S(1)}, bf16[128,2048]{1,0:T(8,128)(2,1)S(1)}, u32[]{:S(2)}, u32[]{:S(2)}) collective-permute-start(bf16[128,2048]{1,0:T(8,128)(2,1)S(1)} %get-tuple-element.33), channel_id=1, source_target_pairs={{0,28},{1,29},{2,30},{3,31},{4,0},{5,1},{6,2},{7,3},{8,4},{9,5},{1... | collective-permute-start | bytes 1572872 | tf_op jit(solution)/shard_map/ppermute | solution.py:111
  11.1 10.4 %collective-permute-start.3 = (bf16[128,512]{1,0:T(8,128)(2,1)S(1)}, bf16[128,512]{1,0:T(8,128)(2,1)S(1)}, u32[]{:S(2)}, u32[]{:S(2)}) collective-permute-start(bf16[128,512]{1,0:T(8,128)(2,1)S(1)} %get-tuple-element.34), channel_id=1, source_target_pairs={{0,31},{1,30},{2,29},{3,28},{4,3},{5,2},{6,1},{7,0},{8,7},{9,6},{1... | collective-permute-start | bytes 393224 | tf_op jit(solution)/shard_map/ppermute | solution.py:111
  14.8 10.8 %collective-permute-start.2 = (bf16[128,512]{1,0:T(8,128)(2,1)S(1)}, bf16[128,512]{1,0:T(8,128)(2,1)S(1)}, u32[]{:S(2)}, u32[]{:S(2)}) collective-permute-start(bf16[128,512]{1,0:T(8,128)(2,1)S(1)} %get-tuple-element.34), channel_id=1, source_target_pairs={{0,30},{1,31},{2,28},{3,29},{4,2},{5,3},{6,0},{7,1},{8,6},{9,7},{1... | collective-permute-start | bytes 393224 | tf_op jit(solution)/shard_map/ppermute | solution.py:111
  14.8 10.8 %collective-permute-start.1 = (bf16[128,512]{1,0:T(8,128)(2,1)S(1)}, bf16[128,512]{1,0:T(8,128)(2,1)S(1)}, u32[]{:S(2)}, u32[]{:S(2)}) collective-permute-start(bf16[128,512]{1,0:T(8,128)(2,1)S(1)} %get-tuple-element.34), channel_id=1, source_target_pairs={{0,29},{1,28},{2,31},{3,30},{4,1},{5,0},{6,3},{7,2},{8,5},{9,4},{1... | collective-permute-start | bytes 393224 | tf_op jit(solution)/shard_map/ppermute | solution.py:111
  28.1 10.6 %collective-permute-start.4 = (bf16[128,2560]{1,0:T(8,128)(2,1)S(1)}, bf16[128,2560]{1,0:T(8,128)(2,1)S(1)}, u32[]{:S(2)}, u32[]{:S(2)}) collective-permute-start(bf16[128,2560]{1,0:T(8,128)(2,1)S(1)} %get-tuple-element.49), channel_id=1, source_target_pairs={{0,28},{1,29},{2,30},{3,31},{4,0},{5,1},{6,2},{7,3},{8,4},{9,5},{1... | collective-permute-start | bytes 1966088 | tf_op jit(solution)/shard_map/ppermute | solution.py:111
  39.9 16.3 %collective-permute-start.8 = (f32[128,512]{1,0:T(8,128)S(1)}, f32[128,512]{1,0:T(8,128)S(1)}, u32[]{:S(2)}, u32[]{:S(2)}) collective-permute-start(f32[128,512]{1,0:T(8,128)S(1)} %shard_map.117), channel_id=1, source_target_pairs={{0,28},{1,29},{2,30},{3,31},{4,0},{5,1},{6,2},{7,3},{8,4},{9,5},{1... | collective-permute-start | bytes 786440 | tf_op jit(solution)/shard_map/ppermute | solution.py:111
  42.7 7.6 %collective-permute-start.7 = (bf16[128,512]{1,0:T(8,128)(2,1)S(1)}, bf16[128,512]{1,0:T(8,128)(2,1)S(1)}, u32[]{:S(2)}, u32[]{:S(2)}) collective-permute-start(bf16[128,512]{1,0:T(8,128)(2,1)S(1)} %get-tuple-element.50), channel_id=1, source_target_pairs={{0,31},{1,30},{2,29},{3,28},{4,3},{5,2},{6,1},{7,0},{8,7},{9,6},{1... | collective-permute-start | bytes 393224 | tf_op jit(solution)/shard_map/ppermute | solution.py:111
  44.7 11.4 %collective-permute-start.6 = (bf16[128,512]{1,0:T(8,128)(2,1)S(1)}, bf16[128,512]{1,0:T(8,128)(2,1)S(1)}, u32[]{:S(2)}, u32[]{:S(2)}) collective-permute-start(bf16[128,512]{1,0:T(8,128)(2,1)S(1)} %get-tuple-element.50), channel_id=1, source_target_pairs={{0,30},{1,31},{2,28},{3,29},{4,2},{5,3},{6,0},{7,1},{8,6},{9,7},{1... | collective-permute-start | bytes 393224 | tf_op jit(solution)/shard_map/ppermute | solution.py:111
  44.7 11.4 %collective-permute-start.5 = (bf16[128,512]{1,0:T(8,128)(2,1)S(1)}, bf16[128,512]{1,0:T(8,128)(2,1)S(1)}, u32[]{:S(2)}, u32[]{:S(2)}) collective-permute-start(bf16[128,512]{1,0:T(8,128)(2,1)S(1)} %get-tuple-element.50), channel_id=1, source_target_pairs={{0,29},{1,28},{2,31},{3,30},{4,1},{5,0},{6,3},{7,2},{8,5},{9,4},{1... | collective-permute-start | bytes 393224 | tf_op jit(solution)/shard_map/ppermute | solution.py:111
  59.4 16.3 %collective-permute-start.9 = (bf16[128,1664]{1,0:T(8,128)(2,1)S(1)}, bf16[128,1664]{1,0:T(8,128)(2,1)S(1)}, u32[]{:S(2)}, u32[]{:S(2)}) collective-permute-start(bf16[128,1664]{1,0:T(8,128)(2,1)S(1)} %get-tuple-element.58), channel_id=1, source_target_pairs={{0,28},{1,29},{2,30},{3,31},{4,0},{5,1},{6,2},{7,3},{8,4},{9,5},{1... | collective-permute-start | bytes 1277960 | tf_op jit(solution)/shard_map/ppermute | solution.py:111
  61.4 8.8 %collective-permute-start.10 = (bf16[128,640]{1,0:T(8,128)(2,1)S(1)}, bf16[128,640]{1,0:T(8,128)(2,1)S(1)}, u32[]{:S(2)}, u32[]{:S(2)}) collective-permute-start(bf16[128,640]{1,0:T(8,128)(2,1)S(1)} %get-tuple-element.59), channel_id=1, source_target_pairs={{0,29},{1,28},{2,31},{3,30},{4,1},{5,0},{6,3},{7,2},{8,5},{9,4},{1... | collective-permute-start | bytes 491528 | tf_op jit(solution)/shard_map/ppermute | solution.py:111
  61.4 14.3 %collective-permute-start.11 = (bf16[128,640]{1,0:T(8,128)(2,1)S(1)}, bf16[128,640]{1,0:T(8,128)(2,1)S(1)}, u32[]{:S(2)}, u32[]{:S(2)}) collective-permute-start(bf16[128,640]{1,0:T(8,128)(2,1)S(1)} %get-tuple-element.60), channel_id=1, source_target_pairs={{0,30},{1,31},{2,28},{3,29},{4,2},{5,3},{6,0},{7,1},{8,6},{9,7},{1... | collective-permute-start | bytes 491528 | tf_op jit(solution)/shard_map/ppermute | solution.py:111
  61.4 14.3 %collective-permute-start.12 = (bf16[128,640]{1,0:T(8,128)(2,1)S(1)}, bf16[128,640]{1,0:T(8,128)(2,1)S(1)}, u32[]{:S(2)}, u32[]{:S(2)}) collective-permute-start(bf16[128,640]{1,0:T(8,128)(2,1)S(1)} %get-tuple-element.61), channel_id=1, source_target_pairs={{0,31},{1,30},{2,29},{3,28},{4,3},{5,2},{6,1},{7,0},{8,7},{9,6},{1... | collective-permute-start | bytes 491528 | tf_op jit(solution)/shard_map/ppermute | solution.py:111

commit v3 on v2

v3 whole, which is shorter than its diff:
```python
import jax
import jax.numpy as jnp
from jax import lax
from jax.experimental import pallas as pl
from jax.experimental.pallas import tpu as pltpu
from jax.sharding import PartitionSpec as P


HEAD_DIM = 128
LOW = jnp.bfloat16
FULL = jnp.float32
VMEM_LIMIT = 8 << 20


def dot(a, b, ca, cb):
    return lax.dot_general(a, b, (((ca,), (cb,)), ((), ())), preferred_element_type=FULL)


def cols(head):
    return slice(head * HEAD_DIM, (head + 1) * HEAD_DIM)


def tree_sum(terms):
    terms = list(terms)
    while len(terms) > 1:
        terms = [
            terms[i] + terms[i + 1] if i + 1 < len(terms) else terms[i]
            for i in range(0, len(terms), 2)
        ]
    return terms[0]


def project(decoded, held, allowed, wq, wk, wv, q_out, k_out, v_out, att_out, ready=None):
    ready = ready or (lambda name: None)
    ready("q")
    q_out[...] = dot(decoded[...], wq[...], 1, 0).astype(LOW)
    ready("k")
    k_out[...] = dot(held[...], wk[...], 1, 0).astype(LOW)
    ready("v")
    v_out[...] = dot(held[...], wv[...], 1, 0).astype(LOW)
    for head in range(q_out.shape[1] // HEAD_DIM):
        scores = dot(q_out[:, cols(head)], k_out[:, cols(head)], 1, 1)
        scores = jnp.where(allowed > 0, scores, FULL(-1e30))
        expo = jnp.exp(scores - jnp.max(scores, axis=-1, keepdims=True))
        att_out[head] = expo * (1.0 / jnp.sum(expo, axis=-1, keepdims=True))


def chain(gradient, k_in, v_in, att, wq, wo, cg_out, sg_out, qg_tmp):
    cg_out[...] = dot(gradient.astype(LOW), wo[...], 1, 1).astype(LOW)
    for head in range(cg_out.shape[1] // HEAD_DIM):
        prob = dot(cg_out[:, cols(head)], v_in[:, cols(head)], 1, 1)
        weight = att[head]
        mean = jnp.sum(weight * prob, axis=-1, keepdims=True)
        sg_out[head] = (weight * (prob - mean)).astype(LOW)
        qg_tmp[:, cols(head)] = dot(sg_out[head], k_in[:, cols(head)], 1, 0).astype(LOW)
    return dot(qg_tmp[...], wq[...], 1, 1).astype(LOW)


def memory_terms(q_in, att, cg, sg, wk, wv, kg_tmp, vg_tmp):
    for head in range(cg.shape[1] // HEAD_DIM):
        kg_tmp[:, cols(head)] = dot(sg[head], q_in[:, cols(head)], 0, 0).astype(LOW)
        vg_tmp[:, cols(head)] = dot(att[head].astype(LOW), cg[:, cols(head)], 0, 0).astype(LOW)
    return dot(kg_tmp[...], wk[...], 1, 1) + dot(vg_tmp[...], wv[...], 1, 1)


def chosen(flag, one, other):
    return jnp.where(flag > 0, one, other)


def halves(refs, width):
    terms = [ref[:, :width].astype(FULL) for ref in refs]
    return tree_sum(terms[0::2]), tree_sum(terms[1::2])


def joined(same, other, odd):
    return jnp.concatenate([chosen(odd, other, same), chosen(odd, same, other)], axis=1)


def kernel(body, outs, scratch, kinds=None, out_space=pltpu.VMEM):
    def call(*args):
        spaces = list(kinds) + [pltpu.VMEM] * (len(args) - len(kinds)) if kinds else [pltpu.VMEM] * len(args)
        args = [
            arg if space == pltpu.SMEM else pltpu.with_memory_space_constraint(arg, space)
            for arg, space in zip(args, spaces)
        ]
        return pl.pallas_call(
            body,
            out_shape=[out_space(shape, kind) for shape, kind in outs],
            in_specs=[pl.BlockSpec(memory_space=space) for space in spaces],
            out_specs=[pl.BlockSpec(memory_space=pltpu.VMEM)] * len(outs),
            scratch_shapes=scratch,
            compiler_params=pltpu.CompilerParams(vmem_limit_bytes=VMEM_LIMIT),
        )(*args)

    return call


def body(
    grad_in, memory, enc_grad_in, act_stash, slot_order, lengths, w_query, w_key, w_value, w_out
):
    segments = lax.axis_size("segment")
    groups = lax.axis_size("head")
    rows, width = grad_in.shape[1:]
    enc_rows = memory.shape[1]
    inner = w_query.shape[2]
    heads = inner // HEAD_DIM
    share = enc_grad_in.shape[2]
    ticks = act_stash.shape[1]
    mine = lax.axis_index("head").astype(jnp.int32).reshape(1)

    def send(value, k):
        pairs = [
            (s * groups + h, ((s - 1) % segments) * groups + (h ^ k))
            for s in range(segments)
            for h in range(groups)
        ]
        return lax.ppermute(value, ("segment", "head"), pairs)

    def sent_pair(value):
        pairs = [(h, h ^ 1) for h in range(groups)]
        return lax.ppermute(value, "head", pairs)

    half = width // 2
    proj_outs = [
        ((rows, inner), LOW),
        ((enc_rows, inner), LOW),
        ((enc_rows, inner), LOW),
        ((heads, rows, enc_rows), FULL),
    ]
    chain_outs = [((rows, inner), LOW), ((heads, rows, enc_rows), LOW)]
    pair_outs = [((rows, half), LOW), ((rows, half), FULL)]
    inner_tmp = pltpu.VMEM((rows, inner), LOW)

    def write_pair(part, base, odd, give, keep):
        left, right = part[:, :half], part[:, half:]
        give[...] = chosen(odd, left, right).astype(LOW)
        keep[...] = chosen(odd, right, left) + base

    def open_body(mine_ref, order_ref, length_ref, *refs):
        (stash, *hbm), refs = refs[:7], refs[7:]
        outs, refs = refs[:15], refs[15:]
        q, att, cg, sg, give, keep, own, flags, place, dec, allowed, wq, wk, wv, wo = outs
        g, mem, k, v, tmp, sems = refs
        local = [wq, mem, wk, wv, g, wo]
        turns = [
            pltpu.make_async_copy(stash.at[0, order_ref[0, t]], dec.at[t], sems.at[len(local) + t])
            for t in range(ticks)
        ]
        copies = [
            pltpu.make_async_copy(src.at[0], dst, sems.at[i])
            for i, (src, dst) in enumerate(zip(hbm, local))
        ]
        copies = turns[:1] + copies + turns[1:]
        for copy in copies:
            copy.start()
        waits = {"q": copies[:2], "k": copies[2:4], "v": copies[4:5]}

        def ready(name):
            for copy in waits[name]:
                copy.wait()

        positions = lax.broadcasted_iota(jnp.int32, (1, enc_rows), 1)
        for t in range(ticks):
            allowed[t : t + 1, :] = (positions < length_ref[0, t]).astype(FULL)
        own[...] = (lax.broadcasted_iota(jnp.int32, own.shape, 1) == mine_ref[0]).astype(FULL)
        flags[...] = jnp.broadcast_to((mine_ref[0] % 2).astype(FULL), flags.shape)
        columns = lax.broadcasted_iota(jnp.int32, place.shape, 1)
        start = (mine_ref[0] // 2) * share
        place[...] = ((columns >= start) & (columns < start + share)).astype(FULL)
        project(dec.at[0], mem, allowed[0:1, :], wq, wk, wv, q, k, v, att, ready)
        for copy in copies[5:]:
            copy.wait()
        odd = flags[0:1, 0:1]
        base = chosen(odd, g[:, half:], g[:, :half]) * place[0:1, :]
        write_pair(chain(g[...], k, v, att, wq, wo, cg, sg, tmp), base, odd, give, keep)

    def add_body(keep, got, place, small, first):
        total = keep[...] + got[...].astype(FULL)
        small[...] = total.astype(LOW)
        first[:, :half] = total.astype(LOW)
        rest = (total - total.astype(LOW).astype(FULL)) * place[0:1, :]
        first[:, half:] = sum(
            rest[:, j * share : (j + 1) * share] for j in range(groups // 2)
        ).astype(LOW)

    def memory_open_body(own, enc, q, att, cg, sg, wk, wv, carry_out, kg_tmp, vg_tmp):
        total = memory_terms(q, att, cg, sg, wk, wv, kg_tmp, vg_tmp)
        for g in range(groups):
            at = slice(g * share, (g + 1) * share)
            carry_out[:, at] = (total[:, at] + enc[0] * own[0:1, g : g + 1]).astype(LOW)

    def memory_body(carry, q, att, cg, sg, wk, wv, carry_out, kg_tmp, vg_tmp):
        total = memory_terms(q, att, cg, sg, wk, wv, kg_tmp, vg_tmp)
        carry_out[...] = (carry[...].astype(FULL) + total).astype(LOW)

    def memory_last_body(own, carry, q, att, cg, sg, wk, wv, *refs):
        outs, (kg_tmp, vg_tmp) = refs[:groups], refs[groups:]
        total = carry[...].astype(FULL) + memory_terms(q, att, cg, sg, wk, wv, kg_tmp, vg_tmp)
        pieces = [total[:, g * share : (g + 1) * share].astype(LOW) for g in range(groups)]
        for j, out in enumerate(outs):
            piece = pieces[0 ^ j]
            for g in range(1, groups):
                piece = jnp.where(own[0:1, g : g + 1] > 0, pieces[g ^ j], piece)
            out[...] = piece

    def project_body(tick):
        def run(held, dec, allowed, wq, wk, wv, q, k, v, att):
            at = slice(tick, tick + 1)
            project(dec.at[tick], held, allowed[at, :], wq, wk, wv, q, k, v, att)

        return run

    def gradient_of(refs, odd):
        same, other = halves(refs, half)
        return same, joined(same, other, odd)

    def step_body(*refs):
        msgs, refs = refs[:groups], refs[groups:]
        flags, place, k, v, att, wq, wo, cg, sg, give, keep, tmp = refs
        odd = flags[0:1, 0:1]
        same, gradient = gradient_of(msgs, odd)
        rest = jnp.concatenate([msgs[0][:, half:].astype(FULL)] * (groups // 2), axis=1)
        base = (same + rest) * place[0:1, :]
        write_pair(chain(gradient, k, v, att, wq, wo, cg, sg, tmp), base, odd, give, keep)

    def add_last_body(keep, got, *refs):
        pieces, msgs = refs[:groups], refs[groups:]
        total = (keep[...] + got[...].astype(FULL)).astype(LOW)
        for piece, msg in zip(pieces, msgs):
            msg[:, :half] = total
            msg[:, half:] = piece[...]

    def close_body(*refs):
        msgs, (flags, grad_out, enc_out) = refs[:groups], refs[groups:]
        grad_out[...] = gradient_of(msgs, flags[0:1, 0:1])[1]
        enc_out[...] = tree_sum([msg[:, half:].astype(FULL) for msg in msgs])

    smem = pltpu.SMEM
    open_outs = proj_outs[:1] + proj_outs[3:] + chain_outs + pair_outs
    open_outs += [((8, groups), FULL), ((8, 128), FULL), ((8, half), FULL)]
    open_outs += [(act_stash.shape[1:], LOW), ((8, enc_rows), FULL)]
    open_outs += [(w.shape[1:], LOW) for w in (w_query, w_key, w_value, w_out)]
    enc_low = ((enc_rows, width), LOW)
    msg_outs = [((rows, half), LOW), ((rows, half + share), LOW)]
    (q, att, cg, sg, give, keep, own, flags, place, dec, allowed, wq, wk, wv, wo) = kernel(
        open_body,
        open_outs,
        [
            pltpu.VMEM((rows, width), FULL),
            pltpu.VMEM((enc_rows, width), LOW),
            pltpu.VMEM((enc_rows, inner), LOW),
            pltpu.VMEM((enc_rows, inner), LOW),
            inner_tmp,
            pltpu.SemaphoreType.DMA((6 + ticks,)),
        ],
        [smem] * 3 + [pltpu.HBM] * 7,
    )(mine, slot_order, lengths, act_stash, w_query, memory, w_key, w_value, grad_in, w_out)
    held = memory[0]
    carry = None
    for tick in range(1, ticks):
        got = sent_pair(give)
        held = send(held, 0)
        (carry,) = kernel(
            memory_body if tick > 1 else memory_open_body, [enc_low], [inner_tmp] * 2
        )(*([carry] if tick > 1 else [own, enc_grad_in]), q, att, cg, sg, wk, wv)
        small, first = kernel(add_body, msg_outs, [])(keep, got, place)
        msgs = [send(small if j else first, j) for j in range(groups)]
        carry = send(carry, 0)
        q, k, v, att = kernel(project_body(tick), proj_outs, [])(held, dec, allowed, wq, wk, wv)
        cg, sg, give, keep = kernel(step_body, chain_outs + pair_outs, [inner_tmp])(
            *msgs, flags, place, k, v, att, wq, wo
        )
    got = sent_pair(give)
    pieces = kernel(
        memory_last_body, [((enc_rows, share), LOW)] * groups, [inner_tmp] * 2
    )(own, carry, q, att, cg, sg, wk, wv)
    outs = kernel(add_last_body, [((rows, half + share), LOW)] * groups, [])(keep, got, *pieces)
    msgs = [send(outs[j], j) for j in range(groups)]
    gradient, carried = kernel(
        close_body, [((rows, width), FULL), ((enc_rows, share), FULL)], [],
        out_space=jax.ShapeDtypeStruct,
    )(*msgs, flags)
    return (gradient[None], carried[None])


def solution(mesh):
    in_specs = (
        P("segment", None, None),
        P("segment", None, None),
        P("segment", None, "head"),
        P("segment", None, None, None),
        P("segment", None),
        P("segment", None),
        P("segment", None, "head"),
        P("segment", None, "head"),
        P("segment", None, "head"),
        P("segment", "head", None),
    )
    out_specs = (P("segment", None, None), P("segment", None, "head"))

    return jax.shard_map(body, mesh=mesh, in_specs=in_specs, out_specs=out_specs, check_vma=False)
```

time: 77.7 us -> 63.1 us (0.81)
  the two profiles are of different devices: /device:TPU:0 before, /device:TPU:1 now
where the time goes in v3:
time: 63.1 us; the launch traced here: 62.9 us
  starting transfers between devices  23.5 us (37%)
  waiting for transfers between devices  21 us (33%)
  Pallas kernels  17 us (27%)
  between operations  0.78 us (1%)
  local copies, waits for them, and re-layouts  0.66 us (1%)
    ppermute x16, starting transfers between devices, send(): return lax.ppermute(value, ('segment', 'head'), pairs)  21.2 us
    pallas_call x12, Pallas kernels, call(): pl.pallas_call(body, out_shape=[out_space(shape, kind) for shape, kind in...  17 us
    ppermute x16, waiting for transfers between devices, send(): return lax.ppermute(value, ('segment', 'head'), pairs)  14.6 us
    ppermute x3, waiting for transfers between devices, sent_pair(): return lax.ppermute(value, 'head', pairs)  6.41 us
    ppermute x3, starting transfers between devices, sent_pair(): return lax.ppermute(value, 'head', pairs)  2.32 us
  transfers between devices with their start and end apart: 19, of which 9 were waited for; matrix products, arithmetic and copies ran while one was open for 0% of the time, Pallas kernels for 16%

profile of v3, /device:TPU:1, one launch (start us, length us, event | category | flops | bytes accessed | tf_op | source)
XLA Modules:
  0.0 62.9 jit_solution(10707697312017366397)
XLA Ops:
  1.3 5.8 %shard_map.113 = (bf16[128,1024]{1,0:T(8,128)(2,1)S(1)}, f32[8,128,128]{2,1,0:T(8,128)S(1)}, bf16[128,1024]{1,0:T(8,128)(2,1)S(1)}, bf16[8,128,128]{2,1,0:T(8,12...) custom-call(s32[1]{0:T(128)} %bitcast.mine_ref, ...), custom_call_target="tpu_custom_call" | custom-call | tf_op jit(solution)/shard_map/pallas_call | solution.py:86
  7.1 2.2 %collective-permute-start = (bf16[128,256]{1,0:T(8,128)(2,1)S(1)}, bf16[128,256]{1,0:T(8,128)(2,1)S(1)}, u32[]{:S(2)}, u32[]{:S(2)}) collective-permute-start(bf16[128,256]{1,0:T(8,128)(2,1)S(1)} %get-tuple-element.48), channel_id=1, source_target_pairs={{0,1},{1,0},{2,3},{3,2},{4,5},{5,4},{6,7},{7,6},{8,9},{9,8},{10,11... | collective-permute-start | bytes 196616 | tf_op jit(solution)/shard_map/ppermute | solution.py:121
  9.3 1.0 %collective-permute-start.5 = (bf16[128,512]{1,0:T(8,128)(2,1)S(1)}, bf16[128,512]{1,0:T(8,128)(2,1)S(1)}, u32[]{:S(2)}, u32[]{:S(2)}) collective-permute-start(bf16[128,512]{1,0:T(8,128)(2,1)S(1)} %bitcast.4), channel_id=1, source_target_pairs={{0,28},{1,29},{2,30},{3,31},{4,0},{5,1},{6,2},{7,3},{8,4},{9,5},{1... | collective-permute-start | bytes 393224 | tf_op jit(solution)/shard_map/ppermute | solution.py:117
  11.0 1.6 %collective-permute-start.1 = (bf16[128,384]{1,0:T(8,128)(2,1)S(1)}, bf16[128,384]{1,0:T(8,128)(2,1)S(1)}, u32[]{:S(2)}, u32[]{:S(2)}) collective-permute-start(bf16[128,384]{1,0:T(8,128)(2,1)S(1)} %get-tuple-element.50), channel_id=1, source_target_pairs={{0,28},{1,29},{2,30},{3,31},{4,0},{5,1},{6,2},{7,3},{8,4},{9,5},{1... | collective-permute-start | bytes 294920 | tf_op jit(solution)/shard_map/ppermute | solution.py:117
  12.6 4.4 %collective-permute-start.4 = (bf16[128,256]{1,0:T(8,128)(2,1)S(1)}, bf16[128,256]{1,0:T(8,128)(2,1)S(1)}, u32[]{:S(2)}, u32[]{:S(2)}) collective-permute-start(bf16[128,256]{1,0:T(8,128)(2,1)S(1)} %get-tuple-element.51), channel_id=1, source_target_pairs={{0,31},{1,30},{2,29},{3,28},{4,3},{5,2},{6,1},{7,0},{8,7},{9,6},{1... | collective-permute-start | bytes 196616 | tf_op jit(solution)/shard_map/ppermute | solution.py:117
  17.7 1.1 %collective-permute-start.2 = (bf16[128,256]{1,0:T(8,128)(2,1)S(1)}, bf16[128,256]{1,0:T(8,128)(2,1)S(1)}, u32[]{:S(2)}, u32[]{:S(2)}) collective-permute-start(bf16[128,256]{1,0:T(8,128)(2,1)S(1)} %get-tuple-element.51), channel_id=1, source_target_pairs={{0,29},{1,28},{2,31},{3,30},{4,1},{5,0},{6,3},{7,2},{8,5},{9,4},{1... | collective-permute-start | bytes 196616 | tf_op jit(solution)/shard_map/ppermute | solution.py:117
  18.8 1.1 %shard_map.120 = bf16[128,512]{1,0:T(8,128)(2,1)S(1)} custom-call(f32[8,4]{1,0:T(8,128)S(1)} %get-tuple-element.71.own, f32[1,128,128]{2,1,0:T(8,128)S(1)} %copy-done, bf16[128,1024]{1,0:T(8,128)(2,1)S(1)} %get-tuple-element.72.q, f32[8,128,128]{2,1,0:T(8,128)S(1)} %get-tuple-element.73.att, bf16[128,1024]{1,0:T(8,128)(2,1)S(1)} %get-tuple-element.74.cg, ...), custom_call_target="tpu_custom_call" | custom-call | tf_op jit(solution)/shard_map/pallas_call | solution.py:86
  20.3 0.8 %collective-permute-start.11 = (bf16[128,512]{1,0:T(8,128)(2,1)S(1)}, bf16[128,512]{1,0:T(8,128)(2,1)S(1)}, u32[]{:S(2)}, u32[]{:S(2)}) collective-permute-start(bf16[128,512]{1,0:T(8,128)(2,1)S(1)} %collective-permute-done.5.held), channel_id=1, source_target_pairs={{0,28},{1,29},{2,30},{3,31},{4,0},{5,1},{6,2},{7,3},{8,4},{9,5},{1... | collective-permute-start | bytes 393224 | tf_op jit(solution)/shard_map/ppermute | solution.py:117
  21.1 1.0 %shard_map.115 = (bf16[128,1024]{1,0:T(8,128)(2,1)S(1)}, bf16[128,1024]{1,0:T(8,128)(2,1)S(1)}, bf16[128,1024]{1,0:T(8,128)(2,1)S(1)}, f32[8,128,128]{2,1,0:T(8,128)S(1)}) custom-call(bf16[128,512]{1,0:T(8,128)(2,1)S(1)} %collective-permute-done.5.held, bf16[3,128,512]{2,1,0:T(8,128)(2,1)S(1)} %get-tuple-element.53.dec, ...), custom_call_target="tpu_custom_call" | custom-call | tf_op jit(solution)/shard_map/pallas_call | solution.py:86
  22.1 1.0 %collective-permute-done.3.refs_2_ = bf16[128,256]{1,0:T(8,128)(2,1)S(1)} collective-permute-done((bf16[128,256]{1,0:T(8,128)(2,1)S(1)}, bf16[128,256]{1,0:T(8,128)(2,1)S(1)}, u32[]{:S(2)}, u32[]{:S(2)}) %collective-permute-start.3) | collective-permute-done | bytes 65568 | tf_op jit(solution)/shard_map/ppermute | solution.py:117
  23.9 2.5 %shard_map.116 = (bf16[128,1024]{1,0:T(8,128)(2,1)S(1)}, bf16[8,128,128]{2,1,0:T(8,128)(2,1)S(1)}, bf16[128,256]{1,0:T(8,128)(2,1)S(1)}, f32[128,256]{1,0:T(8,128)S(1)}) custom-call(bf16[128,384]{1,0:T(8,128)(2,1)S(1)} %collective-permute-done.1.refs_0_, bf16[128,256]{1,0:T(8,128)(2,1)S(1)} %collective-permute-done.2.refs_1_, ...), custom_call_target="tpu_custom_call" | custom-call | tf_op jit(solution)/shard_map/pallas_call | solution.py:86
  26.6 3.1 %collective-permute-done.6.got = bf16[128,256]{1,0:T(8,128)(2,1)S(1)} collective-permute-done((bf16[128,256]{1,0:T(8,128)(2,1)S(1)}, bf16[128,256]{1,0:T(8,128)(2,1)S(1)}, u32[]{:S(2)}, u32[]{:S(2)}) %collective-permute-start.6) | collective-permute-done | bytes 65568 | tf_op jit(solution)/shard_map/ppermute | solution.py:121
  29.7 1.7 %collective-permute-start.7 = (bf16[128,384]{1,0:T(8,128)(2,1)S(1)}, bf16[128,384]{1,0:T(8,128)(2,1)S(1)}, u32[]{:S(2)}, u32[]{:S(2)}) collective-permute-start(bf16[128,384]{1,0:T(8,128)(2,1)S(1)} %get-tuple-element.64), channel_id=1, source_target_pairs={{0,28},{1,29},{2,30},{3,31},{4,0},{5,1},{6,2},{7,3},{8,4},{9,5},{1... | collective-permute-start | bytes 294920 | tf_op jit(solution)/shard_map/ppermute | solution.py:117
  31.4 1.1 %shard_map.121 = bf16[128,512]{1,0:T(8,128)(2,1)S(1)} custom-call(bf16[128,512]{1,0:T(8,128)(2,1)S(1)} %collective-permute-done.13.carry, bf16[128,1024]{1,0:T(8,128)(2,1)S(1)} %get-tuple-element.76.q, f32[8,128,128]{2,1,0:T(8,128)S(1)} %get-tuple-element.60.refs_8_.att, bf16[128,1024]{1,0:T(8,128)(2,1)S(1)} %get-tuple-element.77.cg, ...), custom_call_target="tpu_custom_call" | custom-call | tf_op jit(solution)/shard_map/pallas_call | solution.py:86
  32.5 3.5 %collective-permute-start.10 = (bf16[128,256]{1,0:T(8,128)(2,1)S(1)}, bf16[128,256]{1,0:T(8,128)(2,1)S(1)}, u32[]{:S(2)}, u32[]{:S(2)}) collective-permute-start(bf16[128,256]{1,0:T(8,128)(2,1)S(1)} %get-tuple-element.65), channel_id=1, source_target_pairs={{0,31},{1,30},{2,29},{3,28},{4,3},{5,2},{6,1},{7,0},{8,7},{9,6},{1... | collective-permute-start | bytes 196616 | tf_op jit(solution)/shard_map/ppermute | solution.py:117
  36.3 1.3 %collective-permute-start.14 = (bf16[128,512]{1,0:T(8,128)(2,1)S(1)}, bf16[128,512]{1,0:T(8,128)(2,1)S(1)}, u32[]{:S(2)}, u32[]{:S(2)}) collective-permute-start(bf16[128,512]{1,0:T(8,128)(2,1)S(1)} %shard_map.121), channel_id=1, source_target_pairs={{0,28},{1,29},{2,30},{3,31},{4,0},{5,1},{6,2},{7,3},{8,4},{9,5},{1... | collective-permute-start | bytes 393224 | tf_op jit(solution)/shard_map/ppermute | solution.py:117
  37.6 1.0 %shard_map.118 = (bf16[128,1024]{1,0:T(8,128)(2,1)S(1)}, bf16[128,1024]{1,0:T(8,128)(2,1)S(1)}, bf16[128,1024]{1,0:T(8,128)(2,1)S(1)}, f32[8,128,128]{2,1,0:T(8,128)S(1)}) custom-call(bf16[128,512]{1,0:T(8,128)(2,1)S(1)} %collective-permute-done.11.held, bf16[3,128,512]{2,1,0:T(8,128)(2,1)S(1)} %get-tuple-element.53.dec, ...), custom_call_target="tpu_custom_call" | custom-call | tf_op jit(solution)/shard_map/pallas_call | solution.py:86
  38.9 4.4 %collective-permute-done.9.refs_2_ = bf16[128,256]{1,0:T(8,128)(2,1)S(1)} collective-permute-done((bf16[128,256]{1,0:T(8,128)(2,1)S(1)}, bf16[128,256]{1,0:T(8,128)(2,1)S(1)}, u32[]{:S(2)}, u32[]{:S(2)}) %collective-permute-start.9) | collective-permute-done | bytes 65568 | tf_op jit(solution)/shard_map/ppermute | solution.py:117
  43.4 2.5 %shard_map.119 = (bf16[128,1024]{1,0:T(8,128)(2,1)S(1)}, bf16[8,128,128]{2,1,0:T(8,128)(2,1)S(1)}, bf16[128,256]{1,0:T(8,128)(2,1)S(1)}, f32[128,256]{1,0:T(8,128)S(1)}) custom-call(bf16[128,384]{1,0:T(8,128)(2,1)S(1)} %collective-permute-done.7.refs_0_, bf16[128,256]{1,0:T(8,128)(2,1)S(1)} %collective-permute-done.8.refs_1_, ...), custom_call_target="tpu_custom_call" | custom-call | tf_op jit(solution)/shard_map/pallas_call | solution.py:86
  46.0 1.1 %shard_map.122 = (bf16[128,128]{1,0:T(8,128)(2,1)S(1)}, bf16[128,128]{1,0:T(8,128)(2,1)S(1)}, bf16[128,128]{1,0:T(8,128)(2,1)S(1)}, bf16[128,128]{1,0:T(8,128)(2,1)S(1)}) custom-call(f32[8,4]{1,0:T(8,128)S(1)} %get-tuple-element.71.own, bf16[128,512]{1,0:T(8,128)(2,1)S(1)} %collective-permute-done.14.carry, bf16[128,1024]{1,0:T(8,128)(2,1)S(1)} %get-tuple-element.79.q, ...), custom_call_target="tpu_custom_call" | custom-call | tf_op jit(solution)/shard_map/pallas_call | solution.py:86
  47.1 2.6 %collective-permute-done.12.got = bf16[128,256]{1,0:T(8,128)(2,1)S(1)} collective-permute-done((bf16[128,256]{1,0:T(8,128)(2,1)S(1)}, bf16[128,256]{1,0:T(8,128)(2,1)S(1)}, u32[]{:S(2)}, u32[]{:S(2)}) %collective-permute-start.12) | collective-permute-done | bytes 65568 | tf_op jit(solution)/shard_map/ppermute | solution.py:121
  51.0 2.4 %collective-permute-start.17 = (bf16[128,384]{1,0:T(8,128)(2,1)S(1)}, bf16[128,384]{1,0:T(8,128)(2,1)S(1)}, u32[]{:S(2)}, u32[]{:S(2)}) collective-permute-start(bf16[128,384]{1,0:T(8,128)(2,1)S(1)} %get-tuple-element.88), channel_id=1, source_target_pairs={{0,30},{1,31},{2,28},{3,29},{4,2},{5,3},{6,0},{7,1},{8,6},{9,7},{1... | collective-permute-start | bytes 294920 | tf_op jit(solution)/shard_map/ppermute | solution.py:117
  54.1 3.2 %collective-permute-done.16.refs_1_ = bf16[128,384]{1,0:T(8,128)(2,1)S(1)} collective-permute-done((bf16[128,384]{1,0:T(8,128)(2,1)S(1)}, bf16[128,384]{1,0:T(8,128)(2,1)S(1)}, u32[]{:S(2)}, u32[]{:S(2)}) %collective-permute-start.16) | collective-permute-done | bytes 98336 | tf_op jit(solution)/shard_map/ppermute | solution.py:117
  57.3 4.8 %collective-permute-done.17.refs_2_ = bf16[128,384]{1,0:T(8,128)(2,1)S(1)} collective-permute-done((bf16[128,384]{1,0:T(8,128)(2,1)S(1)}, bf16[128,384]{1,0:T(8,128)(2,1)S(1)}, u32[]{:S(2)}, u32[]{:S(2)}) %collective-permute-start.17) | collective-permute-done | bytes 98336 | tf_op jit(solution)/shard_map/ppermute | solution.py:117
  (34 shorter events, 7.0 us)
Async XLA Ops:
  0.6 0.7 %copy-start.1 = (s32[1,3]{1,0:T(1,128)S(1)}, s32[1,3]{1,0:T(1,128)}, u32[]{:S(2)}) copy-start(s32[1,3]{1,0:T(1,128)} %order_ref.1) | copy-start | bytes 40
  0.6 0.7 %copy-start.2 = (s32[1,3]{1,0:T(1,128)S(1)}, s32[1,3]{1,0:T(1,128)}, u32[]{:S(2)}) copy-start(s32[1,3]{1,0:T(1,128)} %length_ref.1) | copy-start | bytes 40
  1.3 8.0 %copy-start.3 = (bf16[1,128,512]{2,1,0:T(8,128)(2,1)S(1)}, bf16[1,128,512]{2,1,0:T(8,128)(2,1)}, u32[]{:S(2)}) copy-start(bf16[1,128,512]{2,1,0:T(8,128)(2,1)} %refs_2_.1) | copy-start | bytes 393220
  7.1 3.8 %collective-permute-start = (bf16[128,256]{1,0:T(8,128)(2,1)S(1)}, bf16[128,256]{1,0:T(8,128)(2,1)S(1)}, u32[]{:S(2)}, u32[]{:S(2)}) collective-permute-start(bf16[128,256]{1,0:T(8,128)(2,1)S(1)} %get-tuple-element.48), channel_id=1, source_target_pairs={{0,1},{1,0},{2,3},{3,2},{4,5},{5,4},{6,7},{7,6},{8,9},{9,8},{10,11... | collective-permute-start | bytes 196616 | tf_op jit(solution)/shard_map/ppermute | solution.py:121
  9.3 10.6 %collective-permute-start.5 = (bf16[128,512]{1,0:T(8,128)(2,1)S(1)}, bf16[128,512]{1,0:T(8,128)(2,1)S(1)}, u32[]{:S(2)}, u32[]{:S(2)}) collective-permute-start(bf16[128,512]{1,0:T(8,128)(2,1)S(1)} %bitcast.4), channel_id=1, source_target_pairs={{0,28},{1,29},{2,30},{3,31},{4,0},{5,1},{6,2},{7,3},{8,4},{9,5},{1... | collective-permute-start | bytes 393224 | tf_op jit(solution)/shard_map/ppermute | solution.py:117
  11.0 7.9 %copy-start = (f32[1,128,128]{2,1,0:T(8,128)S(1)}, f32[1,128,128]{2,1,0:T(8,128)}, u32[]{:S(2)}) copy-start(f32[1,128,128]{2,1,0:T(8,128)} %enc.1) | copy-start | bytes 196612
  11.0 12.9 %collective-permute-start.1 = (bf16[128,384]{1,0:T(8,128)(2,1)S(1)}, bf16[128,384]{1,0:T(8,128)(2,1)S(1)}, u32[]{:S(2)}, u32[]{:S(2)}) collective-permute-start(bf16[128,384]{1,0:T(8,128)(2,1)S(1)} %get-tuple-element.50), channel_id=1, source_target_pairs={{0,28},{1,29},{2,30},{3,31},{4,0},{5,1},{6,2},{7,3},{8,4},{9,5},{1... | collective-permute-start | bytes 294920 | tf_op jit(solution)/shard_map/ppermute | solution.py:117
  12.6 7.7 %collective-permute-start.4 = (bf16[128,256]{1,0:T(8,128)(2,1)S(1)}, bf16[128,256]{1,0:T(8,128)(2,1)S(1)}, u32[]{:S(2)}, u32[]{:S(2)}) collective-permute-start(bf16[128,256]{1,0:T(8,128)(2,1)S(1)} %get-tuple-element.51), channel_id=1, source_target_pairs={{0,31},{1,30},{2,29},{3,28},{4,3},{5,2},{6,1},{7,0},{8,7},{9,6},{1... | collective-permute-start | bytes 196616 | tf_op jit(solution)/shard_map/ppermute | solution.py:117
  17.0 6.1 %collective-permute-start.3 = (bf16[128,256]{1,0:T(8,128)(2,1)S(1)}, bf16[128,256]{1,0:T(8,128)(2,1)S(1)}, u32[]{:S(2)}, u32[]{:S(2)}) collective-permute-start(bf16[128,256]{1,0:T(8,128)(2,1)S(1)} %get-tuple-element.51), channel_id=1, source_target_pairs={{0,30},{1,31},{2,28},{3,29},{4,2},{5,3},{6,0},{7,1},{8,6},{9,7},{1... | collective-permute-start | bytes 196616 | tf_op jit(solution)/shard_map/ppermute | solution.py:117
  17.7 6.2 %collective-permute-start.2 = (bf16[128,256]{1,0:T(8,128)(2,1)S(1)}, bf16[128,256]{1,0:T(8,128)(2,1)S(1)}, u32[]{:S(2)}, u32[]{:S(2)}) collective-permute-start(bf16[128,256]{1,0:T(8,128)(2,1)S(1)} %get-tuple-element.51), channel_id=1, source_target_pairs={{0,29},{1,28},{2,31},{3,30},{4,1},{5,0},{6,3},{7,2},{8,5},{9,4},{1... | collective-permute-start | bytes 196616 | tf_op jit(solution)/shard_map/ppermute | solution.py:117
  19.9 11.5 %collective-permute-start.13 = (bf16[128,512]{1,0:T(8,128)(2,1)S(1)}, bf16[128,512]{1,0:T(8,128)(2,1)S(1)}, u32[]{:S(2)}, u32[]{:S(2)}) collective-permute-start(bf16[128,512]{1,0:T(8,128)(2,1)S(1)} %shard_map.120), channel_id=1, source_target_pairs={{0,28},{1,29},{2,30},{3,31},{4,0},{5,1},{6,2},{7,3},{8,4},{9,5},{1... | collective-permute-start | bytes 393224 | tf_op jit(solution)/shard_map/ppermute | solution.py:117
  20.3 16.0 %collective-permute-start.11 = (bf16[128,512]{1,0:T(8,128)(2,1)S(1)}, bf16[128,512]{1,0:T(8,128)(2,1)S(1)}, u32[]{:S(2)}, u32[]{:S(2)}) collective-permute-start(bf16[128,512]{1,0:T(8,128)(2,1)S(1)} %collective-permute-done.5.held), channel_id=1, source_target_pairs={{0,28},{1,29},{2,30},{3,31},{4,0},{5,1},{6,2},{7,3},{8,4},{9,5},{1... | collective-permute-start | bytes 393224 | tf_op jit(solution)/shard_map/ppermute | solution.py:117
  26.5 3.2 %collective-permute-start.6 = (bf16[128,256]{1,0:T(8,128)(2,1)S(1)}, bf16[128,256]{1,0:T(8,128)(2,1)S(1)}, u32[]{:S(2)}, u32[]{:S(2)}) collective-permute-start(bf16[128,256]{1,0:T(8,128)(2,1)S(1)} %get-tuple-element.63), channel_id=1, source_target_pairs={{0,1},{1,0},{2,3},{3,2},{4,5},{5,4},{6,7},{7,6},{8,9},{9,8},{10,11... | collective-permute-start | bytes 196616 | tf_op jit(solution)/shard_map/ppermute | solution.py:121
  29.7 13.7 %collective-permute-start.7 = (bf16[128,384]{1,0:T(8,128)(2,1)S(1)}, bf16[128,384]{1,0:T(8,128)(2,1)S(1)}, u32[]{:S(2)}, u32[]{:S(2)}) collective-permute-start(bf16[128,384]{1,0:T(8,128)(2,1)S(1)} %get-tuple-element.64), channel_id=1, source_target_pairs={{0,28},{1,29},{2,30},{3,31},{4,0},{5,1},{6,2},{7,3},{8,4},{9,5},{1... | collective-permute-start | bytes 294920 | tf_op jit(solution)/shard_map/ppermute | solution.py:117
  32.5 6.4 %collective-permute-start.10 = (bf16[128,256]{1,0:T(8,128)(2,1)S(1)}, bf16[128,256]{1,0:T(8,128)(2,1)S(1)}, u32[]{:S(2)}, u32[]{:S(2)}) collective-permute-start(bf16[128,256]{1,0:T(8,128)(2,1)S(1)} %get-tuple-element.65), channel_id=1, source_target_pairs={{0,31},{1,30},{2,29},{3,28},{4,3},{5,2},{6,1},{7,0},{8,7},{9,6},{1... | collective-permute-start | bytes 196616 | tf_op jit(solution)/shard_map/ppermute | solution.py:117
  36.0 7.4 %collective-permute-start.9 = (bf16[128,256]{1,0:T(8,128)(2,1)S(1)}, bf16[128,256]{1,0:T(8,128)(2,1)S(1)}, u32[]{:S(2)}, u32[]{:S(2)}) collective-permute-start(bf16[128,256]{1,0:T(8,128)(2,1)S(1)} %get-tuple-element.65), channel_id=1, source_target_pairs={{0,30},{1,31},{2,28},{3,29},{4,2},{5,3},{6,0},{7,1},{8,6},{9,7},{1... | collective-permute-start | bytes 196616 | tf_op jit(solution)/shard_map/ppermute | solution.py:117
  36.2 7.2 %collective-permute-start.8 = (bf16[128,256]{1,0:T(8,128)(2,1)S(1)}, bf16[128,256]{1,0:T(8,128)(2,1)S(1)}, u32[]{:S(2)}, u32[]{:S(2)}) collective-permute-start(bf16[128,256]{1,0:T(8,128)(2,1)S(1)} %get-tuple-element.65), channel_id=1, source_target_pairs={{0,29},{1,28},{2,31},{3,30},{4,1},{5,0},{6,3},{7,2},{8,5},{9,4},{1... | collective-permute-start | bytes 196616 | tf_op jit(solution)/shard_map/ppermute | solution.py:117
  36.3 9.7 %collective-permute-start.14 = (bf16[128,512]{1,0:T(8,128)(2,1)S(1)}, bf16[128,512]{1,0:T(8,128)(2,1)S(1)}, u32[]{:S(2)}, u32[]{:S(2)}) collective-permute-start(bf16[128,512]{1,0:T(8,128)(2,1)S(1)} %shard_map.121), channel_id=1, source_target_pairs={{0,28},{1,29},{2,30},{3,31},{4,0},{5,1},{6,2},{7,3},{8,4},{9,5},{1... | collective-permute-start | bytes 393224 | tf_op jit(solution)/shard_map/ppermute | solution.py:117
  45.9 3.8 %collective-permute-start.12 = (bf16[128,256]{1,0:T(8,128)(2,1)S(1)}, bf16[128,256]{1,0:T(8,128)(2,1)S(1)}, u32[]{:S(2)}, u32[]{:S(2)}) collective-permute-start(bf16[128,256]{1,0:T(8,128)(2,1)S(1)} %get-tuple-element.70), channel_id=1, source_target_pairs={{0,1},{1,0},{2,3},{3,2},{4,5},{5,4},{6,7},{7,6},{8,9},{9,8},{10,11... | collective-permute-start | bytes 196616 | tf_op jit(solution)/shard_map/ppermute | solution.py:121
  49.7 4.4 %collective-permute-start.15 = (bf16[128,384]{1,0:T(8,128)(2,1)S(1)}, bf16[128,384]{1,0:T(8,128)(2,1)S(1)}, u32[]{:S(2)}, u32[]{:S(2)}) collective-permute-start(bf16[128,384]{1,0:T(8,128)(2,1)S(1)} %get-tuple-element.86), channel_id=1, source_target_pairs={{0,28},{1,29},{2,30},{3,31},{4,0},{5,1},{6,2},{7,3},{8,4},{9,5},{1... | collective-permute-start | bytes 294920 | tf_op jit(solution)/shard_map/ppermute | solution.py:117
  50.6 6.7 %collective-permute-start.16 = (bf16[128,384]{1,0:T(8,128)(2,1)S(1)}, bf16[128,384]{1,0:T(8,128)(2,1)S(1)}, u32[]{:S(2)}, u32[]{:S(2)}) collective-permute-start(bf16[128,384]{1,0:T(8,128)(2,1)S(1)} %get-tuple-element.87), channel_id=1, source_target_pairs={{0,29},{1,28},{2,31},{3,30},{4,1},{5,0},{6,3},{7,2},{8,5},{9,4},{1... | collective-permute-start | bytes 294920 | tf_op jit(solution)/shard_map/ppermute | solution.py:117
  51.0 11.1 %collective-permute-start.17 = (bf16[128,384]{1,0:T(8,128)(2,1)S(1)}, bf16[128,384]{1,0:T(8,128)(2,1)S(1)}, u32[]{:S(2)}, u32[]{:S(2)}) collective-permute-start(bf16[128,384]{1,0:T(8,128)(2,1)S(1)} %get-tuple-element.88), channel_id=1, source_target_pairs={{0,30},{1,31},{2,28},{3,29},{4,2},{5,3},{6,0},{7,1},{8,6},{9,7},{1... | collective-permute-start | bytes 294920 | tf_op jit(solution)/shard_map/ppermute | solution.py:117
  53.4 8.7 %collective-permute-start.18 = (bf16[128,384]{1,0:T(8,128)(2,1)S(1)}, bf16[128,384]{1,0:T(8,128)(2,1)S(1)}, u32[]{:S(2)}, u32[]{:S(2)}) collective-permute-start(bf16[128,384]{1,0:T(8,128)(2,1)S(1)} %get-tuple-element.89), channel_id=1, source_target_pairs={{0,31},{1,30},{2,29},{3,28},{4,3},{5,2},{6,1},{7,0},{8,7},{9,6},{1... | collective-permute-start | bytes 294920 | tf_op jit(solution)/shard_map/ppermute | solution.py:117

commit v4 on v3

--- a/solution.py
+++ b/solution.py
@@ -30,30 +30,42 @@
     return terms[0]
 
 
-def project(decoded, held, allowed, wq, wk, wv, q_out, k_out, v_out, att_out, ready=None):
-    ready = ready or (lambda name: None)
-    ready("q")
-    q_out[...] = dot(decoded[...], wq[...], 1, 0).astype(LOW)
-    ready("k")
-    k_out[...] = dot(held[...], wk[...], 1, 0).astype(LOW)
-    ready("v")
+def attend(queries, keys, allowed, att_out):
+    heads = range(queries.shape[1] // HEAD_DIM)
+    scores = [dot(queries[:, cols(head)], keys[:, cols(head)], 1, 1) for head in heads]
+    for head in heads:
+        masked = jnp.where(allowed > 0, scores[head], FULL(-1e30))
+        expo = jnp.exp(masked - jnp.max(masked, axis=-1, keepdims=True))
+        att_out[head] = expo * (1.0 / jnp.sum(expo, axis=-1, keepdims=True))
+
+
+def project(decoded, held, allowed, wq, wk, wv, q_out, k_out, v_out, att_out):
+    queries = dot(decoded[...], wq[...], 1, 0).astype(LOW)
+    keys = dot(held[...], wk[...], 1, 0).astype(LOW)
+    q_out[...] = queries
+    k_out[...] = keys
     v_out[...] = dot(held[...], wv[...], 1, 0).astype(LOW)
-    for head in range(q_out.shape[1] // HEAD_DIM):
-        scores = dot(q_out[:, cols(head)], k_out[:, cols(head)], 1, 1)
-        scores = jnp.where(allowed > 0, scores, FULL(-1e30))
-        expo = jnp.exp(scores - jnp.max(scores, axis=-1, keepdims=True))
-        att_out[head] = expo * (1.0 / jnp.sum(expo, axis=-1, keepdims=True))
-
-
-def chain(gradient, k_in, v_in, att, wq, wo, cg_out, sg_out, qg_tmp):
-    cg_out[...] = dot(gradient.astype(LOW), wo[...], 1, 1).astype(LOW)
-    for head in range(cg_out.shape[1] // HEAD_DIM):
-        prob = dot(cg_out[:, cols(head)], v_in[:, cols(head)], 1, 1)
+    attend(queries, keys, allowed, att_out)
+
+
+def chain(context, k_in, v_in, att, wq, sg_out, qg_tmp):
+    heads = range(context.shape[1] // HEAD_DIM)
+    probs = [dot(context[:, cols(head)], v_in[:, cols(head)], 1, 1) for head in heads]
+    grads = []
+    for head in heads:
         weight = att[head]
-        mean = jnp.sum(weight * prob, axis=-1, keepdims=True)
-        sg_out[head] = (weight * (prob - mean)).astype(LOW)
-        qg_tmp[:, cols(head)] = dot(sg_out[head], k_in[:, cols(head)], 1, 0).astype(LOW)
-    return dot(qg_tmp[...], wq[...], 1, 1).astype(LOW)
+        mean = jnp.sum(weight * probs[head], axis=-1, keepdims=True)
+        grads.append((weight * (probs[head] - mean)).astype(LOW))
+    for head in heads:
+        sg_out[head] = grads[head]
+        qg_tmp[:, cols(head)] = dot(grads[head], k_in[:, cols(head)], 1, 0).astype(LOW)
+    return dot(qg_tmp[...], wq[...], 1, 1)
+
+
+def context_of(gradient, wo, cg_out):
+    context = dot(gradient.astype(LOW), wo[...], 1, 1).astype(LOW)
+    cg_out[...] = context
+    return context
 
 
 def memory_terms(q_in, att, cg, sg, wk, wv, kg_tmp, vg_tmp):
@@ -136,43 +148,54 @@
         give[...] = chosen(odd, left, right).astype(LOW)
         keep[...] = chosen(odd, right, left) + base
 
-    def open_body(mine_ref, order_ref, length_ref, *refs):
-        (stash, *hbm), refs = refs[:7], refs[7:]
+    def open_body(mine_ref, *refs):
+        (order_hbm, length_hbm, stash, *hbm), refs = refs[:9], refs[9:]
         outs, refs = refs[:15], refs[15:]
-        q, att, cg, sg, give, keep, own, flags, place, dec, allowed, wq, wk, wv, wo = outs
-        g, mem, k, v, tmp, sems = refs
-        local = [wq, mem, wk, wv, g, wo]
-        turns = [
-            pltpu.make_async_copy(stash.at[0, order_ref[0, t]], dec.at[t], sems.at[len(local) + t])
-            for t in range(ticks)
-        ]
+        q, att, cg, sg, give, keep, own, flags, place, dec, allowed, wk, wq, wv, wo = outs
+        g, mem, k, v, tmp, order_ref, length_ref, sems = refs
+        pairs = [(order_hbm, order_ref), (length_hbm, length_ref)]
+        pairs += [(src.at[0], dst) for src, dst in zip(hbm, [mem, wk, wq, wv, g, wo])]
         copies = [
-            pltpu.make_async_copy(src.at[0], dst, sems.at[i])
-            for i, (src, dst) in enumerate(zip(hbm, local))
-        ]
-        copies = turns[:1] + copies + turns[1:]
+            pltpu.make_async_copy(src, dst, sems.at[i]) for i, (src, dst) in enumerate(pairs)
+        ]
         for copy in copies:
             copy.start()
-        waits = {"q": copies[:2], "k": copies[2:4], "v": copies[4:5]}
-
-        def ready(name):
-            for copy in waits[name]:
-                copy.wait()
-
-        positions = lax.broadcasted_iota(jnp.int32, (1, enc_rows), 1)
-        for t in range(ticks):
-            allowed[t : t + 1, :] = (positions < length_ref[0, t]).astype(FULL)
+        order_at, length_at, mem_at, wk_at, wq_at, wv_at, g_at, wo_at = copies
+        order_at.wait()
+        turns = [
+            pltpu.make_async_copy(stash.at[0, order_ref[0, t]], dec.at[t], sems.at[len(copies) + t])
+            for t in range(ticks)
+        ]
+        for turn in turns:
+            turn.start()
         own[...] = (lax.broadcasted_iota(jnp.int32, own.shape, 1) == mine_ref[0]).astype(FULL)
         flags[...] = jnp.broadcast_to((mine_ref[0] % 2).astype(FULL), flags.shape)
         columns = lax.broadcasted_iota(jnp.int32, place.shape, 1)
         start = (mine_ref[0] // 2) * share
         place[...] = ((columns >= start) & (columns < start + share)).astype(FULL)
-        project(dec.at[0], mem, allowed[0:1, :], wq, wk, wv, q, k, v, att, ready)
-        for copy in copies[5:]:
-            copy.wait()
+        length_at.wait()
+        positions = lax.broadcasted_iota(jnp.int32, (1, enc_rows), 1)
+        for t in range(ticks):
+            allowed[t : t + 1, :] = (positions < length_ref[0, t]).astype(FULL)
+        mem_at.wait()
+        wk_at.wait()
+        keys = dot(mem[...], wk[...], 1, 0).astype(LOW)
+        k[...] = keys
+        turns[0].wait()
+        wq_at.wait()
+        queries = dot(dec[0], wq[...], 1, 0).astype(LOW)
+        q[...] = queries
+        attend(queries, keys, allowed[0:1, :], att)
+        wv_at.wait()
+        v[...] = dot(mem[...], wv[...], 1, 0).astype(LOW)
+        g_at.wait()
+        wo_at.wait()
+        context = context_of(g[...], wo, cg)
         odd = flags[0:1, 0:1]
         base = chosen(odd, g[:, half:], g[:, :half]) * place[0:1, :]
-        write_pair(chain(g[...], k, v, att, wq, wo, cg, sg, tmp), base, odd, give, keep)
+        write_pair(chain(context, k, v, att, wq, sg, tmp), base, odd, give, keep)
+        for turn in turns[1:]:
+            turn.wait()
 
     def add_body(keep, got, place, small, first):
         total = keep[...] + got[...].astype(FULL)
@@ -221,7 +244,8 @@
         same, gradient = gradient_of(msgs, odd)
         rest = jnp.concatenate([msgs[0][:, half:].astype(FULL)] * (groups // 2), axis=1)
         base = (same + rest) * place[0:1, :]
-        write_pair(chain(gradient, k, v, att, wq, wo, cg, sg, tmp), base, odd, give, keep)
+        part = chain(context_of(gradient, wo, cg), k, v, att, wq, sg, tmp)
+        write_pair(part, base, odd, give, keep)
 
     def add_last_body(keep, got, *refs):
         pieces, msgs = refs[:groups], refs[groups:]
@@ -239,10 +263,10 @@
     open_outs = proj_outs[:1] + proj_outs[3:] + chain_outs + pair_outs
     open_outs += [((8, groups), FULL), ((8, 128), FULL), ((8, half), FULL)]
     open_outs += [(act_stash.shape[1:], LOW), ((8, enc_rows), FULL)]
-    open_outs += [(w.shape[1:], LOW) for w in (w_query, w_key, w_value, w_out)]
+    open_outs += [(w.shape[1:], LOW) for w in (w_key, w_query, w_value, w_out)]
     enc_low = ((enc_rows, width), LOW)
     msg_outs = [((rows, half), LOW), ((rows, half + share), LOW)]
-    (q, att, cg, sg, give, keep, own, flags, place, dec, allowed, wq, wk, wv, wo) = kernel(
+    (q, att, cg, sg, give, keep, own, flags, place, dec, allowed, wk, wq, wv, wo) = kernel(
         open_body,
         open_outs,
         [
@@ -251,10 +275,12 @@
             pltpu.VMEM((enc_rows, inner), LOW),
             pltpu.VMEM((enc_rows, inner), LOW),
             inner_tmp,
-            pltpu.SemaphoreType.DMA((6 + ticks,)),
+            pltpu.SMEM((1, ticks), jnp.int32),
+            pltpu.SMEM((1, ticks), jnp.int32),
+            pltpu.SemaphoreType.DMA((8 + ticks,)),
         ],
-        [smem] * 3 + [pltpu.HBM] * 7,
-    )(mine, slot_order, lengths, act_stash, w_query, memory, w_key, w_value, grad_in, w_out)
+        [smem] + [pltpu.HBM] * 9,
+    )(mine, slot_order, lengths, act_stash, memory, w_key, w_query, w_value, grad_in, w_out)
     held = memory[0]
     carry = None
     for tick in range(1, ticks):

time: 63.1 us -> 58.8 us (0.932)
  Pallas kernels: 17 us -> 13.4 us
  local copies, waits for them, and re-layouts: 0.66 us -> 0.01 us
    pallas_call x12, Pallas kernels: 17 us -> 13.4 us  [call(): pl.pallas_call(body, out_shape=[out_space(shape, kind) for shape, kind in...]
    unnamed x8 -> x4, local copies, waits for them, and re-layouts: 0.66 us -> 0.01 us
  transfers between devices with their start and end apart: 19 -> 19, of which waited for: 9 -> 9; matrix products, arithmetic and copies ran while one was open for 0% -> 0% of each run, Pallas kernels for 16% -> 13%
where the time goes in v4:
time: 58.8 us; the launch traced here: 58.6 us
  starting transfers between devices  23.5 us (40%)
  waiting for transfers between devices  21 us (36%)
  Pallas kernels  13.4 us (23%)
  between operations  0.77 us (1%)
    ppermute x16, starting transfers between devices, send(): return lax.ppermute(value, ('segment', 'head'), pairs)  21.2 us
    ppermute x16, waiting for transfers between devices, send(): return lax.ppermute(value, ('segment', 'head'), pairs)  14.6 us
    pallas_call x12, Pallas kernels, call(): pl.pallas_call(body, out_shape=[out_space(shape, kind) for shape, kind in...  13.4 us
    ppermute x3, waiting for transfers between devices, sent_pair(): return lax.ppermute(value, 'head', pairs)  6.38 us
    ppermute x3, starting transfers between devices, sent_pair(): return lax.ppermute(value, 'head', pairs)  2.32 us
  transfers between devices with their start and end apart: 19, of which 9 were waited for; matrix products, arithmetic and copies ran while one was open for 0% of the time, Pallas kernels for 13%

profile of v4, /device:TPU:1, one launch (start us, length us, event | category | flops | bytes accessed | tf_op | source)
XLA Modules:
  0.0 58.6 jit_solution(5196071250544734987)
XLA Ops:
  0.6 4.9 %shard_map.113 = (bf16[128,1024]{1,0:T(8,128)(2,1)S(1)}, f32[8,128,128]{2,1,0:T(8,128)S(1)}, bf16[128,1024]{1,0:T(8,128)(2,1)S(1)}, bf16[8,128,128]{2,1,0:T(8,12...) custom-call(s32[1]{0:T(128)} %bitcast.mine_ref, ...), custom_call_target="tpu_custom_call" | custom-call | tf_op jit(solution)/shard_map/pallas_call | solution.py:98
  5.5 2.2 %collective-permute-start = (bf16[128,256]{1,0:T(8,128)(2,1)S(1)}, bf16[128,256]{1,0:T(8,128)(2,1)S(1)}, u32[]{:S(2)}, u32[]{:S(2)}) collective-permute-start(bf16[128,256]{1,0:T(8,128)(2,1)S(1)} %get-tuple-element.48), channel_id=1, source_target_pairs={{0,1},{1,0},{2,3},{3,2},{4,5},{5,4},{6,7},{7,6},{8,9},{9,8},{10,11... | collective-permute-start | bytes 196616 | tf_op jit(solution)/shard_map/ppermute | solution.py:133
  7.7 1.0 %collective-permute-start.5 = (bf16[128,512]{1,0:T(8,128)(2,1)S(1)}, bf16[128,512]{1,0:T(8,128)(2,1)S(1)}, u32[]{:S(2)}, u32[]{:S(2)}) collective-permute-start(bf16[128,512]{1,0:T(8,128)(2,1)S(1)} %bitcast.4), channel_id=1, source_target_pairs={{0,28},{1,29},{2,30},{3,31},{4,0},{5,1},{6,2},{7,3},{8,4},{9,5},{1... | collective-permute-start | bytes 393224 | tf_op jit(solution)/shard_map/ppermute | solution.py:129
  9.4 1.6 %collective-permute-start.1 = (bf16[128,384]{1,0:T(8,128)(2,1)S(1)}, bf16[128,384]{1,0:T(8,128)(2,1)S(1)}, u32[]{:S(2)}, u32[]{:S(2)}) collective-permute-start(bf16[128,384]{1,0:T(8,128)(2,1)S(1)} %get-tuple-element.50), channel_id=1, source_target_pairs={{0,28},{1,29},{2,30},{3,31},{4,0},{5,1},{6,2},{7,3},{8,4},{9,5},{1... | collective-permute-start | bytes 294920 | tf_op jit(solution)/shard_map/ppermute | solution.py:129
  11.0 4.4 %collective-permute-start.4 = (bf16[128,256]{1,0:T(8,128)(2,1)S(1)}, bf16[128,256]{1,0:T(8,128)(2,1)S(1)}, u32[]{:S(2)}, u32[]{:S(2)}) collective-permute-start(bf16[128,256]{1,0:T(8,128)(2,1)S(1)} %get-tuple-element.51), channel_id=1, source_target_pairs={{0,31},{1,30},{2,29},{3,28},{4,3},{5,2},{6,1},{7,0},{8,7},{9,6},{1... | collective-permute-start | bytes 196616 | tf_op jit(solution)/shard_map/ppermute | solution.py:129
  16.1 1.1 %collective-permute-start.2 = (bf16[128,256]{1,0:T(8,128)(2,1)S(1)}, bf16[128,256]{1,0:T(8,128)(2,1)S(1)}, u32[]{:S(2)}, u32[]{:S(2)}) collective-permute-start(bf16[128,256]{1,0:T(8,128)(2,1)S(1)} %get-tuple-element.51), channel_id=1, source_target_pairs={{0,29},{1,28},{2,31},{3,30},{4,1},{5,0},{6,3},{7,2},{8,5},{9,4},{1... | collective-permute-start | bytes 196616 | tf_op jit(solution)/shard_map/ppermute | solution.py:129
  17.2 1.1 %shard_map.120 = bf16[128,512]{1,0:T(8,128)(2,1)S(1)} custom-call(f32[8,4]{1,0:T(8,128)S(1)} %get-tuple-element.71.own, f32[1,128,128]{2,1,0:T(8,128)S(1)} %copy-done, bf16[128,1024]{1,0:T(8,128)(2,1)S(1)} %get-tuple-element.72.q, f32[8,128,128]{2,1,0:T(8,128)S(1)} %get-tuple-element.73.att, bf16[128,1024]{1,0:T(8,128)(2,1)S(1)} %get-tuple-element.74.cg, ...), custom_call_target="tpu_custom_call" | custom-call | tf_op jit(solution)/shard_map/pallas_call | solution.py:98
  19.5 1.0 %shard_map.115 = (bf16[128,1024]{1,0:T(8,128)(2,1)S(1)}, bf16[128,1024]{1,0:T(8,128)(2,1)S(1)}, bf16[128,1024]{1,0:T(8,128)(2,1)S(1)}, f32[8,128,128]{2,1,0:T(8,128)S(1)}) custom-call(bf16[128,512]{1,0:T(8,128)(2,1)S(1)} %collective-permute-done.5.held, bf16[3,128,512]{2,1,0:T(8,128)(2,1)S(1)} %get-tuple-element.53.dec, ...), custom_call_target="tpu_custom_call" | custom-call | tf_op jit(solution)/shard_map/pallas_call | solution.py:98
  20.5 1.0 %collective-permute-done.3.refs_2_ = bf16[128,256]{1,0:T(8,128)(2,1)S(1)} collective-permute-done((bf16[128,256]{1,0:T(8,128)(2,1)S(1)}, bf16[128,256]{1,0:T(8,128)(2,1)S(1)}, u32[]{:S(2)}, u32[]{:S(2)}) %collective-permute-start.3) | collective-permute-done | bytes 65568 | tf_op jit(solution)/shard_map/ppermute | solution.py:129
  22.3 1.2 %shard_map.116 = (bf16[128,1024]{1,0:T(8,128)(2,1)S(1)}, bf16[8,128,128]{2,1,0:T(8,128)(2,1)S(1)}, bf16[128,256]{1,0:T(8,128)(2,1)S(1)}, f32[128,256]{1,0:T(8,128)S(1)}) custom-call(bf16[128,384]{1,0:T(8,128)(2,1)S(1)} %collective-permute-done.1.refs_0_, bf16[128,256]{1,0:T(8,128)(2,1)S(1)} %collective-permute-done.2.refs_1_, ...), custom_call_target="tpu_custom_call" | custom-call | tf_op jit(solution)/shard_map/pallas_call | solution.py:98
  23.6 3.1 %collective-permute-done.6.got = bf16[128,256]{1,0:T(8,128)(2,1)S(1)} collective-permute-done((bf16[128,256]{1,0:T(8,128)(2,1)S(1)}, bf16[128,256]{1,0:T(8,128)(2,1)S(1)}, u32[]{:S(2)}, u32[]{:S(2)}) %collective-permute-start.6) | collective-permute-done | bytes 65568 | tf_op jit(solution)/shard_map/ppermute | solution.py:133
  26.8 1.7 %collective-permute-start.7 = (bf16[128,384]{1,0:T(8,128)(2,1)S(1)}, bf16[128,384]{1,0:T(8,128)(2,1)S(1)}, u32[]{:S(2)}, u32[]{:S(2)}) collective-permute-start(bf16[128,384]{1,0:T(8,128)(2,1)S(1)} %get-tuple-element.64), channel_id=1, source_target_pairs={{0,28},{1,29},{2,30},{3,31},{4,0},{5,1},{6,2},{7,3},{8,4},{9,5},{1... | collective-permute-start | bytes 294920 | tf_op jit(solution)/shard_map/ppermute | solution.py:129
  28.4 1.1 %shard_map.121 = bf16[128,512]{1,0:T(8,128)(2,1)S(1)} custom-call(bf16[128,512]{1,0:T(8,128)(2,1)S(1)} %collective-permute-done.13.carry, bf16[128,1024]{1,0:T(8,128)(2,1)S(1)} %get-tuple-element.76.q, f32[8,128,128]{2,1,0:T(8,128)S(1)} %get-tuple-element.60.refs_8_.att, bf16[128,1024]{1,0:T(8,128)(2,1)S(1)} %get-tuple-element.77.cg, ...), custom_call_target="tpu_custom_call" | custom-call | tf_op jit(solution)/shard_map/pallas_call | solution.py:98
  29.5 3.5 %collective-permute-start.10 = (bf16[128,256]{1,0:T(8,128)(2,1)S(1)}, bf16[128,256]{1,0:T(8,128)(2,1)S(1)}, u32[]{:S(2)}, u32[]{:S(2)}) collective-permute-start(bf16[128,256]{1,0:T(8,128)(2,1)S(1)} %get-tuple-element.65), channel_id=1, source_target_pairs={{0,31},{1,30},{2,29},{3,28},{4,3},{5,2},{6,1},{7,0},{8,7},{9,6},{1... | collective-permute-start | bytes 196616 | tf_op jit(solution)/shard_map/ppermute | solution.py:129
  33.3 1.3 %collective-permute-start.14 = (bf16[128,512]{1,0:T(8,128)(2,1)S(1)}, bf16[128,512]{1,0:T(8,128)(2,1)S(1)}, u32[]{:S(2)}, u32[]{:S(2)}) collective-permute-start(bf16[128,512]{1,0:T(8,128)(2,1)S(1)} %shard_map.121), channel_id=1, source_target_pairs={{0,28},{1,29},{2,30},{3,31},{4,0},{5,1},{6,2},{7,3},{8,4},{9,5},{1... | collective-permute-start | bytes 393224 | tf_op jit(solution)/shard_map/ppermute | solution.py:129
  34.6 1.0 %shard_map.118 = (bf16[128,1024]{1,0:T(8,128)(2,1)S(1)}, bf16[128,1024]{1,0:T(8,128)(2,1)S(1)}, bf16[128,1024]{1,0:T(8,128)(2,1)S(1)}, f32[8,128,128]{2,1,0:T(8,128)S(1)}) custom-call(bf16[128,512]{1,0:T(8,128)(2,1)S(1)} %collective-permute-done.11.held, bf16[3,128,512]{2,1,0:T(8,128)(2,1)S(1)} %get-tuple-element.53.dec, ...), custom_call_target="tpu_custom_call" | custom-call | tf_op jit(solution)/shard_map/pallas_call | solution.py:98
  36.0 4.4 %collective-permute-done.9.refs_2_ = bf16[128,256]{1,0:T(8,128)(2,1)S(1)} collective-permute-done((bf16[128,256]{1,0:T(8,128)(2,1)S(1)}, bf16[128,256]{1,0:T(8,128)(2,1)S(1)}, u32[]{:S(2)}, u32[]{:S(2)}) %collective-permute-start.9) | collective-permute-done | bytes 65568 | tf_op jit(solution)/shard_map/ppermute | solution.py:129
  40.4 1.2 %shard_map.119 = (bf16[128,1024]{1,0:T(8,128)(2,1)S(1)}, bf16[8,128,128]{2,1,0:T(8,128)(2,1)S(1)}, bf16[128,256]{1,0:T(8,128)(2,1)S(1)}, f32[128,256]{1,0:T(8,128)S(1)}) custom-call(bf16[128,384]{1,0:T(8,128)(2,1)S(1)} %collective-permute-done.7.refs_0_, bf16[128,256]{1,0:T(8,128)(2,1)S(1)} %collective-permute-done.8.refs_1_, ...), custom_call_target="tpu_custom_call" | custom-call | tf_op jit(solution)/shard_map/pallas_call | solution.py:98
  41.7 1.1 %shard_map.122 = (bf16[128,128]{1,0:T(8,128)(2,1)S(1)}, bf16[128,128]{1,0:T(8,128)(2,1)S(1)}, bf16[128,128]{1,0:T(8,128)(2,1)S(1)}, bf16[128,128]{1,0:T(8,128)(2,1)S(1)}) custom-call(f32[8,4]{1,0:T(8,128)S(1)} %get-tuple-element.71.own, bf16[128,512]{1,0:T(8,128)(2,1)S(1)} %collective-permute-done.14.carry, bf16[128,1024]{1,0:T(8,128)(2,1)S(1)} %get-tuple-element.79.q, ...), custom_call_target="tpu_custom_call" | custom-call | tf_op jit(solution)/shard_map/pallas_call | solution.py:98
  42.8 2.6 %collective-permute-done.12.got = bf16[128,256]{1,0:T(8,128)(2,1)S(1)} collective-permute-done((bf16[128,256]{1,0:T(8,128)(2,1)S(1)}, bf16[128,256]{1,0:T(8,128)(2,1)S(1)}, u32[]{:S(2)}, u32[]{:S(2)}) %collective-permute-start.12) | collective-permute-done | bytes 65568 | tf_op jit(solution)/shard_map/ppermute | solution.py:133
  45.4 0.9 %collective-permute-start.15 = (bf16[128,384]{1,0:T(8,128)(2,1)S(1)}, bf16[128,384]{1,0:T(8,128)(2,1)S(1)}, u32[]{:S(2)}, u32[]{:S(2)}) collective-permute-start(bf16[128,384]{1,0:T(8,128)(2,1)S(1)} %get-tuple-element.86), channel_id=1, source_target_pairs={{0,28},{1,29},{2,30},{3,31},{4,0},{5,1},{6,2},{7,3},{8,4},{9,5},{1... | collective-permute-start | bytes 294920 | tf_op jit(solution)/shard_map/ppermute | solution.py:129
  46.7 2.4 %collective-permute-start.17 = (bf16[128,384]{1,0:T(8,128)(2,1)S(1)}, bf16[128,384]{1,0:T(8,128)(2,1)S(1)}, u32[]{:S(2)}, u32[]{:S(2)}) collective-permute-start(bf16[128,384]{1,0:T(8,128)(2,1)S(1)} %get-tuple-element.88), channel_id=1, source_target_pairs={{0,30},{1,31},{2,28},{3,29},{4,2},{5,3},{6,0},{7,1},{8,6},{9,7},{1... | collective-permute-start | bytes 294920 | tf_op jit(solution)/shard_map/ppermute | solution.py:129
  49.8 3.1 %collective-permute-done.16.refs_1_ = bf16[128,384]{1,0:T(8,128)(2,1)S(1)} collective-permute-done((bf16[128,384]{1,0:T(8,128)(2,1)S(1)}, bf16[128,384]{1,0:T(8,128)(2,1)S(1)}, u32[]{:S(2)}, u32[]{:S(2)}) %collective-permute-start.16) | collective-permute-done | bytes 98336 | tf_op jit(solution)/shard_map/ppermute | solution.py:129
  53.0 4.9 %collective-permute-done.17.refs_2_ = bf16[128,384]{1,0:T(8,128)(2,1)S(1)} collective-permute-done((bf16[128,384]{1,0:T(8,128)(2,1)S(1)}, bf16[128,384]{1,0:T(8,128)(2,1)S(1)}, u32[]{:S(2)}, u32[]{:S(2)}) %collective-permute-start.17) | collective-permute-done | bytes 98336 | tf_op jit(solution)/shard_map/ppermute | solution.py:129
  (30 shorter events, 6.3 us)
Async XLA Ops:
  0.6 7.1 %copy-start.1 = (bf16[1,128,512]{2,1,0:T(8,128)(2,1)S(1)}, bf16[1,128,512]{2,1,0:T(8,128)(2,1)}, u32[]{:S(2)}) copy-start(bf16[1,128,512]{2,1,0:T(8,128)(2,1)} %refs_3_.1) | copy-start | bytes 393220
  5.5 3.8 %collective-permute-start = (bf16[128,256]{1,0:T(8,128)(2,1)S(1)}, bf16[128,256]{1,0:T(8,128)(2,1)S(1)}, u32[]{:S(2)}, u32[]{:S(2)}) collective-permute-start(bf16[128,256]{1,0:T(8,128)(2,1)S(1)} %get-tuple-element.48), channel_id=1, source_target_pairs={{0,1},{1,0},{2,3},{3,2},{4,5},{5,4},{6,7},{7,6},{8,9},{9,8},{10,11... | collective-permute-start | bytes 196616 | tf_op jit(solution)/shard_map/ppermute | solution.py:133
  7.7 10.6 %collective-permute-start.5 = (bf16[128,512]{1,0:T(8,128)(2,1)S(1)}, bf16[128,512]{1,0:T(8,128)(2,1)S(1)}, u32[]{:S(2)}, u32[]{:S(2)}) collective-permute-start(bf16[128,512]{1,0:T(8,128)(2,1)S(1)} %bitcast.4), channel_id=1, source_target_pairs={{0,28},{1,29},{2,30},{3,31},{4,0},{5,1},{6,2},{7,3},{8,4},{9,5},{1... | collective-permute-start | bytes 393224 | tf_op jit(solution)/shard_map/ppermute | solution.py:129
  9.3 7.9 %copy-start = (f32[1,128,128]{2,1,0:T(8,128)S(1)}, f32[1,128,128]{2,1,0:T(8,128)}, u32[]{:S(2)}) copy-start(f32[1,128,128]{2,1,0:T(8,128)} %enc.1) | copy-start | bytes 196612
  9.4 12.9 %collective-permute-start.1 = (bf16[128,384]{1,0:T(8,128)(2,1)S(1)}, bf16[128,384]{1,0:T(8,128)(2,1)S(1)}, u32[]{:S(2)}, u32[]{:S(2)}) collective-permute-start(bf16[128,384]{1,0:T(8,128)(2,1)S(1)} %get-tuple-element.50), channel_id=1, source_target_pairs={{0,28},{1,29},{2,30},{3,31},{4,0},{5,1},{6,2},{7,3},{8,4},{9,5},{1... | collective-permute-start | bytes 294920 | tf_op jit(solution)/shard_map/ppermute | solution.py:129
  11.0 7.7 %collective-permute-start.4 = (bf16[128,256]{1,0:T(8,128)(2,1)S(1)}, bf16[128,256]{1,0:T(8,128)(2,1)S(1)}, u32[]{:S(2)}, u32[]{:S(2)}) collective-permute-start(bf16[128,256]{1,0:T(8,128)(2,1)S(1)} %get-tuple-element.51), channel_id=1, source_target_pairs={{0,31},{1,30},{2,29},{3,28},{4,3},{5,2},{6,1},{7,0},{8,7},{9,6},{1... | collective-permute-start | bytes 196616 | tf_op jit(solution)/shard_map/ppermute | solution.py:129
  15.4 6.1 %collective-permute-start.3 = (bf16[128,256]{1,0:T(8,128)(2,1)S(1)}, bf16[128,256]{1,0:T(8,128)(2,1)S(1)}, u32[]{:S(2)}, u32[]{:S(2)}) collective-permute-start(bf16[128,256]{1,0:T(8,128)(2,1)S(1)} %get-tuple-element.51), channel_id=1, source_target_pairs={{0,30},{1,31},{2,28},{3,29},{4,2},{5,3},{6,0},{7,1},{8,6},{9,7},{1... | collective-permute-start | bytes 196616 | tf_op jit(solution)/shard_map/ppermute | solution.py:129
  16.1 6.2 %collective-permute-start.2 = (bf16[128,256]{1,0:T(8,128)(2,1)S(1)}, bf16[128,256]{1,0:T(8,128)(2,1)S(1)}, u32[]{:S(2)}, u32[]{:S(2)}) collective-permute-start(bf16[128,256]{1,0:T(8,128)(2,1)S(1)} %get-tuple-element.51), channel_id=1, source_target_pairs={{0,29},{1,28},{2,31},{3,30},{4,1},{5,0},{6,3},{7,2},{8,5},{9,4},{1... | collective-permute-start | bytes 196616 | tf_op jit(solution)/shard_map/ppermute | solution.py:129
  18.3 10.2 %collective-permute-start.13 = (bf16[128,512]{1,0:T(8,128)(2,1)S(1)}, bf16[128,512]{1,0:T(8,128)(2,1)S(1)}, u32[]{:S(2)}, u32[]{:S(2)}) collective-permute-start(bf16[128,512]{1,0:T(8,128)(2,1)S(1)} %shard_map.120), channel_id=1, source_target_pairs={{0,28},{1,29},{2,30},{3,31},{4,0},{5,1},{6,2},{7,3},{8,4},{9,5},{1... | collective-permute-start | bytes 393224 | tf_op jit(solution)/shard_map/ppermute | solution.py:129
  18.7 14.7 %collective-permute-start.11 = (bf16[128,512]{1,0:T(8,128)(2,1)S(1)}, bf16[128,512]{1,0:T(8,128)(2,1)S(1)}, u32[]{:S(2)}, u32[]{:S(2)}) collective-permute-start(bf16[128,512]{1,0:T(8,128)(2,1)S(1)} %collective-permute-done.5.held), channel_id=1, source_target_pairs={{0,28},{1,29},{2,30},{3,31},{4,0},{5,1},{6,2},{7,3},{8,4},{9,5},{1... | collective-permute-start | bytes 393224 | tf_op jit(solution)/shard_map/ppermute | solution.py:129
  23.5 3.2 %collective-permute-start.6 = (bf16[128,256]{1,0:T(8,128)(2,1)S(1)}, bf16[128,256]{1,0:T(8,128)(2,1)S(1)}, u32[]{:S(2)}, u32[]{:S(2)}) collective-permute-start(bf16[128,256]{1,0:T(8,128)(2,1)S(1)} %get-tuple-element.63), channel_id=1, source_target_pairs={{0,1},{1,0},{2,3},{3,2},{4,5},{5,4},{6,7},{7,6},{8,9},{9,8},{10,11... | collective-permute-start | bytes 196616 | tf_op jit(solution)/shard_map/ppermute | solution.py:133
  26.8 13.6 %collective-permute-start.7 = (bf16[128,384]{1,0:T(8,128)(2,1)S(1)}, bf16[128,384]{1,0:T(8,128)(2,1)S(1)}, u32[]{:S(2)}, u32[]{:S(2)}) collective-permute-start(bf16[128,384]{1,0:T(8,128)(2,1)S(1)} %get-tuple-element.64), channel_id=1, source_target_pairs={{0,28},{1,29},{2,30},{3,31},{4,0},{5,1},{6,2},{7,3},{8,4},{9,5},{1... | collective-permute-start | bytes 294920 | tf_op jit(solution)/shard_map/ppermute | solution.py:129
  29.5 6.4 %collective-permute-start.10 = (bf16[128,256]{1,0:T(8,128)(2,1)S(1)}, bf16[128,256]{1,0:T(8,128)(2,1)S(1)}, u32[]{:S(2)}, u32[]{:S(2)}) collective-permute-start(bf16[128,256]{1,0:T(8,128)(2,1)S(1)} %get-tuple-element.65), channel_id=1, source_target_pairs={{0,31},{1,30},{2,29},{3,28},{4,3},{5,2},{6,1},{7,0},{8,7},{9,6},{1... | collective-permute-start | bytes 196616 | tf_op jit(solution)/shard_map/ppermute | solution.py:129
  33.0 7.4 %collective-permute-start.9 = (bf16[128,256]{1,0:T(8,128)(2,1)S(1)}, bf16[128,256]{1,0:T(8,128)(2,1)S(1)}, u32[]{:S(2)}, u32[]{:S(2)}) collective-permute-start(bf16[128,256]{1,0:T(8,128)(2,1)S(1)} %get-tuple-element.65), channel_id=1, source_target_pairs={{0,30},{1,31},{2,28},{3,29},{4,2},{5,3},{6,0},{7,1},{8,6},{9,7},{1... | collective-permute-start | bytes 196616 | tf_op jit(solution)/shard_map/ppermute | solution.py:129
  33.2 7.1 %collective-permute-start.8 = (bf16[128,256]{1,0:T(8,128)(2,1)S(1)}, bf16[128,256]{1,0:T(8,128)(2,1)S(1)}, u32[]{:S(2)}, u32[]{:S(2)}) collective-permute-start(bf16[128,256]{1,0:T(8,128)(2,1)S(1)} %get-tuple-element.65), channel_id=1, source_target_pairs={{0,29},{1,28},{2,31},{3,30},{4,1},{5,0},{6,3},{7,2},{8,5},{9,4},{1... | collective-permute-start | bytes 196616 | tf_op jit(solution)/shard_map/ppermute | solution.py:129
  33.3 8.3 %collective-permute-start.14 = (bf16[128,512]{1,0:T(8,128)(2,1)S(1)}, bf16[128,512]{1,0:T(8,128)(2,1)S(1)}, u32[]{:S(2)}, u32[]{:S(2)}) collective-permute-start(bf16[128,512]{1,0:T(8,128)(2,1)S(1)} %shard_map.121), channel_id=1, source_target_pairs={{0,28},{1,29},{2,30},{3,31},{4,0},{5,1},{6,2},{7,3},{8,4},{9,5},{1... | collective-permute-start | bytes 393224 | tf_op jit(solution)/shard_map/ppermute | solution.py:129
  41.6 3.7 %collective-permute-start.12 = (bf16[128,256]{1,0:T(8,128)(2,1)S(1)}, bf16[128,256]{1,0:T(8,128)(2,1)S(1)}, u32[]{:S(2)}, u32[]{:S(2)}) collective-permute-start(bf16[128,256]{1,0:T(8,128)(2,1)S(1)} %get-tuple-element.70), channel_id=1, source_target_pairs={{0,1},{1,0},{2,3},{3,2},{4,5},{5,4},{6,7},{7,6},{8,9},{9,8},{10,11... | collective-permute-start | bytes 196616 | tf_op jit(solution)/shard_map/ppermute | solution.py:133
  45.4 4.4 %collective-permute-start.15 = (bf16[128,384]{1,0:T(8,128)(2,1)S(1)}, bf16[128,384]{1,0:T(8,128)(2,1)S(1)}, u32[]{:S(2)}, u32[]{:S(2)}) collective-permute-start(bf16[128,384]{1,0:T(8,128)(2,1)S(1)} %get-tuple-element.86), channel_id=1, source_target_pairs={{0,28},{1,29},{2,30},{3,31},{4,0},{5,1},{6,2},{7,3},{8,4},{9,5},{1... | collective-permute-start | bytes 294920 | tf_op jit(solution)/shard_map/ppermute | solution.py:129
  46.3 6.7 %collective-permute-start.16 = (bf16[128,384]{1,0:T(8,128)(2,1)S(1)}, bf16[128,384]{1,0:T(8,128)(2,1)S(1)}, u32[]{:S(2)}, u32[]{:S(2)}) collective-permute-start(bf16[128,384]{1,0:T(8,128)(2,1)S(1)} %get-tuple-element.87), channel_id=1, source_target_pairs={{0,29},{1,28},{2,31},{3,30},{4,1},{5,0},{6,3},{7,2},{8,5},{9,4},{1... | collective-permute-start | bytes 294920 | tf_op jit(solution)/shard_map/ppermute | solution.py:129
  46.7 11.1 %collective-permute-start.17 = (bf16[128,384]{1,0:T(8,128)(2,1)S(1)}, bf16[128,384]{1,0:T(8,128)(2,1)S(1)}, u32[]{:S(2)}, u32[]{:S(2)}) collective-permute-start(bf16[128,384]{1,0:T(8,128)(2,1)S(1)} %get-tuple-element.88), channel_id=1, source_target_pairs={{0,30},{1,31},{2,28},{3,29},{4,2},{5,3},{6,0},{7,1},{8,6},{9,7},{1... | collective-permute-start | bytes 294920 | tf_op jit(solution)/shard_map/ppermute | solution.py:129
  49.1 8.7 %collective-permute-start.18 = (bf16[128,384]{1,0:T(8,128)(2,1)S(1)}, bf16[128,384]{1,0:T(8,128)(2,1)S(1)}, u32[]{:S(2)}, u32[]{:S(2)}) collective-permute-start(bf16[128,384]{1,0:T(8,128)(2,1)S(1)} %get-tuple-element.89), channel_id=1, source_target_pairs={{0,31},{1,30},{2,29},{3,28},{4,3},{5,2},{6,1},{7,0},{8,7},{9,6},{1... | collective-permute-start | bytes 294920 | tf_op jit(solution)/shard_map/ppermute | solution.py:129

commit v5 on v4

--- a/solution.py
+++ b/solution.py
@@ -30,13 +30,13 @@
     return terms[0]
 
 
-def attend(queries, keys, allowed, att_out):
+def attend(queries, keys, allowed, att_out, first=0):
     heads = range(queries.shape[1] // HEAD_DIM)
     scores = [dot(queries[:, cols(head)], keys[:, cols(head)], 1, 1) for head in heads]
     for head in heads:
         masked = jnp.where(allowed > 0, scores[head], FULL(-1e30))
         expo = jnp.exp(masked - jnp.max(masked, axis=-1, keepdims=True))
-        att_out[head] = expo * (1.0 / jnp.sum(expo, axis=-1, keepdims=True))
+        att_out[first + head] = expo * (1.0 / jnp.sum(expo, axis=-1, keepdims=True))
 
 
 def project(decoded, held, allowed, wq, wk, wv, q_out, k_out, v_out, att_out):
@@ -48,17 +48,22 @@
     attend(queries, keys, allowed, att_out)
 
 
-def chain(context, k_in, v_in, att, wq, sg_out, qg_tmp):
+def score_grads(context, keys, values, att, sg_out, qg_tmp, first=0):
     heads = range(context.shape[1] // HEAD_DIM)
-    probs = [dot(context[:, cols(head)], v_in[:, cols(head)], 1, 1) for head in heads]
+    probs = [dot(context[:, cols(head)], values[:, cols(head)], 1, 1) for head in heads]
     grads = []
     for head in heads:
-        weight = att[head]
+        weight = att[first + head]
         mean = jnp.sum(weight * probs[head], axis=-1, keepdims=True)
         grads.append((weight * (probs[head] - mean)).astype(LOW))
     for head in heads:
-        sg_out[head] = grads[head]
-        qg_tmp[:, cols(head)] = dot(grads[head], k_in[:, cols(head)], 1, 0).astype(LOW)
+        sg_out[first + head] = grads[head]
+        query_grad = dot(grads[head], keys[:, cols(head)], 1, 0)
+        qg_tmp[:, cols(first + head)] = query_grad.astype(LOW)
+
+
+def chain(context, k_in, v_in, att, wq, sg_out, qg_tmp):
+    score_grads(context, k_in, v_in, att, sg_out, qg_tmp)
     return dot(qg_tmp[...], wq[...], 1, 1)
 
 
@@ -152,50 +157,53 @@
         (order_hbm, length_hbm, stash, *hbm), refs = refs[:9], refs[9:]
         outs, refs = refs[:15], refs[15:]
         q, att, cg, sg, give, keep, own, flags, place, dec, allowed, wk, wq, wv, wo = outs
-        g, mem, k, v, tmp, order_ref, length_ref, sems = refs
-        pairs = [(order_hbm, order_ref), (length_hbm, length_ref)]
-        pairs += [(src.at[0], dst) for src, dst in zip(hbm, [mem, wk, wq, wv, g, wo])]
-        copies = [
-            pltpu.make_async_copy(src, dst, sems.at[i]) for i, (src, dst) in enumerate(pairs)
+        g, mem, stash_in, tmp, order_ref, length_ref, sems = refs
+        g_hbm, mem_hbm, *weights_hbm = hbm
+        count = iter(range(sems.shape[0]))
+
+        def load(src, dst):
+            return pltpu.make_async_copy(src, dst, sems.at[next(count)])
+
+        small = [load(order_hbm, order_ref), load(length_hbm, length_ref)]
+        small += [load(mem_hbm.at[0], mem), load(stash.at[0], stash_in)]
+        wk_at, wq_at, wv_at, wo_at = [
+            load(src.at[0], dst) for src, dst in zip(weights_hbm, (wk, wq, wv, wo))
         ]
-        for copy in copies:
+        base_at = load(g_hbm.at[0], g)
+        late = [wv_at, wo_at, base_at]
+        for copy in [*small, wk_at, wq_at]:
             copy.start()
-        order_at, length_at, mem_at, wk_at, wq_at, wv_at, g_at, wo_at = copies
-        order_at.wait()
-        turns = [
-            pltpu.make_async_copy(stash.at[0, order_ref[0, t]], dec.at[t], sems.at[len(copies) + t])
-            for t in range(ticks)
-        ]
-        for turn in turns:
-            turn.start()
+        for copy in late:
+            copy.start()
         own[...] = (lax.broadcasted_iota(jnp.int32, own.shape, 1) == mine_ref[0]).astype(FULL)
         flags[...] = jnp.broadcast_to((mine_ref[0] % 2).astype(FULL), flags.shape)
         columns = lax.broadcasted_iota(jnp.int32, place.shape, 1)
         start = (mine_ref[0] // 2) * share
         place[...] = ((columns >= start) & (columns < start + share)).astype(FULL)
-        length_at.wait()
+        for copy in small:
+            copy.wait()
         positions = lax.broadcasted_iota(jnp.int32, (1, enc_rows), 1)
         for t in range(ticks):
             allowed[t : t + 1, :] = (positions < length_ref[0, t]).astype(FULL)
-        mem_at.wait()
+        for t in range(1, ticks):
+            dec[t] = stash_in[order_ref[0, t]]
+        decoded = stash_in[order_ref[0, 0]]
+        held = mem[...]
         wk_at.wait()
-        keys = dot(mem[...], wk[...], 1, 0).astype(LOW)
-        k[...] = keys
-        turns[0].wait()
+        keys = dot(held, wk[...], 1, 0).astype(LOW)
         wq_at.wait()
-        queries = dot(dec[0], wq[...], 1, 0).astype(LOW)
+        queries = dot(decoded, wq[...], 1, 0).astype(LOW)
         q[...] = queries
         attend(queries, keys, allowed[0:1, :], att)
         wv_at.wait()
-        v[...] = dot(mem[...], wv[...], 1, 0).astype(LOW)
-        g_at.wait()
+        values = dot(held, wv[...], 1, 0).astype(LOW)
+        base_at.wait()
         wo_at.wait()
         context = context_of(g[...], wo, cg)
+        score_grads(context, keys, values, att, sg, tmp)
         odd = flags[0:1, 0:1]
         base = chosen(odd, g[:, half:], g[:, :half]) * place[0:1, :]
-        write_pair(chain(context, k, v, att, wq, sg, tmp), base, odd, give, keep)
-        for turn in turns[1:]:
-            turn.wait()
+        write_pair(dot(tmp[...], wq[...], 1, 1), base, odd, give, keep)
 
     def add_body(keep, got, place, small, first):
         total = keep[...] + got[...].astype(FULL)
@@ -216,15 +224,18 @@
         total = memory_terms(q, att, cg, sg, wk, wv, kg_tmp, vg_tmp)
         carry_out[...] = (carry[...].astype(FULL) + total).astype(LOW)
 
-    def memory_last_body(own, carry, q, att, cg, sg, wk, wv, *refs):
-        outs, (kg_tmp, vg_tmp) = refs[:groups], refs[groups:]
+    def memory_last_body(own, carry, q, att, cg, sg, wk, wv, give, keep, kg_tmp, vg_tmp):
         total = carry[...].astype(FULL) + memory_terms(q, att, cg, sg, wk, wv, kg_tmp, vg_tmp)
-        pieces = [total[:, g * share : (g + 1) * share].astype(LOW) for g in range(groups)]
-        for j, out in enumerate(outs):
+        pieces = [total[:, g * share : (g + 1) * share] for g in range(groups)]
+        for j in range(groups):
             piece = pieces[0 ^ j]
             for g in range(1, groups):
                 piece = jnp.where(own[0:1, g : g + 1] > 0, pieces[g ^ j], piece)
-            out[...] = piece
+            at = slice(j // 2 * share, (j // 2 + 1) * share)
+            if j % 2:
+                give[:, at] = piece.astype(LOW)
+            else:
+                keep[:, at] = piece
 
     def project_body(tick):
         def run(held, dec, allowed, wq, wk, wv, q, k, v, att):
@@ -247,17 +258,19 @@
         part = chain(context_of(gradient, wo, cg), k, v, att, wq, sg, tmp)
         write_pair(part, base, odd, give, keep)
 
-    def add_last_body(keep, got, *refs):
-        pieces, msgs = refs[:groups], refs[groups:]
+    def add_half_body(keep, got, small):
+        small[...] = (keep[...] + got[...].astype(FULL)).astype(LOW)
+
+    def add_last_body(small, keep, got, *msgs):
         total = (keep[...] + got[...].astype(FULL)).astype(LOW)
-        for piece, msg in zip(pieces, msgs):
-            msg[:, :half] = total
-            msg[:, half:] = piece[...]
+        for j, msg in enumerate(msgs):
+            msg[:, :half] = small[...]
+            msg[:, half:] = total[:, j * share : (j + 1) * share]
 
     def close_body(*refs):
         msgs, (flags, grad_out, enc_out) = refs[:groups], refs[groups:]
         grad_out[...] = gradient_of(msgs, flags[0:1, 0:1])[1]
-        enc_out[...] = tree_sum([msg[:, half:].astype(FULL) for msg in msgs])
+        enc_out[...] = tree_sum([msg[:, half:].astype(FULL) for msg in msgs[0::2]])
 
     smem = pltpu.SMEM
     open_outs = proj_outs[:1] + proj_outs[3:] + chain_outs + pair_outs
@@ -272,15 +285,14 @@
         [
             pltpu.VMEM((rows, width), FULL),
             pltpu.VMEM((enc_rows, width), LOW),
-            pltpu.VMEM((enc_rows, inner), LOW),
-            pltpu.VMEM((enc_rows, inner), LOW),
+            pltpu.VMEM(act_stash.shape[1:], LOW),
             inner_tmp,
             pltpu.SMEM((1, ticks), jnp.int32),
             pltpu.SMEM((1, ticks), jnp.int32),
-            pltpu.SemaphoreType.DMA((8 + ticks,)),
+            pltpu.SemaphoreType.DMA((16,)),
         ],
         [smem] + [pltpu.HBM] * 9,
-    )(mine, slot_order, lengths, act_stash, memory, w_key, w_query, w_value, grad_in, w_out)
+    )(mine, slot_order, lengths, act_stash, grad_in, memory, w_key, w_query, w_value, w_out)
     held = memory[0]
     carry = None
     for tick in range(1, ticks):
@@ -297,11 +309,16 @@
             *msgs, flags, place, k, v, att, wq, wo
         )
     got = sent_pair(give)
-    pieces = kernel(
-        memory_last_body, [((enc_rows, share), LOW)] * groups, [inner_tmp] * 2
+    enc_half = (enc_rows, groups // 2 * share)
+    enc_give, enc_keep = kernel(
+        memory_last_body, [(enc_half, LOW), (enc_half, FULL)], [inner_tmp] * 2
     )(own, carry, q, att, cg, sg, wk, wv)
-    outs = kernel(add_last_body, [((rows, half + share), LOW)] * groups, [])(keep, got, *pieces)
-    msgs = [send(outs[j], j) for j in range(groups)]
+    enc_got = sent_pair(enc_give)
+    (small,) = kernel(add_half_body, [((rows, half), LOW)], [])(keep, got)
+    wide = kernel(
+        add_last_body, [((rows, half + share), LOW)] * (groups // 2), []
+    )(small, enc_keep, enc_got)
+    msgs = [send(small if j % 2 else wide[j // 2], j) for j in range(groups)]
     gradient, carried = kernel(
         close_body, [((rows, width), FULL), ((enc_rows, share), FULL)], [],
         out_space=jax.ShapeDtypeStruct,

time: 58.8 us -> 58.3 us (level)
  Pallas kernels: 13.4 us -> 12.6 us
  starting transfers between devices: 23.5 us -> 24.3 us
    ppermute x3 -> x4, starting transfers between devices: 2.32 us -> 4.5 us  [sent_pair(): return lax.ppermute(value, 'head', pairs)]
    ppermute x16, starting transfers between devices: 21.2 us -> 19.8 us  [send(): return lax.ppermute(value, ('segment', 'head'), pairs)]
    ppermute x16, waiting for transfers between devices: 14.6 us -> 13.7 us  [send(): return lax.ppermute(value, ('segment', 'head'), pairs)]
    pallas_call x12 -> x13, Pallas kernels: 13.4 us -> 12.6 us  [call(): pl.pallas_call(body, out_shape=[out_space(shape, kind) for shape, kind in...]
    ppermute x3 -> x4, waiting for transfers between devices: 6.38 us -> 6.73 us  [sent_pair(): return lax.ppermute(value, 'head', pairs)]
  transfers between devices with their start and end apart: 19 -> 20, of which waited for: 9 -> 10; matrix products, arithmetic and copies ran while one was open for 0% -> 0% of each run, Pallas kernels for 13% -> 20%
where the time goes in v5:
time: 58.3 us; the launch traced here: 58.1 us
  starting transfers between devices  24.3 us (42%)
  waiting for transfers between devices  20.5 us (35%)
  Pallas kernels  12.6 us (22%)
  between operations  0.75 us (1%)
    ppermute x16, starting transfers between devices, send(): return lax.ppermute(value, ('segment', 'head'), pairs)  19.8 us
    ppermute x16, waiting for transfers between devices, send(): return lax.ppermute(value, ('segment', 'head'), pairs)  13.7 us
    pallas_call x13, Pallas kernels, call(): pl.pallas_call(body, out_shape=[out_space(shape, kind) for shape, kind in...  12.6 us
    ppermute x4, waiting for transfers between devices, sent_pair(): return lax.ppermute(value, 'head', pairs)  6.73 us
    ppermute x4, starting transfers between devices, sent_pair(): return lax.ppermute(value, 'head', pairs)  4.5 us
  transfers between devices with their start and end apart: 20, of which 10 were waited for; matrix products, arithmetic and copies ran while one was open for 0% of the time, Pallas kernels for 20%

profile of v5, /device:TPU:1, one launch (start us, length us, event | category | flops | bytes accessed | tf_op | source)
XLA Modules:
  0.0 58.1 jit_solution(13978153491069691162)
XLA Ops:
  0.7 4.1 %shard_map.113 = (bf16[128,1024]{1,0:T(8,128)(2,1)S(1)}, f32[8,128,128]{2,1,0:T(8,128)S(1)}, bf16[128,1024]{1,0:T(8,128)(2,1)S(1)}, bf16[8,128,128]{2,1,0:T(8,12...) custom-call(s32[1]{0:T(128)} %bitcast.mine_ref, ...), custom_call_target="tpu_custom_call" | custom-call | tf_op jit(solution)/shard_map/pallas_call | solution.py:103
  4.8 2.8 %collective-permute-start = (bf16[128,256]{1,0:T(8,128)(2,1)S(1)}, bf16[128,256]{1,0:T(8,128)(2,1)S(1)}, u32[]{:S(2)}, u32[]{:S(2)}) collective-permute-start(bf16[128,256]{1,0:T(8,128)(2,1)S(1)} %get-tuple-element.44), channel_id=1, source_target_pairs={{0,1},{1,0},{2,3},{3,2},{4,5},{5,4},{6,7},{7,6},{8,9},{9,8},{10,11... | collective-permute-start | bytes 196616 | tf_op jit(solution)/shard_map/ppermute | solution.py:138
  7.6 1.7 %collective-permute-done.got = bf16[128,256]{1,0:T(8,128)(2,1)S(1)} collective-permute-done((bf16[128,256]{1,0:T(8,128)(2,1)S(1)}, bf16[128,256]{1,0:T(8,128)(2,1)S(1)}, u32[]{:S(2)}, u32[]{:S(2)}) %collective-permute-start) | collective-permute-done | bytes 65568 | tf_op jit(solution)/shard_map/ppermute | solution.py:138
  9.3 3.2 %collective-permute-start.1 = (bf16[128,384]{1,0:T(8,128)(2,1)S(1)}, bf16[128,384]{1,0:T(8,128)(2,1)S(1)}, u32[]{:S(2)}, u32[]{:S(2)}) collective-permute-start(bf16[128,384]{1,0:T(8,128)(2,1)S(1)} %get-tuple-element.46), channel_id=1, source_target_pairs={{0,28},{1,29},{2,30},{3,31},{4,0},{5,1},{6,2},{7,3},{8,4},{9,5},{1... | collective-permute-start | bytes 294920 | tf_op jit(solution)/shard_map/ppermute | solution.py:134
  12.6 3.3 %collective-permute-start.4 = (bf16[128,256]{1,0:T(8,128)(2,1)S(1)}, bf16[128,256]{1,0:T(8,128)(2,1)S(1)}, u32[]{:S(2)}, u32[]{:S(2)}) collective-permute-start(bf16[128,256]{1,0:T(8,128)(2,1)S(1)} %get-tuple-element.47), channel_id=1, source_target_pairs={{0,31},{1,30},{2,29},{3,28},{4,3},{5,2},{6,1},{7,0},{8,7},{9,6},{1... | collective-permute-start | bytes 196616 | tf_op jit(solution)/shard_map/ppermute | solution.py:134
  15.9 1.1 %shard_map.121 = bf16[128,512]{1,0:T(8,128)(2,1)S(1)} custom-call(f32[8,4]{1,0:T(8,128)S(1)} %get-tuple-element.67.own, f32[1,128,128]{2,1,0:T(8,128)S(1)} %copy-done, bf16[128,1024]{1,0:T(8,128)(2,1)S(1)} %get-tuple-element.68.q, f32[8,128,128]{2,1,0:T(8,128)S(1)} %get-tuple-element.69.att, bf16[128,1024]{1,0:T(8,128)(2,1)S(1)} %get-tuple-element.70.cg, ...), custom_call_target="tpu_custom_call" | custom-call | tf_op jit(solution)/shard_map/pallas_call | solution.py:103
  17.7 1.1 %collective-permute-start.2 = (bf16[128,256]{1,0:T(8,128)(2,1)S(1)}, bf16[128,256]{1,0:T(8,128)(2,1)S(1)}, u32[]{:S(2)}, u32[]{:S(2)}) collective-permute-start(bf16[128,256]{1,0:T(8,128)(2,1)S(1)} %get-tuple-element.47), channel_id=1, source_target_pairs={{0,29},{1,28},{2,31},{3,30},{4,1},{5,0},{6,3},{7,2},{8,5},{9,4},{1... | collective-permute-start | bytes 196616 | tf_op jit(solution)/shard_map/ppermute | solution.py:134
  20.1 3.5 %collective-permute-done.3.refs_2_ = bf16[128,256]{1,0:T(8,128)(2,1)S(1)} collective-permute-done((bf16[128,256]{1,0:T(8,128)(2,1)S(1)}, bf16[128,256]{1,0:T(8,128)(2,1)S(1)}, u32[]{:S(2)}, u32[]{:S(2)}) %collective-permute-start.3) | collective-permute-done | bytes 65568 | tf_op jit(solution)/shard_map/ppermute | solution.py:134
  23.7 1.2 %shard_map.116 = (bf16[128,1024]{1,0:T(8,128)(2,1)S(1)}, bf16[8,128,128]{2,1,0:T(8,128)(2,1)S(1)}, bf16[128,256]{1,0:T(8,128)(2,1)S(1)}, f32[128,256]{1,0:T(8,128)S(1)}) custom-call(bf16[128,384]{1,0:T(8,128)(2,1)S(1)} %collective-permute-done.1.refs_0_, bf16[128,256]{1,0:T(8,128)(2,1)S(1)} %collective-permute-done.2.refs_1_, ...), custom_call_target="tpu_custom_call" | custom-call | tf_op jit(solution)/shard_map/pallas_call | solution.py:103
  25.0 1.1 %shard_map.122 = bf16[128,512]{1,0:T(8,128)(2,1)S(1)} custom-call(bf16[128,512]{1,0:T(8,128)(2,1)S(1)} %collective-permute-done.13.carry, bf16[128,1024]{1,0:T(8,128)(2,1)S(1)} %get-tuple-element.72.q, f32[8,128,128]{2,1,0:T(8,128)S(1)} %get-tuple-element.56.refs_8_.att, bf16[128,1024]{1,0:T(8,128)(2,1)S(1)} %get-tuple-element.73.cg, ...), custom_call_target="tpu_custom_call" | custom-call | tf_op jit(solution)/shard_map/pallas_call | solution.py:103
  26.1 2.6 %collective-permute-done.6.got = bf16[128,256]{1,0:T(8,128)(2,1)S(1)} collective-permute-done((bf16[128,256]{1,0:T(8,128)(2,1)S(1)}, bf16[128,256]{1,0:T(8,128)(2,1)S(1)}, u32[]{:S(2)}, u32[]{:S(2)}) %collective-permute-start.6) | collective-permute-done | bytes 65568 | tf_op jit(solution)/shard_map/ppermute | solution.py:138
  29.6 2.3 %collective-permute-start.10 = (bf16[128,256]{1,0:T(8,128)(2,1)S(1)}, bf16[128,256]{1,0:T(8,128)(2,1)S(1)}, u32[]{:S(2)}, u32[]{:S(2)}) collective-permute-start(bf16[128,256]{1,0:T(8,128)(2,1)S(1)} %get-tuple-element.61), channel_id=1, source_target_pairs={{0,31},{1,30},{2,29},{3,28},{4,3},{5,2},{6,1},{7,0},{8,7},{9,6},{1... | collective-permute-start | bytes 196616 | tf_op jit(solution)/shard_map/ppermute | solution.py:134
  31.9 2.5 %collective-permute-start.8 = (bf16[128,256]{1,0:T(8,128)(2,1)S(1)}, bf16[128,256]{1,0:T(8,128)(2,1)S(1)}, u32[]{:S(2)}, u32[]{:S(2)}) collective-permute-start(bf16[128,256]{1,0:T(8,128)(2,1)S(1)} %get-tuple-element.61), channel_id=1, source_target_pairs={{0,29},{1,28},{2,31},{3,30},{4,1},{5,0},{6,3},{7,2},{8,5},{9,4},{1... | collective-permute-start | bytes 196616 | tf_op jit(solution)/shard_map/ppermute | solution.py:134
  34.4 1.0 %shard_map.118 = (bf16[128,1024]{1,0:T(8,128)(2,1)S(1)}, bf16[128,1024]{1,0:T(8,128)(2,1)S(1)}, bf16[128,1024]{1,0:T(8,128)(2,1)S(1)}, f32[8,128,128]{2,1,0:T(8,128)S(1)}) custom-call(bf16[128,512]{1,0:T(8,128)(2,1)S(1)} %collective-permute-done.11.held, bf16[3,128,512]{2,1,0:T(8,128)(2,1)S(1)} %get-tuple-element.49.dec, ...), custom_call_target="tpu_custom_call" | custom-call | tf_op jit(solution)/shard_map/pallas_call | solution.py:103
  35.4 1.0 %collective-permute-done.10.refs_3_ = bf16[128,256]{1,0:T(8,128)(2,1)S(1)} collective-permute-done((bf16[128,256]{1,0:T(8,128)(2,1)S(1)}, bf16[128,256]{1,0:T(8,128)(2,1)S(1)}, u32[]{:S(2)}, u32[]{:S(2)}) %collective-permute-start.10) | collective-permute-done | bytes 65568 | tf_op jit(solution)/shard_map/ppermute | solution.py:134
  36.4 2.3 %collective-permute-done.9.refs_2_ = bf16[128,256]{1,0:T(8,128)(2,1)S(1)} collective-permute-done((bf16[128,256]{1,0:T(8,128)(2,1)S(1)}, bf16[128,256]{1,0:T(8,128)(2,1)S(1)}, u32[]{:S(2)}, u32[]{:S(2)}) %collective-permute-start.9) | collective-permute-done | bytes 65568 | tf_op jit(solution)/shard_map/ppermute | solution.py:134
  38.8 1.2 %shard_map.119 = (bf16[128,1024]{1,0:T(8,128)(2,1)S(1)}, bf16[8,128,128]{2,1,0:T(8,128)(2,1)S(1)}, bf16[128,256]{1,0:T(8,128)(2,1)S(1)}, f32[128,256]{1,0:T(8,128)S(1)}) custom-call(bf16[128,384]{1,0:T(8,128)(2,1)S(1)} %collective-permute-done.7.refs_0_, bf16[128,256]{1,0:T(8,128)(2,1)S(1)} %collective-permute-done.8.refs_1_, ...), custom_call_target="tpu_custom_call" | custom-call | tf_op jit(solution)/shard_map/pallas_call | solution.py:103
  40.3 1.1 %shard_map.123 = (bf16[128,256]{1,0:T(8,128)(2,1)S(1)}, f32[128,256]{1,0:T(8,128)S(1)}) custom-call(f32[8,4]{1,0:T(8,128)S(1)} %get-tuple-element.67.own, bf16[128,512]{1,0:T(8,128)(2,1)S(1)} %collective-permute-done.14.carry, bf16[128,1024]{1,0:T(8,128)(2,1)S(1)} %get-tuple-element.75.q, f32[8,128,128]{2,1,0:T(8,128)S(1)} %get-tuple-element.64.refs_8_.att, ...), custom_call_target="tpu_custom_call" | custom-call | tf_op jit(solution)/shard_map/pallas_call | solution.py:103
  41.4 1.3 %collective-permute-start.15 = (bf16[128,256]{1,0:T(8,128)(2,1)S(1)}, bf16[128,256]{1,0:T(8,128)(2,1)S(1)}, u32[]{:S(2)}, u32[]{:S(2)}) collective-permute-start(bf16[128,256]{1,0:T(8,128)(2,1)S(1)} %get-tuple-element.79), channel_id=1, source_target_pairs={{0,1},{1,0},{2,3},{3,2},{4,5},{5,4},{6,7},{7,6},{8,9},{9,8},{10,11... | collective-permute-start | bytes 196616 | tf_op jit(solution)/shard_map/ppermute | solution.py:138
  43.2 2.0 %collective-permute-done.15.got = bf16[128,256]{1,0:T(8,128)(2,1)S(1)} collective-permute-done((bf16[128,256]{1,0:T(8,128)(2,1)S(1)}, bf16[128,256]{1,0:T(8,128)(2,1)S(1)}, u32[]{:S(2)}, u32[]{:S(2)}) %collective-permute-start.15) | collective-permute-done | bytes 65568 | tf_op jit(solution)/shard_map/ppermute | solution.py:138
  45.2 1.1 %collective-permute-start.16 = (bf16[128,384]{1,0:T(8,128)(2,1)S(1)}, bf16[128,384]{1,0:T(8,128)(2,1)S(1)}, u32[]{:S(2)}, u32[]{:S(2)}) collective-permute-start(bf16[128,384]{1,0:T(8,128)(2,1)S(1)} %get-tuple-element.80), channel_id=1, source_target_pairs={{0,28},{1,29},{2,30},{3,31},{4,0},{5,1},{6,2},{7,3},{8,4},{9,5},{1... | collective-permute-start | bytes 294920 | tf_op jit(solution)/shard_map/ppermute | solution.py:134
  46.3 3.3 %collective-permute-start.18 = (bf16[128,384]{1,0:T(8,128)(2,1)S(1)}, bf16[128,384]{1,0:T(8,128)(2,1)S(1)}, u32[]{:S(2)}, u32[]{:S(2)}) collective-permute-start(bf16[128,384]{1,0:T(8,128)(2,1)S(1)} %get-tuple-element.81), channel_id=1, source_target_pairs={{0,30},{1,31},{2,28},{3,29},{4,2},{5,3},{6,0},{7,1},{8,6},{9,7},{1... | collective-permute-start | bytes 294920 | tf_op jit(solution)/shard_map/ppermute | solution.py:134
  50.7 5.5 %collective-permute-done.19.refs_3_ = bf16[128,256]{1,0:T(8,128)(2,1)S(1)} collective-permute-done((bf16[128,256]{1,0:T(8,128)(2,1)S(1)}, bf16[128,256]{1,0:T(8,128)(2,1)S(1)}, u32[]{:S(2)}, u32[]{:S(2)}) %collective-permute-start.19) | collective-permute-done | bytes 65568 | tf_op jit(solution)/shard_map/ppermute | solution.py:134
  56.2 1.2 %collective-permute-done.17.refs_1_ = bf16[128,256]{1,0:T(8,128)(2,1)S(1)} collective-permute-done((bf16[128,256]{1,0:T(8,128)(2,1)S(1)}, bf16[128,256]{1,0:T(8,128)(2,1)S(1)}, u32[]{:S(2)}, u32[]{:S(2)}) %collective-permute-start.17) | collective-permute-done | bytes 65568 | tf_op jit(solution)/shard_map/ppermute | solution.py:134
  (31 shorter events, 6.0 us)
Async XLA Ops:
  0.6 17.1 %collective-permute-start.5 = (bf16[128,512]{1,0:T(8,128)(2,1)}, bf16[128,512]{1,0:T(8,128)(2,1)S(1)}, u32[]{:S(2)}, u32[]{:S(2)}) collective-permute-start(bf16[128,512]{1,0:T(8,128)(2,1)} %bitcast.4), channel_id=1, source_target_pairs={{0,28},{1,29},{2,30},{3,31},{4,0},{5,1},{6,2},{7,3},{8,4},{9,5},{1... | collective-permute-start | bytes 393224 | tf_op jit(solution)/shard_map/ppermute | solution.py:134
  4.8 4.5 %collective-permute-start = (bf16[128,256]{1,0:T(8,128)(2,1)S(1)}, bf16[128,256]{1,0:T(8,128)(2,1)S(1)}, u32[]{:S(2)}, u32[]{:S(2)}) collective-permute-start(bf16[128,256]{1,0:T(8,128)(2,1)S(1)} %get-tuple-element.44), channel_id=1, source_target_pairs={{0,1},{1,0},{2,3},{3,2},{4,5},{5,4},{6,7},{7,6},{8,9},{9,8},{10,11... | collective-permute-start | bytes 196616 | tf_op jit(solution)/shard_map/ppermute | solution.py:138
  9.3 6.6 %copy-start = (f32[1,128,128]{2,1,0:T(8,128)S(1)}, f32[1,128,128]{2,1,0:T(8,128)}, u32[]{:S(2)}) copy-start(f32[1,128,128]{2,1,0:T(8,128)} %enc.1) | copy-start | bytes 196612
  9.3 14.4 %collective-permute-start.1 = (bf16[128,384]{1,0:T(8,128)(2,1)S(1)}, bf16[128,384]{1,0:T(8,128)(2,1)S(1)}, u32[]{:S(2)}, u32[]{:S(2)}) collective-permute-start(bf16[128,384]{1,0:T(8,128)(2,1)S(1)} %get-tuple-element.46), channel_id=1, source_target_pairs={{0,28},{1,29},{2,30},{3,31},{4,0},{5,1},{6,2},{7,3},{8,4},{9,5},{1... | collective-permute-start | bytes 294920 | tf_op jit(solution)/shard_map/ppermute | solution.py:134
  12.6 6.4 %collective-permute-start.4 = (bf16[128,256]{1,0:T(8,128)(2,1)S(1)}, bf16[128,256]{1,0:T(8,128)(2,1)S(1)}, u32[]{:S(2)}, u32[]{:S(2)}) collective-permute-start(bf16[128,256]{1,0:T(8,128)(2,1)S(1)} %get-tuple-element.47), channel_id=1, source_target_pairs={{0,31},{1,30},{2,29},{3,28},{4,3},{5,2},{6,1},{7,0},{8,7},{9,6},{1... | collective-permute-start | bytes 196616 | tf_op jit(solution)/shard_map/ppermute | solution.py:134
  16.9 8.0 %collective-permute-start.13 = (bf16[128,512]{1,0:T(8,128)(2,1)S(1)}, bf16[128,512]{1,0:T(8,128)(2,1)S(1)}, u32[]{:S(2)}, u32[]{:S(2)}) collective-permute-start(bf16[128,512]{1,0:T(8,128)(2,1)S(1)} %shard_map.121), channel_id=1, source_target_pairs={{0,28},{1,29},{2,30},{3,31},{4,0},{5,1},{6,2},{7,3},{8,4},{9,5},{1... | collective-permute-start | bytes 393224 | tf_op jit(solution)/shard_map/ppermute | solution.py:134
  17.7 6.0 %collective-permute-start.3 = (bf16[128,256]{1,0:T(8,128)(2,1)S(1)}, bf16[128,256]{1,0:T(8,128)(2,1)S(1)}, u32[]{:S(2)}, u32[]{:S(2)}) collective-permute-start(bf16[128,256]{1,0:T(8,128)(2,1)S(1)} %get-tuple-element.47), channel_id=1, source_target_pairs={{0,30},{1,31},{2,28},{3,29},{4,2},{5,3},{6,0},{7,1},{8,6},{9,7},{1... | collective-permute-start | bytes 196616 | tf_op jit(solution)/shard_map/ppermute | solution.py:134
  17.7 6.0 %collective-permute-start.2 = (bf16[128,256]{1,0:T(8,128)(2,1)S(1)}, bf16[128,256]{1,0:T(8,128)(2,1)S(1)}, u32[]{:S(2)}, u32[]{:S(2)}) collective-permute-start(bf16[128,256]{1,0:T(8,128)(2,1)S(1)} %get-tuple-element.47), channel_id=1, source_target_pairs={{0,29},{1,28},{2,31},{3,30},{4,1},{5,0},{6,3},{7,2},{8,5},{9,4},{1... | collective-permute-start | bytes 196616 | tf_op jit(solution)/shard_map/ppermute | solution.py:134
  19.0 12.9 %collective-permute-start.11 = (bf16[128,512]{1,0:T(8,128)(2,1)S(1)}, bf16[128,512]{1,0:T(8,128)(2,1)S(1)}, u32[]{:S(2)}, u32[]{:S(2)}) collective-permute-start(bf16[128,512]{1,0:T(8,128)(2,1)S(1)} %collective-permute-done.5.held), channel_id=1, source_target_pairs={{0,28},{1,29},{2,30},{3,31},{4,0},{5,1},{6,2},{7,3},{8,4},{9,5},{1... | collective-permute-start | bytes 393224 | tf_op jit(solution)/shard_map/ppermute | solution.py:134
  24.9 3.8 %collective-permute-start.6 = (bf16[128,256]{1,0:T(8,128)(2,1)S(1)}, bf16[128,256]{1,0:T(8,128)(2,1)S(1)}, u32[]{:S(2)}, u32[]{:S(2)}) collective-permute-start(bf16[128,256]{1,0:T(8,128)(2,1)S(1)} %get-tuple-element.59), channel_id=1, source_target_pairs={{0,1},{1,0},{2,3},{3,2},{4,5},{5,4},{6,7},{7,6},{8,9},{9,8},{10,11... | collective-permute-start | bytes 196616 | tf_op jit(solution)/shard_map/ppermute | solution.py:138
  26.1 14.2 %collective-permute-start.14 = (bf16[128,512]{1,0:T(8,128)(2,1)S(1)}, bf16[128,512]{1,0:T(8,128)(2,1)S(1)}, u32[]{:S(2)}, u32[]{:S(2)}) collective-permute-start(bf16[128,512]{1,0:T(8,128)(2,1)S(1)} %shard_map.122), channel_id=1, source_target_pairs={{0,28},{1,29},{2,30},{3,31},{4,0},{5,1},{6,2},{7,3},{8,4},{9,5},{1... | collective-permute-start | bytes 393224 | tf_op jit(solution)/shard_map/ppermute | solution.py:134
  28.8 10.0 %collective-permute-start.7 = (bf16[128,384]{1,0:T(8,128)(2,1)S(1)}, bf16[128,384]{1,0:T(8,128)(2,1)S(1)}, u32[]{:S(2)}, u32[]{:S(2)}) collective-permute-start(bf16[128,384]{1,0:T(8,128)(2,1)S(1)} %get-tuple-element.60), channel_id=1, source_target_pairs={{0,28},{1,29},{2,30},{3,31},{4,0},{5,1},{6,2},{7,3},{8,4},{9,5},{1... | collective-permute-start | bytes 294920 | tf_op jit(solution)/shard_map/ppermute | solution.py:134
  29.6 6.9 %collective-permute-start.10 = (bf16[128,256]{1,0:T(8,128)(2,1)S(1)}, bf16[128,256]{1,0:T(8,128)(2,1)S(1)}, u32[]{:S(2)}, u32[]{:S(2)}) collective-permute-start(bf16[128,256]{1,0:T(8,128)(2,1)S(1)} %get-tuple-element.61), channel_id=1, source_target_pairs={{0,31},{1,30},{2,29},{3,28},{4,3},{5,2},{6,1},{7,0},{8,7},{9,6},{1... | collective-permute-start | bytes 196616 | tf_op jit(solution)/shard_map/ppermute | solution.py:134
  31.9 6.9 %collective-permute-start.9 = (bf16[128,256]{1,0:T(8,128)(2,1)S(1)}, bf16[128,256]{1,0:T(8,128)(2,1)S(1)}, u32[]{:S(2)}, u32[]{:S(2)}) collective-permute-start(bf16[128,256]{1,0:T(8,128)(2,1)S(1)} %get-tuple-element.61), channel_id=1, source_target_pairs={{0,30},{1,31},{2,28},{3,29},{4,2},{5,3},{6,0},{7,1},{8,6},{9,7},{1... | collective-permute-start | bytes 196616 | tf_op jit(solution)/shard_map/ppermute | solution.py:134
  31.9 6.9 %collective-permute-start.8 = (bf16[128,256]{1,0:T(8,128)(2,1)S(1)}, bf16[128,256]{1,0:T(8,128)(2,1)S(1)}, u32[]{:S(2)}, u32[]{:S(2)}) collective-permute-start(bf16[128,256]{1,0:T(8,128)(2,1)S(1)} %get-tuple-element.61), channel_id=1, source_target_pairs={{0,29},{1,28},{2,31},{3,30},{4,1},{5,0},{6,3},{7,2},{8,5},{9,4},{1... | collective-permute-start | bytes 196616 | tf_op jit(solution)/shard_map/ppermute | solution.py:134
  40.0 3.2 %collective-permute-start.12 = (bf16[128,256]{1,0:T(8,128)(2,1)S(1)}, bf16[128,256]{1,0:T(8,128)(2,1)S(1)}, u32[]{:S(2)}, u32[]{:S(2)}) collective-permute-start(bf16[128,256]{1,0:T(8,128)(2,1)S(1)} %get-tuple-element.66), channel_id=1, source_target_pairs={{0,1},{1,0},{2,3},{3,2},{4,5},{5,4},{6,7},{7,6},{8,9},{9,8},{10,11... | collective-permute-start | bytes 196616 | tf_op jit(solution)/shard_map/ppermute | solution.py:138
  41.4 3.8 %collective-permute-start.15 = (bf16[128,256]{1,0:T(8,128)(2,1)S(1)}, bf16[128,256]{1,0:T(8,128)(2,1)S(1)}, u32[]{:S(2)}, u32[]{:S(2)}) collective-permute-start(bf16[128,256]{1,0:T(8,128)(2,1)S(1)} %get-tuple-element.79), channel_id=1, source_target_pairs={{0,1},{1,0},{2,3},{3,2},{4,5},{5,4},{6,7},{7,6},{8,9},{9,8},{10,11... | collective-permute-start | bytes 196616 | tf_op jit(solution)/shard_map/ppermute | solution.py:138
  45.2 12.2 %collective-permute-start.16 = (bf16[128,384]{1,0:T(8,128)(2,1)S(1)}, bf16[128,384]{1,0:T(8,128)(2,1)S(1)}, u32[]{:S(2)}, u32[]{:S(2)}) collective-permute-start(bf16[128,384]{1,0:T(8,128)(2,1)S(1)} %get-tuple-element.80), channel_id=1, source_target_pairs={{0,28},{1,29},{2,30},{3,31},{4,0},{5,1},{6,2},{7,3},{8,4},{9,5},{1... | collective-permute-start | bytes 294920 | tf_op jit(solution)/shard_map/ppermute | solution.py:134
  46.3 11.1 %collective-permute-start.18 = (bf16[128,384]{1,0:T(8,128)(2,1)S(1)}, bf16[128,384]{1,0:T(8,128)(2,1)S(1)}, u32[]{:S(2)}, u32[]{:S(2)}) collective-permute-start(bf16[128,384]{1,0:T(8,128)(2,1)S(1)} %get-tuple-element.81), channel_id=1, source_target_pairs={{0,30},{1,31},{2,28},{3,29},{4,2},{5,3},{6,0},{7,1},{8,6},{9,7},{1... | collective-permute-start | bytes 294920 | tf_op jit(solution)/shard_map/ppermute | solution.py:134
  49.6 6.6 %collective-permute-start.19 = (bf16[128,256]{1,0:T(8,128)(2,1)S(1)}, bf16[128,256]{1,0:T(8,128)(2,1)S(1)}, u32[]{:S(2)}, u32[]{:S(2)}) collective-permute-start(bf16[128,256]{1,0:T(8,128)(2,1)S(1)} %shard_map.120.small), channel_id=1, source_target_pairs={{0,31},{1,30},{2,29},{3,28},{4,3},{5,2},{6,1},{7,0},{8,7},{9,6},{1... | collective-permute-start | bytes 196616 | tf_op jit(solution)/shard_map/ppermute | solution.py:134
  50.0 7.4 %collective-permute-start.17 = (bf16[128,256]{1,0:T(8,128)(2,1)S(1)}, bf16[128,256]{1,0:T(8,128)(2,1)S(1)}, u32[]{:S(2)}, u32[]{:S(2)}) collective-permute-start(bf16[128,256]{1,0:T(8,128)(2,1)S(1)} %shard_map.120.small), channel_id=1, source_target_pairs={{0,29},{1,28},{2,31},{3,30},{4,1},{5,0},{6,3},{7,2},{8,5},{9,4},{1... | collective-permute-start | bytes 196616 | tf_op jit(solution)/shard_map/ppermute | solution.py:134

commit v6 on v5

--- a/solution.py
+++ b/solution.py
@@ -133,11 +133,12 @@
         ]
         return lax.ppermute(value, ("segment", "head"), pairs)
 
-    def sent_pair(value):
-        pairs = [(h, h ^ 1) for h in range(groups)]
+    def sent_pair(value, k=1):
+        pairs = [(h, h ^ k) for h in range(groups)]
         return lax.ppermute(value, "head", pairs)
 
     half = width // 2
+    near = groups // 2
     proj_outs = [
         ((rows, inner), LOW),
         ((enc_rows, inner), LOW),
@@ -174,7 +175,7 @@
         for copy in [*small, wk_at, wq_at]:
             copy.start()
         for copy in late:
-            copy.start()
+            copy.start(priority=1)
         own[...] = (lax.broadcasted_iota(jnp.int32, own.shape, 1) == mine_ref[0]).astype(FULL)
         flags[...] = jnp.broadcast_to((mine_ref[0] % 2).astype(FULL), flags.shape)
         columns = lax.broadcasted_iota(jnp.int32, place.shape, 1)
@@ -205,14 +206,23 @@
         base = chosen(odd, g[:, half:], g[:, :half]) * place[0:1, :]
         write_pair(dot(tmp[...], wq[...], 1, 1), base, odd, give, keep)
 
-    def add_body(keep, got, place, small, first):
-        total = keep[...] + got[...].astype(FULL)
+    def spread(rest, place):
+        return jnp.concatenate([rest.astype(FULL)] * (groups // 2), axis=1) * place[0:1, :]
+
+    def write_sum(total, place, carry, small, relay):
         small[...] = total.astype(LOW)
-        first[:, :half] = total.astype(LOW)
         rest = (total - total.astype(LOW).astype(FULL)) * place[0:1, :]
-        first[:, half:] = sum(
+        relay[:, :width] = carry[...]
+        relay[:, width:] = sum(
             rest[:, j * share : (j + 1) * share] for j in range(groups // 2)
         ).astype(LOW)
+
+    def add_open_body(keep, got, place, carry, small, relay):
+        write_sum(keep[...] + got[...].astype(FULL), place, carry, small, relay)
+
+    def add_body(last, keep, got, place, carry, small, relay):
+        total = keep[...] + got[...].astype(FULL) + spread(last[:, width:], place)
+        write_sum(total, place, carry, small, relay)
 
     def memory_open_body(own, enc, q, att, cg, sg, wk, wv, carry_out, kg_tmp, vg_tmp):
         total = memory_terms(q, att, cg, sg, wk, wv, kg_tmp, vg_tmp)
@@ -222,17 +232,18 @@
 
     def memory_body(carry, q, att, cg, sg, wk, wv, carry_out, kg_tmp, vg_tmp):
         total = memory_terms(q, att, cg, sg, wk, wv, kg_tmp, vg_tmp)
-        carry_out[...] = (carry[...].astype(FULL) + total).astype(LOW)
+        carry_out[...] = (carry[:, :width].astype(FULL) + total).astype(LOW)
 
     def memory_last_body(own, carry, q, att, cg, sg, wk, wv, give, keep, kg_tmp, vg_tmp):
-        total = carry[...].astype(FULL) + memory_terms(q, att, cg, sg, wk, wv, kg_tmp, vg_tmp)
+        total = memory_terms(q, att, cg, sg, wk, wv, kg_tmp, vg_tmp)
+        total = carry[:, :width].astype(FULL) + total
         pieces = [total[:, g * share : (g + 1) * share] for g in range(groups)]
         for j in range(groups):
             piece = pieces[0 ^ j]
             for g in range(1, groups):
                 piece = jnp.where(own[0:1, g : g + 1] > 0, pieces[g ^ j], piece)
-            at = slice(j // 2 * share, (j // 2 + 1) * share)
-            if j % 2:
+            at = slice(j % near * share, (j % near + 1) * share)
+            if j >= near:
                 give[:, at] = piece.astype(LOW)
             else:
                 keep[:, at] = piece
@@ -253,13 +264,13 @@
         flags, place, k, v, att, wq, wo, cg, sg, give, keep, tmp = refs
         odd = flags[0:1, 0:1]
         same, gradient = gradient_of(msgs, odd)
-        rest = jnp.concatenate([msgs[0][:, half:].astype(FULL)] * (groups // 2), axis=1)
-        base = (same + rest) * place[0:1, :]
+        base = same * place[0:1, :]
         part = chain(context_of(gradient, wo, cg), k, v, att, wq, sg, tmp)
         write_pair(part, base, odd, give, keep)
 
-    def add_half_body(keep, got, small):
-        small[...] = (keep[...] + got[...].astype(FULL)).astype(LOW)
+    def add_half_body(last, keep, got, place, small):
+        total = keep[...] + got[...].astype(FULL) + spread(last[:, width:], place)
+        small[...] = total.astype(LOW)
 
     def add_last_body(small, keep, got, *msgs):
         total = (keep[...] + got[...].astype(FULL)).astype(LOW)
@@ -270,7 +281,7 @@
     def close_body(*refs):
         msgs, (flags, grad_out, enc_out) = refs[:groups], refs[groups:]
         grad_out[...] = gradient_of(msgs, flags[0:1, 0:1])[1]
-        enc_out[...] = tree_sum([msg[:, half:].astype(FULL) for msg in msgs[0::2]])
+        enc_out[...] = tree_sum([msg[:, half:].astype(FULL) for msg in msgs[:near]])
 
     smem = pltpu.SMEM
     open_outs = proj_outs[:1] + proj_outs[3:] + chain_outs + pair_outs
@@ -278,7 +289,7 @@
     open_outs += [(act_stash.shape[1:], LOW), ((8, enc_rows), FULL)]
     open_outs += [(w.shape[1:], LOW) for w in (w_key, w_query, w_value, w_out)]
     enc_low = ((enc_rows, width), LOW)
-    msg_outs = [((rows, half), LOW), ((rows, half + share), LOW)]
+    msg_outs = [((rows, half), LOW), ((enc_rows, width + share), LOW)]
     (q, att, cg, sg, give, keep, own, flags, place, dec, allowed, wk, wq, wv, wo) = kernel(
         open_body,
         open_outs,
@@ -294,16 +305,18 @@
         [smem] + [pltpu.HBM] * 9,
     )(mine, slot_order, lengths, act_stash, grad_in, memory, w_key, w_query, w_value, w_out)
     held = memory[0]
-    carry = None
+    relay = None
     for tick in range(1, ticks):
         got = sent_pair(give)
         held = send(held, 0)
         (carry,) = kernel(
             memory_body if tick > 1 else memory_open_body, [enc_low], [inner_tmp] * 2
-        )(*([carry] if tick > 1 else [own, enc_grad_in]), q, att, cg, sg, wk, wv)
-        small, first = kernel(add_body, msg_outs, [])(keep, got, place)
-        msgs = [send(small if j else first, j) for j in range(groups)]
-        carry = send(carry, 0)
+        )(*([relay] if tick > 1 else [own, enc_grad_in]), q, att, cg, sg, wk, wv)
+        small, relay = kernel(add_body if tick > 1 else add_open_body, msg_outs, [])(
+            *([relay] if tick > 1 else []), keep, got, place, carry
+        )
+        msgs = [send(small, j) for j in range(groups)]
+        relay = send(relay, 0)
         q, k, v, att = kernel(project_body(tick), proj_outs, [])(held, dec, allowed, wq, wk, wv)
         cg, sg, give, keep = kernel(step_body, chain_outs + pair_outs, [inner_tmp])(
             *msgs, flags, place, k, v, att, wq, wo
@@ -312,13 +325,15 @@
     enc_half = (enc_rows, groups // 2 * share)
     enc_give, enc_keep = kernel(
         memory_last_body, [(enc_half, LOW), (enc_half, FULL)], [inner_tmp] * 2
-    )(own, carry, q, att, cg, sg, wk, wv)
-    enc_got = sent_pair(enc_give)
-    (small,) = kernel(add_half_body, [((rows, half), LOW)], [])(keep, got)
+    )(own, relay, q, att, cg, sg, wk, wv)
+    enc_got = sent_pair(enc_give, near)
+    (small,) = kernel(add_half_body, [((rows, half), LOW)], [])(
+        relay, keep, got, place
+    )
     wide = kernel(
         add_last_body, [((rows, half + share), LOW)] * (groups // 2), []
     )(small, enc_keep, enc_got)
-    msgs = [send(small if j % 2 else wide[j // 2], j) for j in range(groups)]
+    msgs = [send(wide[j] if j < near else small, j) for j in range(groups)]
     gradient, carried = kernel(
         close_body, [((rows, width), FULL), ((enc_rows, share), FULL)], [],
         out_space=jax.ShapeDtypeStruct,

time: 58.3 us -> 61.9 us (1.062)
  the two profiles are of different devices: /device:TPU:1 before, /device:TPU:0 now
where the time goes in v6:
time: 61.9 us; the launch traced here: 61.6 us
  starting transfers between devices  29.6 us (48%)
  waiting for transfers between devices  18.6 us (30%)
  Pallas kernels  12.6 us (20%)
  between operations  0.77 us (1%)
    ppermute x16, starting transfers between devices, send(): return lax.ppermute(value, ('segment', 'head'), pairs)  24.6 us
    pallas_call x13, Pallas kernels, call(): pl.pallas_call(body, out_shape=[out_space(shape, kind) for shape, kind in...  12.6 us
    ppermute x16, waiting for transfers between devices, send(): return lax.ppermute(value, ('segment', 'head'), pairs)  10.7 us
    ppermute x4, waiting for transfers between devices, sent_pair(): return lax.ppermute(value, 'head', pairs)  7.87 us
    ppermute x4, starting transfers between devices, sent_pair(): return lax.ppermute(value, 'head', pairs)  4.96 us
  transfers between devices with their start and end apart: 20, of which 9 were waited for; matrix products, arithmetic and copies ran while one was open for 0% of the time, Pallas kernels for 19%

profile of v6, /device:TPU:0, one launch (start us, length us, event | category | flops | bytes accessed | tf_op | source)
XLA Modules:
  0.0 61.6 jit_solution(9869602012709289391)
XLA Ops:
  0.6 3.4 %collective-permute-start.6 = (bf16[128,512]{1,0:T(8,128)(2,1)}, bf16[128,512]{1,0:T(8,128)(2,1)S(1)}, u32[]{:S(2)}, u32[]{:S(2)}) collective-permute-start(bf16[128,512]{1,0:T(8,128)(2,1)} %bitcast.4), channel_id=1, source_target_pairs={{0,28},{1,29},{2,30},{3,31},{4,0},{5,1},{6,2},{7,3},{8,4},{9,5},{1... | collective-permute-start | bytes 393224 | tf_op jit(solution)/shard_map/ppermute | solution.py:134
  4.0 4.1 %shard_map.113 = (bf16[128,1024]{1,0:T(8,128)(2,1)S(1)}, f32[8,128,128]{2,1,0:T(8,128)S(1)}, bf16[128,1024]{1,0:T(8,128)(2,1)S(1)}, bf16[8,128,128]{2,1,0:T(8,12...) custom-call(s32[1]{0:T(128)} %bitcast.mine_ref, ...), custom_call_target="tpu_custom_call" | custom-call | tf_op jit(solution)/shard_map/pallas_call | solution.py:103
  8.2 1.6 %collective-permute-start = (bf16[128,256]{1,0:T(8,128)(2,1)S(1)}, bf16[128,256]{1,0:T(8,128)(2,1)S(1)}, u32[]{:S(2)}, u32[]{:S(2)}) collective-permute-start(bf16[128,256]{1,0:T(8,128)(2,1)S(1)} %get-tuple-element.44), channel_id=1, source_target_pairs={{0,1},{1,0},{2,3},{3,2},{4,5},{5,4},{6,7},{7,6},{8,9},{9,8},{10,11... | collective-permute-start | bytes 196616 | tf_op jit(solution)/shard_map/ppermute | solution.py:138
  9.8 1.1 %shard_map.114.carry = bf16[128,512]{1,0:T(8,128)(2,1)S(1)} custom-call(f32[8,4]{1,0:T(8,128)S(1)} %get-tuple-element.46.own, f32[1,128,128]{2,1,0:T(8,128)S(1)} %copy-done, bf16[128,1024]{1,0:T(8,128)(2,1)S(1)} %get-tuple-element.47.q, f32[8,128,128]{2,1,0:T(8,128)S(1)} %get-tuple-element.48.att, bf16[128,1024]{1,0:T(8,128)(2,1)S(1)} %get-tuple-element.49.cg, ...), custom_call_target="tpu_custom_call" | custom-call | tf_op jit(solution)/shard_map/pallas_call | solution.py:103
  10.9 1.6 %collective-permute-done.got = bf16[128,256]{1,0:T(8,128)(2,1)S(1)} collective-permute-done((bf16[128,256]{1,0:T(8,128)(2,1)S(1)}, bf16[128,256]{1,0:T(8,128)(2,1)S(1)}, u32[]{:S(2)}, u32[]{:S(2)}) %collective-permute-start) | collective-permute-done | bytes 65568 | tf_op jit(solution)/shard_map/ppermute | solution.py:138
  13.5 1.1 %collective-permute-start.3 = (bf16[128,256]{1,0:T(8,128)(2,1)S(1)}, bf16[128,256]{1,0:T(8,128)(2,1)S(1)}, u32[]{:S(2)}, u32[]{:S(2)}) collective-permute-start(bf16[128,256]{1,0:T(8,128)(2,1)S(1)} %get-tuple-element.54), channel_id=1, source_target_pairs={{0,29},{1,28},{2,31},{3,30},{4,1},{5,0},{6,3},{7,2},{8,5},{9,4},{1... | collective-permute-start | bytes 196616 | tf_op jit(solution)/shard_map/ppermute | solution.py:134
  14.6 3.4 %collective-permute-start.4 = (bf16[128,256]{1,0:T(8,128)(2,1)S(1)}, bf16[128,256]{1,0:T(8,128)(2,1)S(1)}, u32[]{:S(2)}, u32[]{:S(2)}) collective-permute-start(bf16[128,256]{1,0:T(8,128)(2,1)S(1)} %get-tuple-element.54), channel_id=1, source_target_pairs={{0,30},{1,31},{2,28},{3,29},{4,2},{5,3},{6,0},{7,1},{8,6},{9,7},{1... | collective-permute-start | bytes 196616 | tf_op jit(solution)/shard_map/ppermute | solution.py:134
  19.0 1.1 %collective-permute-done.4.refs_2_ = bf16[128,256]{1,0:T(8,128)(2,1)S(1)} collective-permute-done((bf16[128,256]{1,0:T(8,128)(2,1)S(1)}, bf16[128,256]{1,0:T(8,128)(2,1)S(1)}, u32[]{:S(2)}, u32[]{:S(2)}) %collective-permute-start.4) | collective-permute-done | bytes 65568 | tf_op jit(solution)/shard_map/ppermute | solution.py:134
  20.1 4.1 %collective-permute-done.5.refs_3_ = bf16[128,256]{1,0:T(8,128)(2,1)S(1)} collective-permute-done((bf16[128,256]{1,0:T(8,128)(2,1)S(1)}, bf16[128,256]{1,0:T(8,128)(2,1)S(1)}, u32[]{:S(2)}, u32[]{:S(2)}) %collective-permute-start.5) | collective-permute-done | bytes 65568 | tf_op jit(solution)/shard_map/ppermute | solution.py:134
  24.2 1.2 %shard_map.117 = (bf16[128,1024]{1,0:T(8,128)(2,1)S(1)}, bf16[8,128,128]{2,1,0:T(8,128)(2,1)S(1)}, bf16[128,256]{1,0:T(8,128)(2,1)S(1)}, f32[128,256]{1,0:T(8,128)S(1)}) custom-call(bf16[128,256]{1,0:T(8,128)(2,1)S(1)} %collective-permute-done.2.refs_0_, bf16[128,256]{1,0:T(8,128)(2,1)S(1)} %collective-permute-done.3.refs_1_, ...), custom_call_target="tpu_custom_call" | custom-call | tf_op jit(solution)/shard_map/pallas_call | solution.py:103
  25.5 2.6 %collective-permute-start.13 = (bf16[128,512]{1,0:T(8,128)(2,1)S(1)}, bf16[128,512]{1,0:T(8,128)(2,1)S(1)}, u32[]{:S(2)}, u32[]{:S(2)}) collective-permute-start(bf16[128,512]{1,0:T(8,128)(2,1)S(1)} %collective-permute-done.6.held), channel_id=1, source_target_pairs={{0,28},{1,29},{2,30},{3,31},{4,0},{5,1},{6,2},{7,3},{8,4},{9,5},{1... | collective-permute-start | bytes 393224 | tf_op jit(solution)/shard_map/ppermute | solution.py:134
  28.1 1.1 %shard_map.118.carry = bf16[128,512]{1,0:T(8,128)(2,1)S(1)} custom-call(bf16[128,640]{1,0:T(8,128)(2,1)S(1)} %collective-permute-done.1.carry.last, bf16[128,1024]{1,0:T(8,128)(2,1)S(1)} %get-tuple-element.65.q, f32[8,128,128]{2,1,0:T(8,128)S(1)} %get-tuple-element.61.refs_8_.att, bf16[128,1024]{1,0:T(8,128)(2,1)S(1)} %get-tuple-element.66.cg, ...), custom_call_target="tpu_custom_call" | custom-call | tf_op jit(solution)/shard_map/pallas_call | solution.py:103
  31.4 2.4 %collective-permute-start.11 = (bf16[128,256]{1,0:T(8,128)(2,1)S(1)}, bf16[128,256]{1,0:T(8,128)(2,1)S(1)}, u32[]{:S(2)}, u32[]{:S(2)}) collective-permute-start(bf16[128,256]{1,0:T(8,128)(2,1)S(1)} %get-tuple-element.69), channel_id=1, source_target_pairs={{0,30},{1,31},{2,28},{3,29},{4,2},{5,3},{6,0},{7,1},{8,6},{9,7},{1... | collective-permute-start | bytes 196616 | tf_op jit(solution)/shard_map/ppermute | solution.py:134
  33.8 3.1 %collective-permute-start.12 = (bf16[128,256]{1,0:T(8,128)(2,1)S(1)}, bf16[128,256]{1,0:T(8,128)(2,1)S(1)}, u32[]{:S(2)}, u32[]{:S(2)}) collective-permute-start(bf16[128,256]{1,0:T(8,128)(2,1)S(1)} %get-tuple-element.69), channel_id=1, source_target_pairs={{0,31},{1,30},{2,29},{3,28},{4,3},{5,2},{6,1},{7,0},{8,7},{9,6},{1... | collective-permute-start | bytes 196616 | tf_op jit(solution)/shard_map/ppermute | solution.py:134
  37.9 1.5 %collective-permute-done.12.refs_3_ = bf16[128,256]{1,0:T(8,128)(2,1)S(1)} collective-permute-done((bf16[128,256]{1,0:T(8,128)(2,1)S(1)}, bf16[128,256]{1,0:T(8,128)(2,1)S(1)}, u32[]{:S(2)}, u32[]{:S(2)}) %collective-permute-start.12) | collective-permute-done | bytes 65568 | tf_op jit(solution)/shard_map/ppermute | solution.py:134
  39.4 1.2 %shard_map.121 = (bf16[128,1024]{1,0:T(8,128)(2,1)S(1)}, bf16[8,128,128]{2,1,0:T(8,128)(2,1)S(1)}, bf16[128,256]{1,0:T(8,128)(2,1)S(1)}, f32[128,256]{1,0:T(8,128)S(1)}) custom-call(bf16[128,256]{1,0:T(8,128)(2,1)S(1)} %collective-permute-done.9.refs_0_, bf16[128,256]{1,0:T(8,128)(2,1)S(1)} %collective-permute-done.10.refs_1_, ...), custom_call_target="tpu_custom_call" | custom-call | tf_op jit(solution)/shard_map/pallas_call | solution.py:103
  40.7 2.1 %collective-permute-start.14 = (bf16[128,256]{1,0:T(8,128)(2,1)S(1)}, bf16[128,256]{1,0:T(8,128)(2,1)S(1)}, u32[]{:S(2)}, u32[]{:S(2)}) collective-permute-start(bf16[128,256]{1,0:T(8,128)(2,1)S(1)} %get-tuple-element.74), channel_id=1, source_target_pairs={{0,1},{1,0},{2,3},{3,2},{4,5},{5,4},{6,7},{7,6},{8,9},{9,8},{10,11... | collective-permute-start | bytes 196616 | tf_op jit(solution)/shard_map/ppermute | solution.py:138
  42.8 1.1 %shard_map.123 = (bf16[128,256]{1,0:T(8,128)(2,1)S(1)}, f32[128,256]{1,0:T(8,128)S(1)}) custom-call(f32[8,4]{1,0:T(8,128)S(1)} %get-tuple-element.46.own, bf16[128,640]{1,0:T(8,128)(2,1)S(1)} %collective-permute-done.8.last.carry, bf16[128,1024]{1,0:T(8,128)(2,1)S(1)} %get-tuple-element.75.q, f32[8,128,128]{2,1,0:T(8,128)S(1)} %get-tuple-element.72.refs_8_.att, ...), custom_call_target="tpu_custom_call" | custom-call | tf_op jit(solution)/shard_map/pallas_call | solution.py:103
  43.9 1.1 %collective-permute-start.15 = (bf16[128,256]{1,0:T(8,128)(2,1)S(1)}, bf16[128,256]{1,0:T(8,128)(2,1)S(1)}, u32[]{:S(2)}, u32[]{:S(2)}) collective-permute-start(bf16[128,256]{1,0:T(8,128)(2,1)S(1)} %get-tuple-element.79), channel_id=1, source_target_pairs={{0,2},{1,3},{2,0},{3,1},{4,6},{5,7},{6,4},{7,5},{8,10},{9,11},{10,... | collective-permute-start | bytes 196616 | tf_op jit(solution)/shard_map/ppermute | solution.py:138
  45.2 5.5 %collective-permute-done.15.got = bf16[128,256]{1,0:T(8,128)(2,1)S(1)} collective-permute-done((bf16[128,256]{1,0:T(8,128)(2,1)S(1)}, bf16[128,256]{1,0:T(8,128)(2,1)S(1)}, u32[]{:S(2)}, u32[]{:S(2)}) %collective-permute-start.15) | collective-permute-done | bytes 65568 | tf_op jit(solution)/shard_map/ppermute | solution.py:138
  50.7 1.5 %collective-permute-start.16 = (bf16[128,384]{1,0:T(8,128)(2,1)S(1)}, bf16[128,384]{1,0:T(8,128)(2,1)S(1)}, u32[]{:S(2)}, u32[]{:S(2)}) collective-permute-start(bf16[128,384]{1,0:T(8,128)(2,1)S(1)} %get-tuple-element.80), channel_id=1, source_target_pairs={{0,28},{1,29},{2,30},{3,31},{4,0},{5,1},{6,2},{7,3},{8,4},{9,5},{1... | collective-permute-start | bytes 294920 | tf_op jit(solution)/shard_map/ppermute | solution.py:134
  52.2 2.8 %collective-permute-start.18 = (bf16[128,256]{1,0:T(8,128)(2,1)S(1)}, bf16[128,256]{1,0:T(8,128)(2,1)S(1)}, u32[]{:S(2)}, u32[]{:S(2)}) collective-permute-start(bf16[128,256]{1,0:T(8,128)(2,1)S(1)} %shard_map.122.small), channel_id=1, source_target_pairs={{0,30},{1,31},{2,28},{3,29},{4,2},{5,3},{6,0},{7,1},{8,6},{9,7},{1... | collective-permute-start | bytes 196616 | tf_op jit(solution)/shard_map/ppermute | solution.py:134
  55.0 1.8 %collective-permute-start.19 = (bf16[128,256]{1,0:T(8,128)(2,1)S(1)}, bf16[128,256]{1,0:T(8,128)(2,1)S(1)}, u32[]{:S(2)}, u32[]{:S(2)}) collective-permute-start(bf16[128,256]{1,0:T(8,128)(2,1)S(1)} %shard_map.122.small), channel_id=1, source_target_pairs={{0,31},{1,30},{2,29},{3,28},{4,3},{5,2},{6,1},{7,0},{8,7},{9,6},{1... | collective-permute-start | bytes 196616 | tf_op jit(solution)/shard_map/ppermute | solution.py:134
  57.1 3.7 %collective-permute-done.19.refs_3_ = bf16[128,256]{1,0:T(8,128)(2,1)S(1)} collective-permute-done((bf16[128,256]{1,0:T(8,128)(2,1)S(1)}, bf16[128,256]{1,0:T(8,128)(2,1)S(1)}, u32[]{:S(2)}, u32[]{:S(2)}) %collective-permute-start.19) | collective-permute-done | bytes 65568 | tf_op jit(solution)/shard_map/ppermute | solution.py:134
  (31 shorter events, 6.7 us)
Async XLA Ops:
  0.6 17.4 %collective-permute-start.6 = (bf16[128,512]{1,0:T(8,128)(2,1)}, bf16[128,512]{1,0:T(8,128)(2,1)S(1)}, u32[]{:S(2)}, u32[]{:S(2)}) collective-permute-start(bf16[128,512]{1,0:T(8,128)(2,1)} %bitcast.4), channel_id=1, source_target_pairs={{0,28},{1,29},{2,30},{3,31},{4,0},{5,1},{6,2},{7,3},{8,4},{9,5},{1... | collective-permute-start | bytes 393224 | tf_op jit(solution)/shard_map/ppermute | solution.py:134
  4.0 5.8 %copy-start = (f32[1,128,128]{2,1,0:T(8,128)S(1)}, f32[1,128,128]{2,1,0:T(8,128)}, u32[]{:S(2)}) copy-start(f32[1,128,128]{2,1,0:T(8,128)} %enc.1) | copy-start | bytes 196612
  8.2 4.3 %collective-permute-start = (bf16[128,256]{1,0:T(8,128)(2,1)S(1)}, bf16[128,256]{1,0:T(8,128)(2,1)S(1)}, u32[]{:S(2)}, u32[]{:S(2)}) collective-permute-start(bf16[128,256]{1,0:T(8,128)(2,1)S(1)} %get-tuple-element.44), channel_id=1, source_target_pairs={{0,1},{1,0},{2,3},{3,2},{4,5},{5,4},{6,7},{7,6},{8,9},{9,8},{10,11... | collective-permute-start | bytes 196616 | tf_op jit(solution)/shard_map/ppermute | solution.py:138
  12.5 15.6 %collective-permute-start.1 = (bf16[128,640]{1,0:T(8,128)(2,1)S(1)}, bf16[128,640]{1,0:T(8,128)(2,1)S(1)}, u32[]{:S(2)}, u32[]{:S(2)}) collective-permute-start(bf16[128,640]{1,0:T(8,128)(2,1)S(1)} %get-tuple-element.53), channel_id=1, source_target_pairs={{0,28},{1,29},{2,30},{3,31},{4,0},{5,1},{6,2},{7,3},{8,4},{9,5},{1... | collective-permute-start | bytes 491528 | tf_op jit(solution)/shard_map/ppermute | solution.py:134
  12.6 6.4 %collective-permute-start.2 = (bf16[128,256]{1,0:T(8,128)(2,1)S(1)}, bf16[128,256]{1,0:T(8,128)(2,1)S(1)}, u32[]{:S(2)}, u32[]{:S(2)}) collective-permute-start(bf16[128,256]{1,0:T(8,128)(2,1)S(1)} %get-tuple-element.54), channel_id=1, source_target_pairs={{0,28},{1,29},{2,30},{3,31},{4,0},{5,1},{6,2},{7,3},{8,4},{9,5},{1... | collective-permute-start | bytes 196616 | tf_op jit(solution)/shard_map/ppermute | solution.py:134
  13.5 5.5 %collective-permute-start.3 = (bf16[128,256]{1,0:T(8,128)(2,1)S(1)}, bf16[128,256]{1,0:T(8,128)(2,1)S(1)}, u32[]{:S(2)}, u32[]{:S(2)}) collective-permute-start(bf16[128,256]{1,0:T(8,128)(2,1)S(1)} %get-tuple-element.54), channel_id=1, source_target_pairs={{0,29},{1,28},{2,31},{3,30},{4,1},{5,0},{6,3},{7,2},{8,5},{9,4},{1... | collective-permute-start | bytes 196616 | tf_op jit(solution)/shard_map/ppermute | solution.py:134
  14.6 5.6 %collective-permute-start.4 = (bf16[128,256]{1,0:T(8,128)(2,1)S(1)}, bf16[128,256]{1,0:T(8,128)(2,1)S(1)}, u32[]{:S(2)}, u32[]{:S(2)}) collective-permute-start(bf16[128,256]{1,0:T(8,128)(2,1)S(1)} %get-tuple-element.54), channel_id=1, source_target_pairs={{0,30},{1,31},{2,28},{3,29},{4,2},{5,3},{6,0},{7,1},{8,6},{9,7},{1... | collective-permute-start | bytes 196616 | tf_op jit(solution)/shard_map/ppermute | solution.py:134
  18.0 6.2 %collective-permute-start.5 = (bf16[128,256]{1,0:T(8,128)(2,1)S(1)}, bf16[128,256]{1,0:T(8,128)(2,1)S(1)}, u32[]{:S(2)}, u32[]{:S(2)}) collective-permute-start(bf16[128,256]{1,0:T(8,128)(2,1)S(1)} %get-tuple-element.54), channel_id=1, source_target_pairs={{0,31},{1,30},{2,29},{3,28},{4,3},{5,2},{6,1},{7,0},{8,7},{9,6},{1... | collective-permute-start | bytes 196616 | tf_op jit(solution)/shard_map/ppermute | solution.py:134
  25.4 4.3 %collective-permute-start.7 = (bf16[128,256]{1,0:T(8,128)(2,1)S(1)}, bf16[128,256]{1,0:T(8,128)(2,1)S(1)}, u32[]{:S(2)}, u32[]{:S(2)}) collective-permute-start(bf16[128,256]{1,0:T(8,128)(2,1)S(1)} %get-tuple-element.64), channel_id=1, source_target_pairs={{0,1},{1,0},{2,3},{3,2},{4,5},{5,4},{6,7},{7,6},{8,9},{9,8},{10,11... | collective-permute-start | bytes 196616 | tf_op jit(solution)/shard_map/ppermute | solution.py:138
  25.5 8.3 %collective-permute-start.13 = (bf16[128,512]{1,0:T(8,128)(2,1)S(1)}, bf16[128,512]{1,0:T(8,128)(2,1)S(1)}, u32[]{:S(2)}, u32[]{:S(2)}) collective-permute-start(bf16[128,512]{1,0:T(8,128)(2,1)S(1)} %collective-permute-done.6.held), channel_id=1, source_target_pairs={{0,28},{1,29},{2,30},{3,31},{4,0},{5,1},{6,2},{7,3},{8,4},{9,5},{1... | collective-permute-start | bytes 393224 | tf_op jit(solution)/shard_map/ppermute | solution.py:134
  29.8 13.0 %collective-permute-start.8 = (bf16[128,640]{1,0:T(8,128)(2,1)S(1)}, bf16[128,640]{1,0:T(8,128)(2,1)S(1)}, u32[]{:S(2)}, u32[]{:S(2)}) collective-permute-start(bf16[128,640]{1,0:T(8,128)(2,1)S(1)} %get-tuple-element.68), channel_id=1, source_target_pairs={{0,28},{1,29},{2,30},{3,31},{4,0},{5,1},{6,2},{7,3},{8,4},{9,5},{1... | collective-permute-start | bytes 491528 | tf_op jit(solution)/shard_map/ppermute | solution.py:134
  30.8 7.1 %collective-permute-start.9 = (bf16[128,256]{1,0:T(8,128)(2,1)S(1)}, bf16[128,256]{1,0:T(8,128)(2,1)S(1)}, u32[]{:S(2)}, u32[]{:S(2)}) collective-permute-start(bf16[128,256]{1,0:T(8,128)(2,1)S(1)} %get-tuple-element.69), channel_id=1, source_target_pairs={{0,28},{1,29},{2,30},{3,31},{4,0},{5,1},{6,2},{7,3},{8,4},{9,5},{1... | collective-permute-start | bytes 196616 | tf_op jit(solution)/shard_map/ppermute | solution.py:134
  31.0 6.9 %collective-permute-start.10 = (bf16[128,256]{1,0:T(8,128)(2,1)S(1)}, bf16[128,256]{1,0:T(8,128)(2,1)S(1)}, u32[]{:S(2)}, u32[]{:S(2)}) collective-permute-start(bf16[128,256]{1,0:T(8,128)(2,1)S(1)} %get-tuple-element.69), channel_id=1, source_target_pairs={{0,29},{1,28},{2,31},{3,30},{4,1},{5,0},{6,3},{7,2},{8,5},{9,4},{1... | collective-permute-start | bytes 196616 | tf_op jit(solution)/shard_map/ppermute | solution.py:134
  31.4 6.5 %collective-permute-start.11 = (bf16[128,256]{1,0:T(8,128)(2,1)S(1)}, bf16[128,256]{1,0:T(8,128)(2,1)S(1)}, u32[]{:S(2)}, u32[]{:S(2)}) collective-permute-start(bf16[128,256]{1,0:T(8,128)(2,1)S(1)} %get-tuple-element.69), channel_id=1, source_target_pairs={{0,30},{1,31},{2,28},{3,29},{4,2},{5,3},{6,0},{7,1},{8,6},{9,7},{1... | collective-permute-start | bytes 196616 | tf_op jit(solution)/shard_map/ppermute | solution.py:134
  33.8 5.6 %collective-permute-start.12 = (bf16[128,256]{1,0:T(8,128)(2,1)S(1)}, bf16[128,256]{1,0:T(8,128)(2,1)S(1)}, u32[]{:S(2)}, u32[]{:S(2)}) collective-permute-start(bf16[128,256]{1,0:T(8,128)(2,1)S(1)} %get-tuple-element.69), channel_id=1, source_target_pairs={{0,31},{1,30},{2,29},{3,28},{4,3},{5,2},{6,1},{7,0},{8,7},{9,6},{1... | collective-permute-start | bytes 196616 | tf_op jit(solution)/shard_map/ppermute | solution.py:134
  40.7 4.5 %collective-permute-start.14 = (bf16[128,256]{1,0:T(8,128)(2,1)S(1)}, bf16[128,256]{1,0:T(8,128)(2,1)S(1)}, u32[]{:S(2)}, u32[]{:S(2)}) collective-permute-start(bf16[128,256]{1,0:T(8,128)(2,1)S(1)} %get-tuple-element.74), channel_id=1, source_target_pairs={{0,1},{1,0},{2,3},{3,2},{4,5},{5,4},{6,7},{7,6},{8,9},{9,8},{10,11... | collective-permute-start | bytes 196616 | tf_op jit(solution)/shard_map/ppermute | solution.py:138
  43.9 6.8 %collective-permute-start.15 = (bf16[128,256]{1,0:T(8,128)(2,1)S(1)}, bf16[128,256]{1,0:T(8,128)(2,1)S(1)}, u32[]{:S(2)}, u32[]{:S(2)}) collective-permute-start(bf16[128,256]{1,0:T(8,128)(2,1)S(1)} %get-tuple-element.79), channel_id=1, source_target_pairs={{0,2},{1,3},{2,0},{3,1},{4,6},{5,7},{6,4},{7,5},{8,10},{9,11},{10,... | collective-permute-start | bytes 196616 | tf_op jit(solution)/shard_map/ppermute | solution.py:138
  50.7 10.1 %collective-permute-start.16 = (bf16[128,384]{1,0:T(8,128)(2,1)S(1)}, bf16[128,384]{1,0:T(8,128)(2,1)S(1)}, u32[]{:S(2)}, u32[]{:S(2)}) collective-permute-start(bf16[128,384]{1,0:T(8,128)(2,1)S(1)} %get-tuple-element.80), channel_id=1, source_target_pairs={{0,28},{1,29},{2,30},{3,31},{4,0},{5,1},{6,2},{7,3},{8,4},{9,5},{1... | collective-permute-start | bytes 294920 | tf_op jit(solution)/shard_map/ppermute | solution.py:134
  52.2 8.6 %collective-permute-start.17 = (bf16[128,384]{1,0:T(8,128)(2,1)S(1)}, bf16[128,384]{1,0:T(8,128)(2,1)S(1)}, u32[]{:S(2)}, u32[]{:S(2)}) collective-permute-start(bf16[128,384]{1,0:T(8,128)(2,1)S(1)} %get-tuple-element.81), channel_id=1, source_target_pairs={{0,29},{1,28},{2,31},{3,30},{4,1},{5,0},{6,3},{7,2},{8,5},{9,4},{1... | collective-permute-start | bytes 294920 | tf_op jit(solution)/shard_map/ppermute | solution.py:134
  52.2 4.9 %collective-permute-start.18 = (bf16[128,256]{1,0:T(8,128)(2,1)S(1)}, bf16[128,256]{1,0:T(8,128)(2,1)S(1)}, u32[]{:S(2)}, u32[]{:S(2)}) collective-permute-start(bf16[128,256]{1,0:T(8,128)(2,1)S(1)} %shard_map.122.small), channel_id=1, source_target_pairs={{0,30},{1,31},{2,28},{3,29},{4,2},{5,3},{6,0},{7,1},{8,6},{9,7},{1... | collective-permute-start | bytes 196616 | tf_op jit(solution)/shard_map/ppermute | solution.py:134
  55.0 5.8 %collective-permute-start.19 = (bf16[128,256]{1,0:T(8,128)(2,1)S(1)}, bf16[128,256]{1,0:T(8,128)(2,1)S(1)}, u32[]{:S(2)}, u32[]{:S(2)}) collective-permute-start(bf16[128,256]{1,0:T(8,128)(2,1)S(1)} %shard_map.122.small), channel_id=1, source_target_pairs={{0,31},{1,30},{2,29},{3,28},{4,3},{5,2},{6,1},{7,0},{8,7},{9,6},{1... | collective-permute-start | bytes 196616 | tf_op jit(solution)/shard_map/ppermute | solution.py:134
